TPU v7x, 256 devices: a whole 4x4x8 slice. The times are simulated.
256 devices in a mesh: row: 32 (over x, z), col: 8 (over y, core).
Axes of the slice: x: 4, y: 4, z: 8, core: 2. Of those that a mesh axis runs over, the one named last changes fastest.
Arguments:
- kernel: float32 [2048, 65536], P('row', 'col'), may hold values from -6 to 6
- basis: float32 [65536, 128], P('col', 'row'), may hold values from -0.0234375 to 0.0234375
- responses: float32 [2048, 512], P('row', 'col'), may hold values from -6 to 6
Outputs:
- scores: float32 [2048, 128], P('row')
- loadings: float32 [128, 65536], P('row', 'col')
- weights: float32 [512, 128], P('col')
- deflated: float32 [2048, 65536], P('row', 'col')
- basis_next: float32 [2048, 128], P('row')
All inputs are finite; a program needn't handle non-finite values.
Results may differ from a plain program's by a relative error of at most 0.00012.
Values sent between devices are 32-bit elements; how exact they have to be, the bound alone decides.
No kernel may reach another device: no remote copies, remote signals or barrier semaphores. Data moves between devices by JAX's collectives and lax.ppermute only.
A program may use at most 64 MiB of HBM per device.

v0:
```python
import functools
import math

import jax
import jax.numpy as jnp
from jax import lax
from jax.experimental import pallas as pl
from jax.experimental.pallas import tpu as pltpu
from jax.sharding import Mesh
from jax.sharding import PartitionSpec as P

HIGH = lax.Precision.HIGH
HIGHEST = lax.Precision.HIGHEST
XS, ZS, YS, CS = 4, 8, 4, 2
SIZES = {"x": XS, "z": ZS, "y": YS, "c": CS}
PANEL = 16
SUB = 8


def moved(a, axis, step):
    n = SIZES[axis]
    return lax.ppermute(a, axis, [(i, (i + step) % n) for i in range(n)])


def dot(a, b, dims, precision=HIGHEST):
    return lax.dot_general(
        a, b, (dims, ((), ())), precision=precision, preferred_element_type=jnp.float32
    )


def halves(v):
    top = v.astype(jnp.bfloat16)
    return top, (v - top.astype(jnp.float32)).astype(jnp.bfloat16)


def exchanged(blocks):
    out = [blocks[0]] + [None] * (XS - 1)
    for d in (1, 3, 2):
        out[-d % XS] = moved(blocks[d], "x", d)
    return out


def in_order(blocks, x):
    out = []
    for want in range(XS):
        v = blocks[want]
        for at in range(1, XS):
            v = jnp.where(x == at, blocks[(want - at) % XS], v)
        out.append(v)
    return out


def call(body, out_shapes, ins, limit, spaces=None, outs=None, scratch=()):
    vmem = pltpu.VMEM
    spaces = spaces or [vmem] * len(ins)
    outs = outs or [vmem] * len(out_shapes)
    return pl.pallas_call(
        body,
        out_shape=[jax.ShapeDtypeStruct(s, jnp.float32) for s in out_shapes],
        in_specs=[pl.BlockSpec(memory_space=m) for m in spaces],
        out_specs=[pl.BlockSpec(memory_space=m) for m in outs],
        scratch_shapes=scratch,
        compiler_params=pltpu.CompilerParams(vmem_limit_bytes=limit << 20),
    )(*ins)


def ring_gather(own):
    out = [own] + [None] * (ZS - 1)
    half = own.shape[1] // 2
    up = down = own
    for s in range(1, ZS // 2):
        up = moved(up, "z", 1)
        down = moved(down, "z", -1)
        up, down = lax.optimization_barrier((up, down))
        out[-s % ZS], out[s] = up, down
    out[ZS // 2 :] = [moved(up[:, :half], "z", 1), moved(down[:, half:], "z", -1)] + out[ZS // 2 + 1 :]
    return out


def merged_kernel(up_ref, down_ref, before_ref, after_ref, up_out, down_out):
    half = up_ref.shape[1]
    up_out[:, :half] = before_ref[:, :half] + up_ref[...]
    up_out[:, half:] = before_ref[:, half:]
    down_out[:, :half] = after_ref[:, :half]
    down_out[:, half:] = after_ref[:, half:] + down_ref[...]


def ring_scatter(parts):
    far = ZS // 2
    first, second = parts[far], parts[far + 1]
    parts = parts[: far + 1] + parts[far + 2 :]
    up, down = lax.optimization_barrier((moved(first, "z", 1), moved(second, "z", -1)))
    ends = [up, down, parts[far - 1], parts[far + 1]]
    up, down = call(merged_kernel, [parts[0].shape] * 2, ends, 4)
    for s in range(far - 2, -1, -1):
        up, down = lax.optimization_barrier((moved(up, "z", 1), moved(down, "z", -1)))
        if s:
            up, down = up + parts[s], down + parts[-s % ZS]
    return parts[0] + (up + down)


def summed_col(v):
    v = v + moved(v, "c", 1)
    v = v + lax.ppermute(v, "y", [(i, i ^ 1) for i in range(YS)])
    return v + moved(v, "y", 2)


def places(comp, own, z):
    at = lax.broadcasted_iota(jnp.int32, (comp, comp), 0)
    to = lax.broadcasted_iota(jnp.int32, (comp, comp), 1)
    group = own * XS
    home = (at // own % XS * ZS + (at // group + z) % ZS) * own + at % own
    return (home == to).astype(jnp.float32)


def stacked_kernel(*refs):
    *ins, out = refs
    deep, far = ins[0].shape[0], ZS // 2
    half, wide = ins[far].shape[1], ins[0].shape[1]
    for j in range(ZS):
        rows = pl.ds(j * deep, deep)
        if j == far:
            out[rows, :half] = ins[far][...]
            out[rows, half:wide] = ins[far + 1][...]
        else:
            out[rows, :wide] = ins[j + (j > far)][...]
    out[:, wide:] = jnp.zeros((out.shape[0], out.shape[1] - wide), jnp.float32)


def cut_kernel(k_ref, r_ref, *refs):
    outs, (held, sems) = refs[:XS], refs[XS:]
    rows, lanes = outs[0].shape
    wide = k_ref.shape[1] // XS
    copies = []
    for j in reversed(range(XS)):
        at = pl.multiple_of(lax.rem(lax.axis_index("x") + j, XS) * wide, 128)
        copies.append(
            pltpu.make_async_copy(k_ref.at[:, pl.ds(at, wide)], outs[j].at[:, pl.ds(0, wide)], sems.at[j])
        )
        copies[-1].start()
    copies.append(pltpu.make_async_copy(r_ref, held, sems.at[XS]))
    copies[-1].start()
    pad = jnp.zeros((rows, lanes - wide - r_ref.shape[1]), jnp.float32)
    copies[-1].wait()
    tail = jnp.concatenate([held[...], pad], 1)
    for j in range(XS):
        outs[j][:, wide:] = tail
    for copy in copies[:-1]:
        copy.wait()


def joined_kernel(*refs):
    blocks, (d_ref, l_ref, sems) = refs[:XS], refs[XS:]
    rows, wide = d_ref.shape[0], blocks[0].shape[1]
    copies = []
    for j in range(XS):
        at = pl.multiple_of(lax.rem(lax.axis_index("x") + j, XS) * wide, 128)
        copies.append(
            pltpu.make_async_copy(blocks[j].at[pl.ds(0, rows), :], d_ref.at[:, pl.ds(at, wide)], sems.at[j])
        )
        copies[-1].start()
    for j in range(XS):
        at = pl.multiple_of(lax.rem(lax.axis_index("x") + j, XS) * wide, 128)
        l_ref[:, pl.ds(at, wide)] = blocks[j][rows : rows + l_ref.shape[0], :]
    for copy in copies:
        copy.wait()


def parts_kernel(own, proj_ref, *refs):
    k_refs, proj_out, part_refs = refs[:XS], refs[XS], refs[XS + 1 :]
    comp = proj_ref.shape[1]
    group, far = own * XS, ZS // 2
    rows, lanes = k_refs[0].shape
    wide = lanes - comp
    half = part_refs[far].shape[1]
    x, z = lax.axis_index("x"), lax.axis_index("z")

    def put(at, value):
        end = at + value.shape[1]
        for j in range(ZS):
            v = value[j * group : (j + 1) * group]
            if j != far:
                part_refs[j + (j > far)][:, at:end] = v
            else:
                if at < half:
                    part_refs[far][:, at : min(end, half)] = v[:, : min(end, half) - at]
                if end > half:
                    part_refs[far + 1][:, max(at, half) - half : end - half] = v[:, max(at, half) - at :]

    proj = proj_ref[...]
    proj_abs = dot(proj, places(comp, own, z), ((1,), (0,)))
    proj_out[...] = proj_abs

    def by_x(v):
        return jnp.concatenate(in_order(v, x), 0)

    def split(v):
        return [v[j * rows : (j + 1) * rows] for j in range(XS)]

    right = jnp.concatenate([by_x(split(proj_abs)), by_x([k[:, wide:] for k in k_refs])], 1)
    put(wide, dot(by_x(split(proj)), right, ((0,), (0,))))
    top, rest = halves(proj)
    step = 512
    for at in range(0, wide, step):
        k_top, k_rest = halves(jnp.concatenate([k[:, at : at + step] for k in k_refs], 0))
        dims = ((0,), (0,))
        put(at, dot(top, k_top, dims, None) + (dot(top, k_rest, dims, None) + dot(rest, k_top, dims, None)))


def inverse_factor(w_ref, v_ref, comp):
    row = lax.broadcasted_iota(jnp.int32, (PANEL, comp), 0)
    v_ref[...] = jnp.where(
        lax.broadcasted_iota(jnp.int32, (comp, comp), 0)
        == lax.broadcasted_iota(jnp.int32, (comp, comp), 1),
        1.0,
        0.0,
    )

    def panel(p, _):
        rows = pl.ds(pl.multiple_of(p * PANEL, PANEL), PANEL)
        w, v = w_ref[rows, :], v_ref[rows, :]
        turned = pltpu.roll(w, (comp - p * PANEL) % comp, 1)
        cols = [jnp.broadcast_to(turned[:, i : i + 1], (PANEL, comp)) for i in range(PANEL)]
        for i in range(PANEL):
            pivot = jnp.broadcast_to(cols[i][i : i + 1, :], (PANEL, comp))
            scale = lax.rsqrt(pivot)
            times = cols[i] * scale

            def step(a):
                b = jnp.broadcast_to(a[i : i + 1, :], (PANEL, comp)) * scale
                return jnp.where(row > i, a - times * b, jnp.where(row == i, b, a))

            w, v = step(w), step(v)
            cols = [step(c) if k > i else c for k, c in enumerate(cols)]
        v_ref[rows, :] = v
        below = lax.broadcasted_iota(jnp.int32, (comp, comp), 0) >= (p + 1) * PANEL
        change = dot(w, jnp.concatenate([w, v], 1), ((0,), (0,)))
        w_ref[...] = w_ref[...] - change[:, :comp]
        v_ref[...] = v_ref[...] - jnp.where(below, change[:, comp:], 0.0)
        return 0

    lax.fori_loop(0, comp // PANEL, panel, 0)


def finish_kernel(own, row_count, *refs):
    k_refs, g_refs = refs[:XS], refs[XS : XS + ZS + 1]
    proj_ref, resp_ref = refs[XS + ZS + 1 : XS + ZS + 3]
    scores_ref, weights_ref, next_ref, *d_refs = refs[XS + ZS + 3 : -4]
    w_ref, v_ref, small_ref, raw_ref = refs[-4:]
    comp = proj_ref.shape[1]
    group = own * XS
    rows = k_refs[0].shape[0]
    wide = k_refs[0].shape[1] - comp
    resp = resp_ref.shape[1]
    root_rows = math.sqrt(row_count)
    x, z = lax.axis_index("x"), lax.axis_index("z")
    far = ZS // 2
    half = (g_refs[far].shape[1])
    for j in range(ZS):
        at = pl.ds(j * group, group)
        if j == far:
            raw_ref[at, :half] = g_refs[far][...]
            raw_ref[at, half:] = g_refs[far + 1][:, : wide - half]
            small_ref[at, :] = g_refs[far + 1][:, wide - half :]
        else:
            ref = g_refs[j if j < far else j + 1]
            raw_ref[at, :] = ref[:, :wide]
            small_ref[at, :] = ref[:, wide:]

    place = places(comp, own, z)
    small = dot(place, small_ref[...], ((0,), (0,)))
    w_ref[...] = small[:, :comp] * (1.0 / row_count)
    inverse_factor(w_ref, v_ref, comp)
    inv = v_ref[...]
    inv_place = dot(inv, place, ((1,), (1,)))
    scores_all = dot(proj_ref[...], inv, ((1,), (1,)))
    scores_ref[...] = scores_all[:rows]
    back = dot(scores_all, inv_place, ((1,), (0,))) * (1.0 / row_count)
    weights = dot(small[:, comp : comp + resp], inv, ((0,), (1,))) * (1.0 / root_rows)
    weights_ref[...] = weights
    next_ref[...] = dot(resp_ref[...], weights, ((1,), (0,)))

    at = lax.broadcasted_iota(jnp.int32, (XS * SUB, comp), 0)
    to = lax.broadcasted_iota(jnp.int32, (XS * SUB, comp), 1)
    wanted = (((x + at // SUB) % XS) * ZS + z) * own + at % SUB
    pick = jnp.where((wanted == to) & (at % SUB < own), 1.0, 0.0)
    picks = dot(pick, inv_place, ((1,), (0,))) * (1.0 / root_rows)
    left = []
    for j in range(XS):
        left += [back[j * rows : (j + 1) * rows], picks[j * SUB : (j + 1) * SUB]]
    left = jnp.concatenate(left, 0)
    left_top, left_rest = halves(left)
    step = 512

    def tile(t, _):
        at = pl.ds(pl.multiple_of(t * step, step), step)
        top, rest = halves(raw_ref[:, at])
        dims = ((1,), (0,))
        out = dot(left_top, top, dims, None) + (
            dot(left_top, rest, dims, None) + dot(left_rest, top, dims, None)
        )
        for j in range(XS):
            base = j * (rows + SUB)
            d_refs[j][:rows, at] = k_refs[j][:, at] - out[base : base + rows]
            d_refs[j][rows:, at] = out[base + rows : base + rows + SUB]
        return 0

    lax.fori_loop(0, wide // step, tile, 0)


def local(kernel, basis, responses):
    rows, cols = kernel.shape
    own = basis.shape[1]
    resp = responses.shape[1]
    comp = own * XS * ZS
    row_count = rows * XS * ZS
    resp_count = resp * YS * CS
    wide = cols // XS
    x, c = lax.axis_index("x"), lax.axis_index("c")
    hbm, vmem = pl.ANY, pltpu.VMEM
    dma = [pltpu.SemaphoreType.DMA((XS,))]

    basis_t = basis.T
    b_blocks = exchanged(
        [lax.dynamic_slice(basis_t, (0, ((x + j) % XS) * wide), (own, wide)) for j in range(XS)]
    )
    lanes = wide + comp
    k_blocks = call(
        cut_kernel,
        [(rows, lanes)] * XS,
        [pltpu.with_memory_space_constraint(a, pltpu.HBM) for a in (kernel, responses)],
        8,
        [pltpu.HBM] * 2,
        None,
        [pltpu.VMEM((rows, resp), jnp.float32), pltpu.SemaphoreType.DMA((XS + 1,))],
    )
    first = jnp.concatenate(in_order(b_blocks, x), 0)
    first, *k_blocks = lax.optimization_barrier((first, *k_blocks))
    k_blocks = exchanged(k_blocks)
    b_parts = ring_gather(first)
    (b_all,) = call(stacked_kernel, [(comp, lanes)], b_parts, 8)
    k_all = jnp.concatenate(k_blocks, 0)

    proj = dot(k_all, b_all, ((1,), (1,)), HIGH).reshape(XS, CS, rows // CS, comp)
    mine = lax.dynamic_slice_in_dim(proj, c, 1, 1)
    other = lax.dynamic_slice_in_dim(proj, 1 - c, 1, 1)
    proj = mine + moved(other, "c", 1)
    one, two, three = (jnp.roll(moved(proj, "x", d), -d, 0) for d in (1, 2, 3))
    proj = (proj + two) + (one + three)
    one, two, three = (moved(proj, "y", d) for d in (1, 2, 3))
    proj = (proj + two) + (one + three)
    other = moved(proj, "c", 1)
    proj = jnp.concatenate([jnp.where(c == 0, proj, other), jnp.where(c == 0, other, proj)], 1)
    proj = proj.reshape(XS * rows, comp)

    group, full = own * XS, lanes + comp
    shapes = [(group, full)] * (ZS + 1)
    shapes[ZS // 2 : ZS // 2 + 2] = [(group, full // 2)] * 2
    proj_abs, *parts = call(
        functools.partial(parts_kernel, own), [(XS * rows, comp)] + shapes, [proj, *k_blocks], 24
    )
    total = ring_gather(ring_scatter(parts))
    scores, weights, nxt, *d_blocks = call(
        functools.partial(finish_kernel, own, row_count),
        [(rows, comp), (resp, comp), (rows, comp)] + [(rows + SUB, wide)] * XS,
        [*k_blocks, *total, proj_abs, responses],
        24,
        None,
        None,
        [pltpu.VMEM(s, jnp.float32) for s in ((comp, comp), (comp, comp), (comp, full - wide), (comp, wide))],
    )
    d_blocks = exchanged(d_blocks)
    basis_next = summed_col(nxt) / math.sqrt(resp_count)
    deflated, loadings = call(
        joined_kernel, [(rows, cols), (own, cols)], d_blocks, 8, None, [hbm, vmem], dma
    )
    return (scores, loadings, weights, deflated, basis_next)


def solution(mesh):
    finer = Mesh(mesh.devices.reshape(XS, ZS, YS, CS), ("x", "z", "y", "c"))
    row, col = ("x", "z"), ("y", "c")
    in_specs = (P(row, col), P(col, row), P(row, col))
    out_specs = (P(row, None), P(row, col), P(col, None), P(row, col), P(row, None))

    return jax.shard_map(local, mesh=finer, in_specs=in_specs, out_specs=out_specs, check_vma=False)
```

profile of v0, /device:TPU:8, one launch (start us, length us, event | category | flops | bytes accessed | tf_op | source)
XLA Modules:
  0.0 158.0 jit_solution(13998926719827627745)
XLA Ops:
  3.0 2.7 %collective-permute-start.1 = (f32[4,2048]{1,0:T(4,128)S(1)}, f32[4,2048]{1,0:T(4,128)S(1)}, u32[]{:S(2)}, u32[]{:S(2)}) collective-permute-start(f32[4,2048]{1,0:T(4,128)S(1)} %get-tuple-element.112), channel_id=1, source_target_pairs={{0,128},{64,192},{128,0},{192,64},{1,129},{65,193},{129,1},{193,65... | collective-permute-start | bytes 98312 | tf_op jit(solution)/shard_map/ppermute | solution.py:22
  7.2 2.7 %shard_map.74 = (f32[64,2176]{1,0:T(8,128)S(1)}, f32[64,2176]{1,0:T(8,128)}, f32[64,2176]{1,0:T(8,128)}, f32[64,2176]{1,0:T(8,128)}) custom-call(f32[64,8192]{1,0:T(8,128)} %k_ref.1, f32[64,64]{1,0:T(8,128)} %refs_14_.1), custom_call_target="tpu_custom_call" | custom-call | tf_op jit(solution)/shard_map/pallas_call | solution.py:57
  10.8 2.4 %collective-permute-start.3 = (f32[64,2176]{1,0:T(8,128)}, f32[64,2176]{1,0:T(8,128)S(1)}, u32[]{:S(2)}, u32[]{:S(2)}) collective-permute-start(f32[64,2176]{1,0:T(8,128)} %get-tuple-element.60), channel_id=1, source_target_pairs={{0,192},{64,0},{128,64},{192,128},{1,193},{65,1},{129,65},{193,129... | collective-permute-start | bytes 1671176 | tf_op jit(solution)/shard_map/ppermute | solution.py:22
  14.2 5.9 %collective-permute-start.7 = (f32[16,2048]{1,0:T(8,128)S(1)}, f32[16,2048]{1,0:T(8,128)S(1)}, u32[]{:S(2)}, u32[]{:S(2)}) collective-permute-start(f32[16,2048]{1,0:T(8,128)S(1)} %pad_maximum_fusion.refs_0_), channel_id=1, source_target_pairs={{0,56},{8,0},{16,8},{24,16},{32,24},{40,32},{48,40},{56,48},{1,57}... | collective-permute-start | bytes 393224 | tf_op jit(solution)/shard_map/ppermute | solution.py:22
  20.1 2.5 %collective-permute-done.7.refs_1_ = f32[16,2048]{1,0:T(8,128)S(1)} collective-permute-done((f32[16,2048]{1,0:T(8,128)S(1)}, f32[16,2048]{1,0:T(8,128)S(1)}, u32[]{:S(2)}, u32[]{:S(2)}) %collective-permute-start.7) | collective-permute-done | bytes 131104 | tf_op jit(solution)/shard_map/ppermute | solution.py:22
  22.6 3.7 %collective-permute-done.6.refs_8_ = f32[16,2048]{1,0:T(8,128)S(1)} collective-permute-done((f32[16,2048]{1,0:T(8,128)S(1)}, f32[16,2048]{1,0:T(8,128)S(1)}, u32[]{:S(2)}, u32[]{:S(2)}) %collective-permute-start.6) | collective-permute-done | bytes 131104 | tf_op jit(solution)/shard_map/ppermute | solution.py:22
  28.3 3.3 %collective-permute-done.9.refs_2_ = f32[16,2048]{1,0:T(8,128)S(1)} collective-permute-done((f32[16,2048]{1,0:T(8,128)S(1)}, f32[16,2048]{1,0:T(8,128)S(1)}, u32[]{:S(2)}, u32[]{:S(2)}) %collective-permute-start.9) | collective-permute-done | bytes 131104 | tf_op jit(solution)/shard_map/ppermute | solution.py:22
  34.8 3.5 %collective-permute-done.11.refs_3_ = f32[16,2048]{1,0:T(8,128)S(1)} collective-permute-done((f32[16,2048]{1,0:T(8,128)S(1)}, f32[16,2048]{1,0:T(8,128)S(1)}, u32[]{:S(2)}, u32[]{:S(2)}) %collective-permute-start.11) | collective-permute-done | bytes 131104 | tf_op jit(solution)/shard_map/ppermute | solution.py:22
  39.9 3.2 %collective-permute-start.13 = (f32[16,1024]{1,0:T(8,128)S(1)}, f32[16,1024]{1,0:T(8,128)S(1)}, u32[]{:S(2)}, u32[]{:S(2)}) collective-permute-start(f32[16,1024]{1,0:T(8,128)S(1)} %slice.37), channel_id=1, source_target_pairs={{0,56},{8,0},{16,8},{24,16},{32,24},{40,32},{48,40},{56,48},{1,57}... | collective-permute-start | bytes 196616 | tf_op jit(solution)/shard_map/ppermute | solution.py:22
  43.1 2.2 %collective-permute-done.12.refs_4_ = f32[16,1024]{1,0:T(8,128)S(1)} collective-permute-done((f32[16,1024]{1,0:T(8,128)S(1)}, f32[16,1024]{1,0:T(8,128)S(1)}, u32[]{:S(2)}, u32[]{:S(2)}) %collective-permute-start.12) | collective-permute-done | bytes 65568 | tf_op jit(solution)/shard_map/ppermute | solution.py:22
  48.1 2.3 %collective-permute-start.17 = (f32[4,1,32,128]{3,2,1,0:T(8,128)S(1)}, f32[4,1,32,128]{3,2,1,0:T(8,128)S(1)}, u32[]{:S(2)}, u32[]{:S(2)}) collective-permute-start(f32[4,1,32,128]{3,2,1,0:T(8,128)S(1)} %dynamic-slice_add_fusion), channel_id=1, source_target_pairs={{0,192},{64,0},{128,64},{192,128},{1,193},{65,1},{129,65},{193,129... | collective-permute-start | bytes 196616 | tf_op jit(solution)/shard_map/ppermute | solution.py:22
  53.7 3.7 %collective-permute-done.16 = f32[4,1,32,128]{3,2,1,0:T(8,128)S(1)} collective-permute-done((f32[4,1,32,128]{3,2,1,0:T(8,128)S(1)}, f32[4,1,32,128]{3,2,1,0:T(8,128)S(1)}, u32[]{:S(2)}, u32[]{:S(2)}) %collective-permute-start.16) | collective-permute-done | bytes 65568 | tf_op jit(solution)/shard_map/ppermute | solution.py:22
  59.5 3.5 %collective-permute-start.18 = (f32[4,1,32,128]{3,2,1,0:T(8,128)S(1)}, f32[4,1,32,128]{3,2,1,0:T(8,128)S(1)}, u32[]{:S(2)}, u32[]{:S(2)}) collective-permute-start(f32[4,1,32,128]{3,2,1,0:T(8,128)S(1)} %fusion.8), channel_id=1, source_target_pairs={{0,4},{2,6},{4,0},{6,2},{1,5},{3,7},{5,1},{7,3},{8,12},{10,14},{12... | collective-permute-start | bytes 196616 | tf_op jit(solution)/shard_map/ppermute | solution.py:22
  67.9 3.3 %collective-permute-start.23 = (f32[16,1152]{1,0:T(8,128)S(1)}, f32[16,1152]{1,0:T(8,128)S(1)}, u32[]{:S(2)}, u32[]{:S(2)}) collective-permute-start(f32[16,1152]{1,0:T(8,128)S(1)} %get-tuple-element.72), channel_id=1, source_target_pairs={{0,56},{8,0},{16,8},{24,16},{32,24},{40,32},{48,40},{56,48},{1,57}... | collective-permute-start | bytes 221192 | tf_op jit(solution)/shard_map/ppermute | solution.py:22
  71.2 2.5 %collective-permute-done.22.up_ref = f32[16,1152]{1,0:T(8,128)S(1)} collective-permute-done((f32[16,1152]{1,0:T(8,128)S(1)}, f32[16,1152]{1,0:T(8,128)S(1)}, u32[]{:S(2)}, u32[]{:S(2)}) %collective-permute-start.22) | collective-permute-done | bytes 73760 | tf_op jit(solution)/shard_map/ppermute | solution.py:22
  73.9 3.2 %collective-permute-start.25 = (f32[16,2304]{1,0:T(8,128)S(1)}, f32[16,2304]{1,0:T(8,128)S(1)}, u32[]{:S(2)}, u32[]{:S(2)}) collective-permute-start(f32[16,2304]{1,0:T(8,128)S(1)} %get-tuple-element.78), channel_id=1, source_target_pairs={{0,56},{8,0},{16,8},{24,16},{32,24},{40,32},{48,40},{56,48},{1,57}... | collective-permute-start | bytes 442376 | tf_op jit(solution)/shard_map/ppermute | solution.py:22
  77.1 3.3 %collective-permute-done.24 = f32[16,2304]{1,0:T(8,128)S(1)} collective-permute-done((f32[16,2304]{1,0:T(8,128)S(1)}, f32[16,2304]{1,0:T(8,128)S(1)}, u32[]{:S(2)}, u32[]{:S(2)}) %collective-permute-start.24) | collective-permute-done | bytes 147488 | tf_op jit(solution)/shard_map/ppermute | solution.py:22
  80.4 3.1 %collective-permute-start.27 = (f32[16,2304]{1,0:T(8,128)S(1)}, f32[16,2304]{1,0:T(8,128)S(1)}, u32[]{:S(2)}, u32[]{:S(2)}) collective-permute-start(f32[16,2304]{1,0:T(8,128)S(1)} %add.118), channel_id=1, source_target_pairs={{0,56},{8,0},{16,8},{24,16},{32,24},{40,32},{48,40},{56,48},{1,57}... | collective-permute-start | bytes 442376 | tf_op jit(solution)/shard_map/ppermute | solution.py:22
  83.7 2.6 %collective-permute-done.27 = f32[16,2304]{1,0:T(8,128)S(1)} collective-permute-done((f32[16,2304]{1,0:T(8,128)S(1)}, f32[16,2304]{1,0:T(8,128)S(1)}, u32[]{:S(2)}, u32[]{:S(2)}) %collective-permute-start.27) | collective-permute-done | bytes 147488 | tf_op jit(solution)/shard_map/ppermute | solution.py:22
  86.2 3.8 %collective-permute-done.26 = f32[16,2304]{1,0:T(8,128)S(1)} collective-permute-done((f32[16,2304]{1,0:T(8,128)S(1)}, f32[16,2304]{1,0:T(8,128)S(1)}, u32[]{:S(2)}, u32[]{:S(2)}) %collective-permute-start.26) | collective-permute-done | bytes 147488 | tf_op jit(solution)/shard_map/ppermute | solution.py:22
  90.1 2.1 %collective-permute-start.28 = (f32[16,2304]{1,0:T(8,128)S(1)}, f32[16,2304]{1,0:T(8,128)S(1)}, u32[]{:S(2)}, u32[]{:S(2)}) collective-permute-start(f32[16,2304]{1,0:T(8,128)S(1)} %add.119), channel_id=1, source_target_pairs={{0,8},{8,16},{16,24},{24,32},{32,40},{40,48},{48,56},{56,0},{1,9},... | collective-permute-start | bytes 442376 | tf_op jit(solution)/shard_map/ppermute | solution.py:22
  92.2 3.2 %collective-permute-done.29 = f32[16,2304]{1,0:T(8,128)S(1)} collective-permute-done((f32[16,2304]{1,0:T(8,128)S(1)}, f32[16,2304]{1,0:T(8,128)S(1)}, u32[]{:S(2)}, u32[]{:S(2)}) %collective-permute-start.29) | collective-permute-done | bytes 147488 | tf_op jit(solution)/shard_map/ppermute | solution.py:22
  99.1 4.6 %collective-permute-done.31.refs_5_ = f32[16,2304]{1,0:T(8,128)S(1)} collective-permute-done((f32[16,2304]{1,0:T(8,128)S(1)}, f32[16,2304]{1,0:T(8,128)S(1)}, u32[]{:S(2)}, u32[]{:S(2)}) %collective-permute-start.31) | collective-permute-done | bytes 147488 | tf_op jit(solution)/shard_map/ppermute | solution.py:22
  107.0 3.6 %collective-permute-done.33.refs_6_ = f32[16,2304]{1,0:T(8,128)S(1)} collective-permute-done((f32[16,2304]{1,0:T(8,128)S(1)}, f32[16,2304]{1,0:T(8,128)S(1)}, u32[]{:S(2)}, u32[]{:S(2)}) %collective-permute-start.33) | collective-permute-done | bytes 147488 | tf_op jit(solution)/shard_map/ppermute | solution.py:22
  113.8 3.1 %collective-permute-done.35.refs_7_ = f32[16,2304]{1,0:T(8,128)S(1)} collective-permute-done((f32[16,2304]{1,0:T(8,128)S(1)}, f32[16,2304]{1,0:T(8,128)S(1)}, u32[]{:S(2)}, u32[]{:S(2)}) %collective-permute-start.35) | collective-permute-done | bytes 147488 | tf_op jit(solution)/shard_map/ppermute | solution.py:22
  119.1 2.7 %collective-permute-start.37 = (f32[16,1152]{1,0:T(8,128)S(1)}, f32[16,1152]{1,0:T(8,128)S(1)}, u32[]{:S(2)}, u32[]{:S(2)}) collective-permute-start(f32[16,1152]{1,0:T(8,128)S(1)} %slice.45), channel_id=1, source_target_pairs={{0,56},{8,0},{16,8},{24,16},{32,24},{40,32},{48,40},{56,48},{1,57}... | collective-permute-start | bytes 221192 | tf_op jit(solution)/shard_map/ppermute | solution.py:22
  121.8 2.3 %collective-permute-done.36.refs_8_ = f32[16,1152]{1,0:T(8,128)S(1)} collective-permute-done((f32[16,1152]{1,0:T(8,128)S(1)}, f32[16,1152]{1,0:T(8,128)S(1)}, u32[]{:S(2)}, u32[]{:S(2)}) %collective-permute-start.36) | collective-permute-done | bytes 73760 | tf_op jit(solution)/shard_map/ppermute | solution.py:22
  124.1 8.8 %shard_map.78 = (f32[64,128]{1,0:T(8,128)}, f32[64,128]{1,0:T(8,128)}, f32[64,128]{1,0:T(8,128)S(1)}, f32[72,2048]{1,0:T(8,128)S(1)}, f32[72,2048]{1,0:T(8,128)S...) custom-call(f32[64,2176]{1,0:T(8,128)S(1)} %get-tuple-element.59.refs_0_, ...), custom_call_target="tpu_custom_call" | custom-call | tf_op jit(solution)/shard_map/pallas_call | solution.py:57
  133.0 2.1 %collective-permute-start.38 = (f32[72,2048]{1,0:T(8,128)S(1)}, f32[72,2048]{1,0:T(8,128)S(1)}, u32[]{:S(2)}, u32[]{:S(2)}) collective-permute-start(f32[72,2048]{1,0:T(8,128)S(1)} %get-tuple-element.98), channel_id=1, source_target_pairs={{0,192},{64,0},{128,64},{192,128},{1,193},{65,1},{129,65},{193,129... | collective-permute-start | bytes 1769480 | tf_op jit(solution)/shard_map/ppermute | solution.py:22
  141.8 3.5 %collective-permute-start.43 = (f32[64,128]{1,0:T(8,128)S(1)}, f32[64,128]{1,0:T(8,128)S(1)}, u32[]{:S(2)}, u32[]{:S(2)}) collective-permute-start(f32[64,128]{1,0:T(8,128)S(1)} %add.124), channel_id=1, source_target_pairs={{0,4},{2,6},{4,0},{6,2},{1,5},{3,7},{5,1},{7,3},{8,12},{10,14},{12... | collective-permute-start | bytes 98312 | tf_op jit(solution)/shard_map/ppermute | solution.py:22
  147.9 4.2 %collective-permute-done.38.refs_1_ = f32[72,2048]{1,0:T(8,128)S(1)} collective-permute-done((f32[72,2048]{1,0:T(8,128)S(1)}, f32[72,2048]{1,0:T(8,128)S(1)}, u32[]{:S(2)}, u32[]{:S(2)}) %collective-permute-start.38) | collective-permute-done | bytes 589856 | tf_op jit(solution)/shard_map/ppermute | solution.py:22
  152.1 3.7 %collective-permute-done.40.refs_3_ = f32[72,2048]{1,0:T(8,128)S(1)} collective-permute-done((f32[72,2048]{1,0:T(8,128)S(1)}, f32[72,2048]{1,0:T(8,128)S(1)}, u32[]{:S(2)}, u32[]{:S(2)}) %collective-permute-start.40) | collective-permute-done | bytes 589856 | tf_op jit(solution)/shard_map/ppermute | solution.py:22
  (91 shorter events, 49.3 us)
Async XLA Ops:
  1.5 8.5 %collective-permute-start.2 = (f32[4,2048]{1,0:T(4,128)S(1)}, f32[4,2048]{1,0:T(4,128)S(1)}, u32[]{:S(2)}, u32[]{:S(2)}) collective-permute-start(f32[4,2048]{1,0:T(4,128)S(1)} %get-tuple-element.111), channel_id=1, source_target_pairs={{0,64},{64,128},{128,192},{192,0},{1,65},{65,129},{129,193},{193,1... | collective-permute-start | bytes 98312 | tf_op jit(solution)/shard_map/ppermute | solution.py:22
  3.0 6.9 %collective-permute-start.1 = (f32[4,2048]{1,0:T(4,128)S(1)}, f32[4,2048]{1,0:T(4,128)S(1)}, u32[]{:S(2)}, u32[]{:S(2)}) collective-permute-start(f32[4,2048]{1,0:T(4,128)S(1)} %get-tuple-element.112), channel_id=1, source_target_pairs={{0,128},{64,192},{128,0},{192,64},{1,129},{65,193},{129,1},{193,65... | collective-permute-start | bytes 98312 | tf_op jit(solution)/shard_map/ppermute | solution.py:22
  10.8 34.6 %collective-permute-start.3 = (f32[64,2176]{1,0:T(8,128)}, f32[64,2176]{1,0:T(8,128)S(1)}, u32[]{:S(2)}, u32[]{:S(2)}) collective-permute-start(f32[64,2176]{1,0:T(8,128)} %get-tuple-element.60), channel_id=1, source_target_pairs={{0,192},{64,0},{128,64},{192,128},{1,193},{65,1},{129,65},{193,129... | collective-permute-start | bytes 1671176 | tf_op jit(solution)/shard_map/ppermute | solution.py:22
  13.2 32.2 %collective-permute-start.4 = (f32[64,2176]{1,0:T(8,128)}, f32[64,2176]{1,0:T(8,128)S(1)}, u32[]{:S(2)}, u32[]{:S(2)}) collective-permute-start(f32[64,2176]{1,0:T(8,128)} %get-tuple-element.61), channel_id=1, source_target_pairs={{0,128},{64,192},{128,0},{192,64},{1,129},{65,193},{129,1},{193,65... | collective-permute-start | bytes 1671176 | tf_op jit(solution)/shard_map/ppermute | solution.py:22
  13.6 31.9 %collective-permute-start.5 = (f32[64,2176]{1,0:T(8,128)}, f32[64,2176]{1,0:T(8,128)S(1)}, u32[]{:S(2)}, u32[]{:S(2)}) collective-permute-start(f32[64,2176]{1,0:T(8,128)} %get-tuple-element.62), channel_id=1, source_target_pairs={{0,64},{64,128},{128,192},{192,0},{1,65},{65,129},{129,193},{193,1... | collective-permute-start | bytes 1671176 | tf_op jit(solution)/shard_map/ppermute | solution.py:22
  14.2 8.4 %collective-permute-start.7 = (f32[16,2048]{1,0:T(8,128)S(1)}, f32[16,2048]{1,0:T(8,128)S(1)}, u32[]{:S(2)}, u32[]{:S(2)}) collective-permute-start(f32[16,2048]{1,0:T(8,128)S(1)} %pad_maximum_fusion.refs_0_), channel_id=1, source_target_pairs={{0,56},{8,0},{16,8},{24,16},{32,24},{40,32},{48,40},{56,48},{1,57}... | collective-permute-start | bytes 393224 | tf_op jit(solution)/shard_map/ppermute | solution.py:22
  20.1 6.2 %collective-permute-start.6 = (f32[16,2048]{1,0:T(8,128)S(1)}, f32[16,2048]{1,0:T(8,128)S(1)}, u32[]{:S(2)}, u32[]{:S(2)}) collective-permute-start(f32[16,2048]{1,0:T(8,128)S(1)} %pad_maximum_fusion.refs_0_), channel_id=1, source_target_pairs={{0,8},{8,16},{16,24},{24,32},{32,40},{40,48},{48,56},{56,0},{1,9},... | collective-permute-start | bytes 393224 | tf_op jit(solution)/shard_map/ppermute | solution.py:22
  26.2 6.6 %collective-permute-start.8 = (f32[16,2048]{1,0:T(8,128)S(1)}, f32[16,2048]{1,0:T(8,128)S(1)}, u32[]{:S(2)}, u32[]{:S(2)}) collective-permute-start(f32[16,2048]{1,0:T(8,128)S(1)} %collective-permute-done.6.refs_8_), channel_id=1, source_target_pairs={{0,8},{8,16},{16,24},{24,32},{32,40},{40,48},{48,56},{56,0},{1,9},... | collective-permute-start | bytes 393224 | tf_op jit(solution)/shard_map/ppermute | solution.py:22
  32.8 5.6 %collective-permute-start.11 = (f32[16,2048]{1,0:T(8,128)S(1)}, f32[16,2048]{1,0:T(8,128)S(1)}, u32[]{:S(2)}, u32[]{:S(2)}) collective-permute-start(f32[16,2048]{1,0:T(8,128)S(1)} %collective-permute-done.9.refs_2_), channel_id=1, source_target_pairs={{0,56},{8,0},{16,8},{24,16},{32,24},{40,32},{48,40},{56,48},{1,57}... | collective-permute-start | bytes 393224 | tf_op jit(solution)/shard_map/ppermute | solution.py:22
  32.9 6.9 %collective-permute-start.10 = (f32[16,2048]{1,0:T(8,128)S(1)}, f32[16,2048]{1,0:T(8,128)S(1)}, u32[]{:S(2)}, u32[]{:S(2)}) collective-permute-start(f32[16,2048]{1,0:T(8,128)S(1)} %collective-permute-done.8.refs_7_), channel_id=1, source_target_pairs={{0,8},{8,16},{16,24},{24,32},{32,40},{40,48},{48,56},{56,0},{1,9},... | collective-permute-start | bytes 393224 | tf_op jit(solution)/shard_map/ppermute | solution.py:22
  39.8 5.6 %collective-permute-start.12 = (f32[16,1024]{1,0:T(8,128)S(1)}, f32[16,1024]{1,0:T(8,128)S(1)}, u32[]{:S(2)}, u32[]{:S(2)}) collective-permute-start(f32[16,1024]{1,0:T(8,128)S(1)} %slice.36), channel_id=1, source_target_pairs={{0,8},{8,16},{16,24},{24,32},{32,40},{40,48},{48,56},{56,0},{1,9},... | collective-permute-start | bytes 196616 | tf_op jit(solution)/shard_map/ppermute | solution.py:22
  48.1 5.5 %collective-permute-start.17 = (f32[4,1,32,128]{3,2,1,0:T(8,128)S(1)}, f32[4,1,32,128]{3,2,1,0:T(8,128)S(1)}, u32[]{:S(2)}, u32[]{:S(2)}) collective-permute-start(f32[4,1,32,128]{3,2,1,0:T(8,128)S(1)} %dynamic-slice_add_fusion), channel_id=1, source_target_pairs={{0,192},{64,0},{128,64},{192,128},{1,193},{65,1},{129,65},{193,129... | collective-permute-start | bytes 196616 | tf_op jit(solution)/shard_map/ppermute | solution.py:22
  50.5 6.9 %collective-permute-start.16 = (f32[4,1,32,128]{3,2,1,0:T(8,128)S(1)}, f32[4,1,32,128]{3,2,1,0:T(8,128)S(1)}, u32[]{:S(2)}, u32[]{:S(2)}) collective-permute-start(f32[4,1,32,128]{3,2,1,0:T(8,128)S(1)} %dynamic-slice_add_fusion), channel_id=1, source_target_pairs={{0,64},{64,128},{128,192},{192,0},{1,65},{65,129},{129,193},{193,1... | collective-permute-start | bytes 196616 | tf_op jit(solution)/shard_map/ppermute | solution.py:22
  51.3 6.0 %collective-permute-start.15 = (f32[4,1,32,128]{3,2,1,0:T(8,128)S(1)}, f32[4,1,32,128]{3,2,1,0:T(8,128)S(1)}, u32[]{:S(2)}, u32[]{:S(2)}) collective-permute-start(f32[4,1,32,128]{3,2,1,0:T(8,128)S(1)} %dynamic-slice_add_fusion), channel_id=1, source_target_pairs={{0,128},{64,192},{128,0},{192,64},{1,129},{65,193},{129,1},{193,65... | collective-permute-start | bytes 196616 | tf_op jit(solution)/shard_map/ppermute | solution.py:22
  57.4 5.6 %collective-permute-start.20 = (f32[4,1,32,128]{3,2,1,0:T(8,128)S(1)}, f32[4,1,32,128]{3,2,1,0:T(8,128)S(1)}, u32[]{:S(2)}, u32[]{:S(2)}) collective-permute-start(f32[4,1,32,128]{3,2,1,0:T(8,128)S(1)} %fusion.8), channel_id=1, source_target_pairs={{0,6},{2,0},{4,2},{6,4},{1,7},{3,1},{5,3},{7,5},{8,14},{10,8},{12,... | collective-permute-start | bytes 196616 | tf_op jit(solution)/shard_map/ppermute | solution.py:22
  59.5 5.8 %collective-permute-start.18 = (f32[4,1,32,128]{3,2,1,0:T(8,128)S(1)}, f32[4,1,32,128]{3,2,1,0:T(8,128)S(1)}, u32[]{:S(2)}, u32[]{:S(2)}) collective-permute-start(f32[4,1,32,128]{3,2,1,0:T(8,128)S(1)} %fusion.8), channel_id=1, source_target_pairs={{0,4},{2,6},{4,0},{6,2},{1,5},{3,7},{5,1},{7,3},{8,12},{10,14},{12... | collective-permute-start | bytes 196616 | tf_op jit(solution)/shard_map/ppermute | solution.py:22
  67.8 5.9 %collective-permute-start.22 = (f32[16,1152]{1,0:T(8,128)S(1)}, f32[16,1152]{1,0:T(8,128)S(1)}, u32[]{:S(2)}, u32[]{:S(2)}) collective-permute-start(f32[16,1152]{1,0:T(8,128)S(1)} %get-tuple-element.71), channel_id=1, source_target_pairs={{0,8},{8,16},{16,24},{24,32},{32,40},{40,48},{48,56},{56,0},{1,9},... | collective-permute-start | bytes 221192 | tf_op jit(solution)/shard_map/ppermute | solution.py:22
  67.9 5.8 %collective-permute-start.23 = (f32[16,1152]{1,0:T(8,128)S(1)}, f32[16,1152]{1,0:T(8,128)S(1)}, u32[]{:S(2)}, u32[]{:S(2)}) collective-permute-start(f32[16,1152]{1,0:T(8,128)S(1)} %get-tuple-element.72), channel_id=1, source_target_pairs={{0,56},{8,0},{16,8},{24,16},{32,24},{40,32},{48,40},{56,48},{1,57}... | collective-permute-start | bytes 221192 | tf_op jit(solution)/shard_map/ppermute | solution.py:22
  73.8 6.6 %collective-permute-start.24 = (f32[16,2304]{1,0:T(8,128)S(1)}, f32[16,2304]{1,0:T(8,128)S(1)}, u32[]{:S(2)}, u32[]{:S(2)}) collective-permute-start(f32[16,2304]{1,0:T(8,128)S(1)} %get-tuple-element.77), channel_id=1, source_target_pairs={{0,8},{8,16},{16,24},{24,32},{32,40},{40,48},{48,56},{56,0},{1,9},... | collective-permute-start | bytes 442376 | tf_op jit(solution)/shard_map/ppermute | solution.py:22
  73.9 6.5 %collective-permute-start.25 = (f32[16,2304]{1,0:T(8,128)S(1)}, f32[16,2304]{1,0:T(8,128)S(1)}, u32[]{:S(2)}, u32[]{:S(2)}) collective-permute-start(f32[16,2304]{1,0:T(8,128)S(1)} %get-tuple-element.78), channel_id=1, source_target_pairs={{0,56},{8,0},{16,8},{24,16},{32,24},{40,32},{48,40},{56,48},{1,57}... | collective-permute-start | bytes 442376 | tf_op jit(solution)/shard_map/ppermute | solution.py:22
  80.4 5.8 %collective-permute-start.27 = (f32[16,2304]{1,0:T(8,128)S(1)}, f32[16,2304]{1,0:T(8,128)S(1)}, u32[]{:S(2)}, u32[]{:S(2)}) collective-permute-start(f32[16,2304]{1,0:T(8,128)S(1)} %add.118), channel_id=1, source_target_pairs={{0,56},{8,0},{16,8},{24,16},{32,24},{40,32},{48,40},{56,48},{1,57}... | collective-permute-start | bytes 442376 | tf_op jit(solution)/shard_map/ppermute | solution.py:22
  83.6 6.4 %collective-permute-start.26 = (f32[16,2304]{1,0:T(8,128)S(1)}, f32[16,2304]{1,0:T(8,128)S(1)}, u32[]{:S(2)}, u32[]{:S(2)}) collective-permute-start(f32[16,2304]{1,0:T(8,128)S(1)} %add.117), channel_id=1, source_target_pairs={{0,8},{8,16},{16,24},{24,32},{32,40},{40,48},{48,56},{56,0},{1,9},... | collective-permute-start | bytes 442376 | tf_op jit(solution)/shard_map/ppermute | solution.py:22
  90.1 6.6 %collective-permute-start.28 = (f32[16,2304]{1,0:T(8,128)S(1)}, f32[16,2304]{1,0:T(8,128)S(1)}, u32[]{:S(2)}, u32[]{:S(2)}) collective-permute-start(f32[16,2304]{1,0:T(8,128)S(1)} %add.119), channel_id=1, source_target_pairs={{0,8},{8,16},{16,24},{24,32},{32,40},{40,48},{48,56},{56,0},{1,9},... | collective-permute-start | bytes 442376 | tf_op jit(solution)/shard_map/ppermute | solution.py:22
  96.8 6.9 %collective-permute-start.31 = (f32[16,2304]{1,0:T(8,128)S(1)}, f32[16,2304]{1,0:T(8,128)S(1)}, u32[]{:S(2)}, u32[]{:S(2)}) collective-permute-start(f32[16,2304]{1,0:T(8,128)S(1)} %add_add_fusion.refs_4_), channel_id=1, source_target_pairs={{0,56},{8,0},{16,8},{24,16},{32,24},{40,32},{48,40},{56,48},{1,57}... | collective-permute-start | bytes 442376 | tf_op jit(solution)/shard_map/ppermute | solution.py:22
  97.1 7.8 %collective-permute-start.30 = (f32[16,2304]{1,0:T(8,128)S(1)}, f32[16,2304]{1,0:T(8,128)S(1)}, u32[]{:S(2)}, u32[]{:S(2)}) collective-permute-start(f32[16,2304]{1,0:T(8,128)S(1)} %add_add_fusion.refs_4_), channel_id=1, source_target_pairs={{0,8},{8,16},{16,24},{24,32},{32,40},{40,48},{48,56},{56,0},{1,9},... | collective-permute-start | bytes 442376 | tf_op jit(solution)/shard_map/ppermute | solution.py:22
  104.9 5.7 %collective-permute-start.33 = (f32[16,2304]{1,0:T(8,128)S(1)}, f32[16,2304]{1,0:T(8,128)S(1)}, u32[]{:S(2)}, u32[]{:S(2)}) collective-permute-start(f32[16,2304]{1,0:T(8,128)S(1)} %collective-permute-done.31.refs_5_), channel_id=1, source_target_pairs={{0,56},{8,0},{16,8},{24,16},{32,24},{40,32},{48,40},{56,48},{1,57}... | collective-permute-start | bytes 442376 | tf_op jit(solution)/shard_map/ppermute | solution.py:22
  104.9 6.9 %collective-permute-start.32 = (f32[16,2304]{1,0:T(8,128)S(1)}, f32[16,2304]{1,0:T(8,128)S(1)}, u32[]{:S(2)}, u32[]{:S(2)}) collective-permute-start(f32[16,2304]{1,0:T(8,128)S(1)} %collective-permute-done.30.refs_12_), channel_id=1, source_target_pairs={{0,8},{8,16},{16,24},{24,32},{32,40},{40,48},{48,56},{56,0},{1,9},... | collective-permute-start | bytes 442376 | tf_op jit(solution)/shard_map/ppermute | solution.py:22
  112.1 6.4 %collective-permute-start.34 = (f32[16,2304]{1,0:T(8,128)S(1)}, f32[16,2304]{1,0:T(8,128)S(1)}, u32[]{:S(2)}, u32[]{:S(2)}) collective-permute-start(f32[16,2304]{1,0:T(8,128)S(1)} %collective-permute-done.32.refs_11_), channel_id=1, source_target_pairs={{0,8},{8,16},{16,24},{24,32},{32,40},{40,48},{48,56},{56,0},{1,9},... | collective-permute-start | bytes 442376 | tf_op jit(solution)/shard_map/ppermute | solution.py:22
  118.5 5.6 %collective-permute-start.36 = (f32[16,1152]{1,0:T(8,128)S(1)}, f32[16,1152]{1,0:T(8,128)S(1)}, u32[]{:S(2)}, u32[]{:S(2)}) collective-permute-start(f32[16,1152]{1,0:T(8,128)S(1)} %slice.44), channel_id=1, source_target_pairs={{0,8},{8,16},{16,24},{24,32},{32,40},{40,48},{48,56},{56,0},{1,9},... | collective-permute-start | bytes 221192 | tf_op jit(solution)/shard_map/ppermute | solution.py:22
  133.0 19.2 %collective-permute-start.38 = (f32[72,2048]{1,0:T(8,128)S(1)}, f32[72,2048]{1,0:T(8,128)S(1)}, u32[]{:S(2)}, u32[]{:S(2)}) collective-permute-start(f32[72,2048]{1,0:T(8,128)S(1)} %get-tuple-element.98), channel_id=1, source_target_pairs={{0,192},{64,0},{128,64},{192,128},{1,193},{65,1},{129,65},{193,129... | collective-permute-start | bytes 1769480 | tf_op jit(solution)/shard_map/ppermute | solution.py:22
  135.1 17.0 %collective-permute-start.39 = (f32[72,2048]{1,0:T(8,128)S(1)}, f32[72,2048]{1,0:T(8,128)S(1)}, u32[]{:S(2)}, u32[]{:S(2)}) collective-permute-start(f32[72,2048]{1,0:T(8,128)S(1)} %get-tuple-element.99), channel_id=1, source_target_pairs={{0,128},{64,192},{128,0},{192,64},{1,129},{65,193},{129,1},{193,65... | collective-permute-start | bytes 1769480 | tf_op jit(solution)/shard_map/ppermute | solution.py:22
  136.7 19.1 %collective-permute-start.40 = (f32[72,2048]{1,0:T(8,128)S(1)}, f32[72,2048]{1,0:T(8,128)S(1)}, u32[]{:S(2)}, u32[]{:S(2)}) collective-permute-start(f32[72,2048]{1,0:T(8,128)S(1)} %get-tuple-element.100), channel_id=1, source_target_pairs={{0,64},{64,128},{128,192},{192,0},{1,65},{65,129},{129,193},{193,1... | collective-permute-start | bytes 1769480 | tf_op jit(solution)/shard_map/ppermute | solution.py:22
  (13 other events, 105.7 us)
where the time goes:
time: 159 us; the launch traced here: 158 us
  waiting for transfers between devices  74.1 us (47%)
  starting transfers between devices  64.3 us (40%)
  Pallas kernels  14.8 us (9%)
  other arithmetic  1.63 us (1%)
    ppermute x43, waiting for transfers between devices, moved(): return lax.ppermute(a, axis, [(i, (i + step) % n) for i in range(n)])  72 us
    ppermute x43, starting transfers between devices, moved(): return lax.ppermute(a, axis, [(i, (i + step) % n) for i in range(n)])  62.4 us
    pallas_call x6, Pallas kernels, call(): pl.pallas_call(body, out_shape=[jax.ShapeDtypeStruct(s, jnp.float32) for...  14.8 us
  transfers between devices with their start and end apart: 44, of which 31 were waited for; matrix products, arithmetic and copies ran while one was open for 0% of the time, Pallas kernels for 2%

commit v1 on v0

--- a/solution.py
+++ b/solution.py
@@ -124,54 +124,91 @@
             out[rows, half:wide] = ins[far + 1][...]
         else:
             out[rows, :wide] = ins[j + (j > far)][...]
-    out[:, wide:] = jnp.zeros((out.shape[0], out.shape[1] - wide), jnp.float32)
-
-
-def cut_kernel(k_ref, r_ref, *refs):
-    outs, (held, sems) = refs[:XS], refs[XS:]
-    rows, lanes = outs[0].shape
-    wide = k_ref.shape[1] // XS
-    copies = []
-    for j in reversed(range(XS)):
+
+
+def pack_kernel(b_hbm, r_hbm, *refs):
+    outs, (b_ref, r_ref, sems) = refs[:XS], refs[XS:]
+    copies = [pltpu.make_async_copy(r_hbm, r_ref, sems.at[0]), pltpu.make_async_copy(b_hbm, b_ref, sems.at[1])]
+    for copy in copies:
+        copy.start()
+    for copy in copies:
+        copy.wait()
+    wide = b_ref.shape[1] // XS
+    half = wide // 2
+    r = r_ref[...]
+    pairs = [
+        jnp.concatenate([r[16 * i : 16 * i + 8], r[16 * i + 8 : 16 * i + 16]], 1)
+        for i in range(r.shape[0] // 16)
+    ]
+    tail = jnp.concatenate(pairs, 1)
+    for j in range(XS):
         at = pl.multiple_of(lax.rem(lax.axis_index("x") + j, XS) * wide, 128)
-        copies.append(
-            pltpu.make_async_copy(k_ref.at[:, pl.ds(at, wide)], outs[j].at[:, pl.ds(0, wide)], sems.at[j])
-        )
-        copies[-1].start()
-    copies.append(pltpu.make_async_copy(r_ref, held, sems.at[XS]))
-    copies[-1].start()
-    pad = jnp.zeros((rows, lanes - wide - r_ref.shape[1]), jnp.float32)
-    copies[-1].wait()
-    tail = jnp.concatenate([held[...], pad], 1)
+        outs[j][: b_ref.shape[0], :half] = b_ref[:, pl.ds(at, half)]
+        outs[j][b_ref.shape[0] :, :half] = b_ref[:, pl.ds(at + half, half)]
+        outs[j][:, half:] = tail
+
+
+def unpack_kernel(*refs):
+    ins, (b_out, r_out) = refs[:XS], refs[XS:]
+    x = lax.axis_index("x")
+    half, own = b_out.shape[1] // 2, b_out.shape[0] // XS
+    rows = r_out.shape[0] // XS
+    resp = (ins[0].shape[1] - half) * 16 // (2 * rows)
+    r_out[...] = jnp.zeros(r_out.shape, jnp.float32)
+    for at, block in enumerate(in_order([ref[...] for ref in ins], x)):
+        b_out[at * own : (at + 1) * own, :half] = block[:own, :half]
+        b_out[at * own : (at + 1) * own, half:] = block[own : 2 * own, :half]
+        for i in range(rows // 16):
+            pair = block[:, half + 2 * resp * i : half + 2 * resp * (i + 1)]
+            r_out[at * rows + 16 * i : at * rows + 16 * i + 8, :resp] = pair[:, :resp]
+            r_out[at * rows + 16 * i + 8 : at * rows + 16 * i + 16, :resp] = pair[:, resp:]
+
+
+def cut_kernel(k_ref, *refs):
+    outs, (held, in_sems, out_sems) = refs[:XS], refs[XS:]
+    wide = outs[0].shape[1]
+    ins = []
     for j in range(XS):
-        outs[j][:, wide:] = tail
-    for copy in copies[:-1]:
+        at = pl.multiple_of(lax.rem(lax.axis_index("x") + j, XS) * wide, 128)
+        to = held.at[j - 1] if j else outs[0]
+        ins.append(pltpu.make_async_copy(k_ref.at[:, pl.ds(at, wide)], to, in_sems.at[j]))
+    back = [pltpu.make_async_copy(held.at[j - 1], outs[j], out_sems.at[j - 1]) for j in range(1, XS)]
+    for j in (1, 2, 3, 0):
+        ins[j].start()
+    for j in (1, 2, 3):
+        ins[j].wait()
+        back[j - 1].start()
+    ins[0].wait()
+    for copy in back:
         copy.wait()
 
 
 def joined_kernel(*refs):
     blocks, (d_ref, l_ref, sems) = refs[:XS], refs[XS:]
-    rows, wide = d_ref.shape[0], blocks[0].shape[1]
+    own, wide = l_ref.shape[0], d_ref.shape[1] // XS
     copies = []
     for j in range(XS):
         at = pl.multiple_of(lax.rem(lax.axis_index("x") + j, XS) * wide, 128)
         copies.append(
-            pltpu.make_async_copy(blocks[j].at[pl.ds(0, rows), :], d_ref.at[:, pl.ds(at, wide)], sems.at[j])
+            pltpu.make_async_copy(blocks[j].at[:, pl.ds(0, wide)], d_ref.at[:, pl.ds(at, wide)], sems.at[j])
         )
         copies[-1].start()
     for j in range(XS):
         at = pl.multiple_of(lax.rem(lax.axis_index("x") + j, XS) * wide, 128)
-        l_ref[:, pl.ds(at, wide)] = blocks[j][rows : rows + l_ref.shape[0], :]
+        for u in range(wide // 256):
+            low = blocks[j][SUB * u : SUB * u + own, wide:]
+            high = blocks[j][SUB * u + own : SUB * (u + 1), wide:]
+            l_ref[:, pl.ds(at + 128 * u, 128)] = low
+            l_ref[:, pl.ds(at + wide // 2 + 128 * u, 128)] = high
     for copy in copies:
         copy.wait()
 
 
-def parts_kernel(own, proj_ref, *refs):
+def parts_kernel(own, proj_ref, r_ref, *refs):
     k_refs, proj_out, part_refs = refs[:XS], refs[XS], refs[XS + 1 :]
     comp = proj_ref.shape[1]
     group, far = own * XS, ZS // 2
-    rows, lanes = k_refs[0].shape
-    wide = lanes - comp
+    rows, wide = k_refs[0].shape
     half = part_refs[far].shape[1]
     x, z = lax.axis_index("x"), lax.axis_index("z")
 
@@ -197,7 +234,7 @@
     def split(v):
         return [v[j * rows : (j + 1) * rows] for j in range(XS)]
 
-    right = jnp.concatenate([by_x(split(proj_abs)), by_x([k[:, wide:] for k in k_refs])], 1)
+    right = jnp.concatenate([by_x(split(proj_abs)), r_ref[...]], 1)
     put(wide, dot(by_x(split(proj)), right, ((0,), (0,))))
     top, rest = halves(proj)
     step = 512
@@ -209,21 +246,23 @@
 
 def inverse_factor(w_ref, v_ref, comp):
     row = lax.broadcasted_iota(jnp.int32, (PANEL, comp), 0)
-    v_ref[...] = jnp.where(
-        lax.broadcasted_iota(jnp.int32, (comp, comp), 0)
-        == lax.broadcasted_iota(jnp.int32, (comp, comp), 1),
-        1.0,
-        0.0,
-    )
-
-    def panel(p, _):
+    whole = lax.broadcasted_iota(jnp.int32, (comp, comp), 0)
+    v_ref[...] = jnp.where(whole == lax.broadcasted_iota(jnp.int32, (comp, comp), 1), 1.0, 0.0)
+
+    def panel(p, last):
+        last_w, last_v = last
         rows = pl.ds(pl.multiple_of(p * PANEL, PANEL), PANEL)
-        w, v = w_ref[rows, :], v_ref[rows, :]
-        turned = pltpu.roll(w, (comp - p * PANEL) % comp, 1)
+        shift = (comp - p * PANEL) % comp
+        both = jnp.concatenate([last_w, last_v], 1)
+        near = dot(pltpu.roll(last_w, shift, 1)[:, :PANEL], both, ((0,), (0,)))
+        w, v = w_ref[rows, :] - near[:, :comp], v_ref[rows, :] - near[:, comp:]
+        change = dot(last_w, both, ((0,), (0,)))
+        w_ref[...] = w_ref[...] - change[:, :comp]
+        v_ref[...] = v_ref[...] - jnp.where(whole >= (p + 1) * PANEL, change[:, comp:], 0.0)
+        turned = pltpu.roll(w, shift, 1)
         cols = [jnp.broadcast_to(turned[:, i : i + 1], (PANEL, comp)) for i in range(PANEL)]
         for i in range(PANEL):
-            pivot = jnp.broadcast_to(cols[i][i : i + 1, :], (PANEL, comp))
-            scale = lax.rsqrt(pivot)
+            scale = lax.rsqrt(jnp.broadcast_to(cols[i][i : i + 1, :], (PANEL, comp)))
             times = cols[i] * scale
 
             def step(a):
@@ -233,13 +272,10 @@
             w, v = step(w), step(v)
             cols = [step(c) if k > i else c for k, c in enumerate(cols)]
         v_ref[rows, :] = v
-        below = lax.broadcasted_iota(jnp.int32, (comp, comp), 0) >= (p + 1) * PANEL
-        change = dot(w, jnp.concatenate([w, v], 1), ((0,), (0,)))
-        w_ref[...] = w_ref[...] - change[:, :comp]
-        v_ref[...] = v_ref[...] - jnp.where(below, change[:, comp:], 0.0)
-        return 0
-
-    lax.fori_loop(0, comp // PANEL, panel, 0)
+        return w, v
+
+    zero = jnp.zeros((PANEL, comp), jnp.float32)
+    lax.fori_loop(0, comp // PANEL, panel, (zero, zero))
 
 
 def finish_kernel(own, row_count, *refs):
@@ -249,8 +285,7 @@
     w_ref, v_ref, small_ref, raw_ref = refs[-4:]
     comp = proj_ref.shape[1]
     group = own * XS
-    rows = k_refs[0].shape[0]
-    wide = k_refs[0].shape[1] - comp
+    rows, wide = k_refs[0].shape
     resp = resp_ref.shape[1]
     root_rows = math.sqrt(row_count)
     x, z = lax.axis_index("x"), lax.axis_index("z")
@@ -282,8 +317,8 @@
 
     at = lax.broadcasted_iota(jnp.int32, (XS * SUB, comp), 0)
     to = lax.broadcasted_iota(jnp.int32, (XS * SUB, comp), 1)
-    wanted = (((x + at // SUB) % XS) * ZS + z) * own + at % SUB
-    pick = jnp.where((wanted == to) & (at % SUB < own), 1.0, 0.0)
+    wanted = (((x + at // SUB) % XS) * ZS + z) * own + at % own
+    pick = jnp.where(wanted == to, 1.0, 0.0)
     picks = dot(pick, inv_place, ((1,), (0,))) * (1.0 / root_rows)
     left = []
     for j in range(XS):
@@ -291,6 +326,7 @@
     left = jnp.concatenate(left, 0)
     left_top, left_rest = halves(left)
     step = 512
+    upper = lax.broadcasted_iota(jnp.int32, (SUB, 128), 0) < own
 
     def tile(t, _):
         at = pl.ds(pl.multiple_of(t * step, step), step)
@@ -302,7 +338,13 @@
         for j in range(XS):
             base = j * (rows + SUB)
             d_refs[j][:rows, at] = k_refs[j][:, at] - out[base : base + rows]
-            d_refs[j][rows:, at] = out[base + rows : base + rows + SUB]
+            both = out[base + rows : base + rows + SUB]
+            for u in range(step // 128):
+                spot = pl.ds(pl.multiple_of((t % (wide // 2 // step) * (step // 128) + u) * SUB, SUB), SUB)
+                kept = upper == (t < wide // 2 // step)
+                d_refs[j][spot, wide:] = jnp.where(
+                    kept, both[:, 128 * u : 128 * (u + 1)], d_refs[j][spot, wide:]
+                )
         return 0
 
     lax.fori_loop(0, wide // step, tile, 0)
@@ -316,29 +358,42 @@
     row_count = rows * XS * ZS
     resp_count = resp * YS * CS
     wide = cols // XS
-    x, c = lax.axis_index("x"), lax.axis_index("c")
+    c = lax.axis_index("c")
     hbm, vmem = pl.ANY, pltpu.VMEM
     dma = [pltpu.SemaphoreType.DMA((XS,))]
 
+    packed = [(2 * own, wide // 2 + rows // 16 * 2 * resp)] * XS
     basis_t = basis.T
     b_blocks = exchanged(
-        [lax.dynamic_slice(basis_t, (0, ((x + j) % XS) * wide), (own, wide)) for j in range(XS)]
+        call(
+            pack_kernel,
+            packed,
+            [pltpu.with_memory_space_constraint(a, pltpu.HBM) for a in (basis_t, responses)],
+            4,
+            [pltpu.HBM] * 2,
+            None,
+            [pltpu.VMEM(a.shape, jnp.float32) for a in (basis_t, responses)] + [pltpu.SemaphoreType.DMA((2,))],
+        )
     )
-    lanes = wide + comp
     k_blocks = call(
         cut_kernel,
-        [(rows, lanes)] * XS,
-        [pltpu.with_memory_space_constraint(a, pltpu.HBM) for a in (kernel, responses)],
+        [(rows, wide)] * XS,
+        [pltpu.with_memory_space_constraint(kernel, pltpu.HBM)],
         8,
-        [pltpu.HBM] * 2,
-        None,
-        [pltpu.VMEM((rows, resp), jnp.float32), pltpu.SemaphoreType.DMA((XS + 1,))],
+        [pltpu.HBM],
+        [vmem] + [pltpu.HBM] * (XS - 1),
+        [
+            pltpu.VMEM((XS - 1, rows, wide), jnp.float32),
+            pltpu.SemaphoreType.DMA((XS,)),
+            pltpu.SemaphoreType.DMA((XS - 1,)),
+        ],
     )
-    first = jnp.concatenate(in_order(b_blocks, x), 0)
+    group = own * XS
+    first, r_all = call(unpack_kernel, [(group, wide), (XS * rows, comp)], b_blocks, 4)
     first, *k_blocks = lax.optimization_barrier((first, *k_blocks))
     k_blocks = exchanged(k_blocks)
     b_parts = ring_gather(first)
-    (b_all,) = call(stacked_kernel, [(comp, lanes)], b_parts, 8)
+    (b_all,) = call(stacked_kernel, [(comp, wide)], b_parts, 8)
     k_all = jnp.concatenate(k_blocks, 0)
 
     proj = dot(k_all, b_all, ((1,), (1,)), HIGH).reshape(XS, CS, rows // CS, comp)
@@ -353,16 +408,16 @@
     proj = jnp.concatenate([jnp.where(c == 0, proj, other), jnp.where(c == 0, other, proj)], 1)
     proj = proj.reshape(XS * rows, comp)
 
-    group, full = own * XS, lanes + comp
+    full = wide + 2 * comp
     shapes = [(group, full)] * (ZS + 1)
     shapes[ZS // 2 : ZS // 2 + 2] = [(group, full // 2)] * 2
     proj_abs, *parts = call(
-        functools.partial(parts_kernel, own), [(XS * rows, comp)] + shapes, [proj, *k_blocks], 24
+        functools.partial(parts_kernel, own), [(XS * rows, comp)] + shapes, [proj, r_all, *k_blocks], 24
     )
     total = ring_gather(ring_scatter(parts))
     scores, weights, nxt, *d_blocks = call(
         functools.partial(finish_kernel, own, row_count),
-        [(rows, comp), (resp, comp), (rows, comp)] + [(rows + SUB, wide)] * XS,
+        [(rows, comp), (resp, comp), (rows, comp)] + [(rows, wide + comp)] * XS,
         [*k_blocks, *total, proj_abs, responses],
         24,
         None,
@@ -371,9 +426,7 @@
     )
     d_blocks = exchanged(d_blocks)
     basis_next = summed_col(nxt) / math.sqrt(resp_count)
-    deflated, loadings = call(
-        joined_kernel, [(rows, cols), (own, cols)], d_blocks, 8, None, [hbm, vmem], dma
-    )
+    deflated, loadings = call(joined_kernel, [(rows, cols), (own, cols)], d_blocks, 8, None, [hbm, vmem], dma)
     return (scores, loadings, weights, deflated, basis_next)
 
 

time: 159 us -> 157 us (0.987)
    pallas_call x6 -> x8, Pallas kernels: 14.8 us -> 15.3 us  [call(): pl.pallas_call(body, out_shape=[jax.ShapeDtypeStruct(s, jnp.float32) for...]
  transfers between devices with their start and end apart: 44 -> 44, of which waited for: 31 -> 33; matrix products, arithmetic and copies ran while one was open for 0% -> 0% of each run, Pallas kernels for 2% -> 1%
where the time goes in v1:
time: 157 us; the launch traced here: 155 us
  waiting for transfers between devices  74.1 us (47%)
  starting transfers between devices  63 us (40%)
  Pallas kernels  15.3 us (10%)
    ppermute x43, waiting for transfers between devices, moved(): return lax.ppermute(a, axis, [(i, (i + step) % n) for i in range(n)])  72 us
    ppermute x43, starting transfers between devices, moved(): return lax.ppermute(a, axis, [(i, (i + step) % n) for i in range(n)])  61.1 us
    pallas_call x8, Pallas kernels, call(): pl.pallas_call(body, out_shape=[jax.ShapeDtypeStruct(s, jnp.float32) for...  15.3 us
  transfers between devices with their start and end apart: 44, of which 33 were waited for; matrix products, arithmetic and copies ran while one was open for 0% of the time, Pallas kernels for 1%

profile of v1, /device:TPU:8, one launch (start us, length us, event | category | flops | bytes accessed | tf_op | source)
XLA Modules:
  0.0 155.3 jit_solution(6117718203951478531)
XLA Ops:
  1.7 2.8 %collective-permute-start = (f32[8,1536]{1,0:T(8,128)S(1)}, f32[8,1536]{1,0:T(8,128)S(1)}, u32[]{:S(2)}, u32[]{:S(2)}) collective-permute-start(f32[8,1536]{1,0:T(8,128)S(1)} %get-tuple-element.62), channel_id=1, source_target_pairs={{0,192},{64,0},{128,64},{192,128},{1,193},{65,1},{129,65},{193,129... | collective-permute-start | bytes 147464 | tf_op jit(solution)/shard_map/ppermute | solution.py:22
  6.2 2.2 %shard_map.76 = (f32[64,2048]{1,0:T(8,128)S(1)}, f32[64,2048]{1,0:T(8,128)}, f32[64,2048]{1,0:T(8,128)}, f32[64,2048]{1,0:T(8,128)}) custom-call(f32[64,8192]{1,0:T(8,128)} %k_ref.1), custom_call_target="tpu_custom_call" | custom-call | tf_op jit(solution)/shard_map/pallas_call | solution.py:57
  13.7 5.9 %collective-permute-start.7 = (f32[16,2048]{1,0:T(8,128)S(1)}, f32[16,2048]{1,0:T(8,128)S(1)}, u32[]{:S(2)}, u32[]{:S(2)}) collective-permute-start(f32[16,2048]{1,0:T(8,128)S(1)} %get-tuple-element.74.refs_0_), channel_id=1, source_target_pairs={{0,56},{8,0},{16,8},{24,16},{32,24},{40,32},{48,40},{56,48},{1,57}... | collective-permute-start | bytes 393224 | tf_op jit(solution)/shard_map/ppermute | solution.py:22
  19.6 2.5 %collective-permute-done.7.refs_1_ = f32[16,2048]{1,0:T(8,128)S(1)} collective-permute-done((f32[16,2048]{1,0:T(8,128)S(1)}, f32[16,2048]{1,0:T(8,128)S(1)}, u32[]{:S(2)}, u32[]{:S(2)}) %collective-permute-start.7) | collective-permute-done | bytes 131104 | tf_op jit(solution)/shard_map/ppermute | solution.py:22
  22.1 3.7 %collective-permute-done.6.refs_8_ = f32[16,2048]{1,0:T(8,128)S(1)} collective-permute-done((f32[16,2048]{1,0:T(8,128)S(1)}, f32[16,2048]{1,0:T(8,128)S(1)}, u32[]{:S(2)}, u32[]{:S(2)}) %collective-permute-start.6) | collective-permute-done | bytes 131104 | tf_op jit(solution)/shard_map/ppermute | solution.py:22
  27.8 3.5 %collective-permute-done.9.refs_2_ = f32[16,2048]{1,0:T(8,128)S(1)} collective-permute-done((f32[16,2048]{1,0:T(8,128)S(1)}, f32[16,2048]{1,0:T(8,128)S(1)}, u32[]{:S(2)}, u32[]{:S(2)}) %collective-permute-start.9) | collective-permute-done | bytes 131104 | tf_op jit(solution)/shard_map/ppermute | solution.py:22
  34.6 3.6 %collective-permute-done.11.refs_3_ = f32[16,2048]{1,0:T(8,128)S(1)} collective-permute-done((f32[16,2048]{1,0:T(8,128)S(1)}, f32[16,2048]{1,0:T(8,128)S(1)}, u32[]{:S(2)}, u32[]{:S(2)}) %collective-permute-start.11) | collective-permute-done | bytes 131104 | tf_op jit(solution)/shard_map/ppermute | solution.py:22
  39.7 3.2 %collective-permute-start.13 = (f32[16,1024]{1,0:T(8,128)S(1)}, f32[16,1024]{1,0:T(8,128)S(1)}, u32[]{:S(2)}, u32[]{:S(2)}) collective-permute-start(f32[16,1024]{1,0:T(8,128)S(1)} %slice.37), channel_id=1, source_target_pairs={{0,56},{8,0},{16,8},{24,16},{32,24},{40,32},{48,40},{56,48},{1,57}... | collective-permute-start | bytes 196616 | tf_op jit(solution)/shard_map/ppermute | solution.py:22
  42.8 2.2 %collective-permute-done.12.refs_4_ = f32[16,1024]{1,0:T(8,128)S(1)} collective-permute-done((f32[16,1024]{1,0:T(8,128)S(1)}, f32[16,1024]{1,0:T(8,128)S(1)}, u32[]{:S(2)}, u32[]{:S(2)}) %collective-permute-start.12) | collective-permute-done | bytes 65568 | tf_op jit(solution)/shard_map/ppermute | solution.py:22
  49.9 3.1 %collective-permute-start.15 = (f32[4,1,32,128]{3,2,1,0:T(8,128)S(1)}, f32[4,1,32,128]{3,2,1,0:T(8,128)S(1)}, u32[]{:S(2)}, u32[]{:S(2)}) collective-permute-start(f32[4,1,32,128]{3,2,1,0:T(8,128)S(1)} %dynamic-slice_add_fusion), channel_id=1, source_target_pairs={{0,128},{64,192},{128,0},{192,64},{1,129},{65,193},{129,1},{193,65... | collective-permute-start | bytes 196616 | tf_op jit(solution)/shard_map/ppermute | solution.py:22
  53.0 2.5 %collective-permute-done.16 = f32[4,1,32,128]{3,2,1,0:T(8,128)S(1)} collective-permute-done((f32[4,1,32,128]{3,2,1,0:T(8,128)S(1)}, f32[4,1,32,128]{3,2,1,0:T(8,128)S(1)}, u32[]{:S(2)}, u32[]{:S(2)}) %collective-permute-start.16) | collective-permute-done | bytes 65568 | tf_op jit(solution)/shard_map/ppermute | solution.py:22
  58.3 3.5 %collective-permute-start.18 = (f32[4,1,32,128]{3,2,1,0:T(8,128)S(1)}, f32[4,1,32,128]{3,2,1,0:T(8,128)S(1)}, u32[]{:S(2)}, u32[]{:S(2)}) collective-permute-start(f32[4,1,32,128]{3,2,1,0:T(8,128)S(1)} %fusion.8), channel_id=1, source_target_pairs={{0,4},{2,6},{4,0},{6,2},{1,5},{3,7},{5,1},{7,3},{8,12},{10,14},{12... | collective-permute-start | bytes 196616 | tf_op jit(solution)/shard_map/ppermute | solution.py:22
  67.3 2.8 %collective-permute-start.23 = (f32[16,1152]{1,0:T(8,128)S(1)}, f32[16,1152]{1,0:T(8,128)S(1)}, u32[]{:S(2)}, u32[]{:S(2)}) collective-permute-start(f32[16,1152]{1,0:T(8,128)S(1)} %get-tuple-element.84), channel_id=1, source_target_pairs={{0,56},{8,0},{16,8},{24,16},{32,24},{40,32},{48,40},{56,48},{1,57}... | collective-permute-start | bytes 221192 | tf_op jit(solution)/shard_map/ppermute | solution.py:22
  70.1 2.5 %collective-permute-done.22.up_ref = f32[16,1152]{1,0:T(8,128)S(1)} collective-permute-done((f32[16,1152]{1,0:T(8,128)S(1)}, f32[16,1152]{1,0:T(8,128)S(1)}, u32[]{:S(2)}, u32[]{:S(2)}) %collective-permute-start.22) | collective-permute-done | bytes 73760 | tf_op jit(solution)/shard_map/ppermute | solution.py:22
  72.7 3.2 %collective-permute-start.25 = (f32[16,2304]{1,0:T(8,128)S(1)}, f32[16,2304]{1,0:T(8,128)S(1)}, u32[]{:S(2)}, u32[]{:S(2)}) collective-permute-start(f32[16,2304]{1,0:T(8,128)S(1)} %get-tuple-element.90), channel_id=1, source_target_pairs={{0,56},{8,0},{16,8},{24,16},{32,24},{40,32},{48,40},{56,48},{1,57}... | collective-permute-start | bytes 442376 | tf_op jit(solution)/shard_map/ppermute | solution.py:22
  75.9 3.3 %collective-permute-done.24 = f32[16,2304]{1,0:T(8,128)S(1)} collective-permute-done((f32[16,2304]{1,0:T(8,128)S(1)}, f32[16,2304]{1,0:T(8,128)S(1)}, u32[]{:S(2)}, u32[]{:S(2)}) %collective-permute-start.24) | collective-permute-done | bytes 147488 | tf_op jit(solution)/shard_map/ppermute | solution.py:22
  79.3 3.1 %collective-permute-start.27 = (f32[16,2304]{1,0:T(8,128)S(1)}, f32[16,2304]{1,0:T(8,128)S(1)}, u32[]{:S(2)}, u32[]{:S(2)}) collective-permute-start(f32[16,2304]{1,0:T(8,128)S(1)} %add.73), channel_id=1, source_target_pairs={{0,56},{8,0},{16,8},{24,16},{32,24},{40,32},{48,40},{56,48},{1,57}... | collective-permute-start | bytes 442376 | tf_op jit(solution)/shard_map/ppermute | solution.py:22
  82.5 2.6 %collective-permute-done.27 = f32[16,2304]{1,0:T(8,128)S(1)} collective-permute-done((f32[16,2304]{1,0:T(8,128)S(1)}, f32[16,2304]{1,0:T(8,128)S(1)}, u32[]{:S(2)}, u32[]{:S(2)}) %collective-permute-start.27) | collective-permute-done | bytes 147488 | tf_op jit(solution)/shard_map/ppermute | solution.py:22
  85.1 3.8 %collective-permute-done.26 = f32[16,2304]{1,0:T(8,128)S(1)} collective-permute-done((f32[16,2304]{1,0:T(8,128)S(1)}, f32[16,2304]{1,0:T(8,128)S(1)}, u32[]{:S(2)}, u32[]{:S(2)}) %collective-permute-start.26) | collective-permute-done | bytes 147488 | tf_op jit(solution)/shard_map/ppermute | solution.py:22
  89.0 2.1 %collective-permute-start.28 = (f32[16,2304]{1,0:T(8,128)S(1)}, f32[16,2304]{1,0:T(8,128)S(1)}, u32[]{:S(2)}, u32[]{:S(2)}) collective-permute-start(f32[16,2304]{1,0:T(8,128)S(1)} %add.74), channel_id=1, source_target_pairs={{0,8},{8,16},{16,24},{24,32},{32,40},{40,48},{48,56},{56,0},{1,9},... | collective-permute-start | bytes 442376 | tf_op jit(solution)/shard_map/ppermute | solution.py:22
  91.1 3.2 %collective-permute-done.29 = f32[16,2304]{1,0:T(8,128)S(1)} collective-permute-done((f32[16,2304]{1,0:T(8,128)S(1)}, f32[16,2304]{1,0:T(8,128)S(1)}, u32[]{:S(2)}, u32[]{:S(2)}) %collective-permute-start.29) | collective-permute-done | bytes 147488 | tf_op jit(solution)/shard_map/ppermute | solution.py:22
  98.0 4.6 %collective-permute-done.31.refs_5_ = f32[16,2304]{1,0:T(8,128)S(1)} collective-permute-done((f32[16,2304]{1,0:T(8,128)S(1)}, f32[16,2304]{1,0:T(8,128)S(1)}, u32[]{:S(2)}, u32[]{:S(2)}) %collective-permute-start.31) | collective-permute-done | bytes 147488 | tf_op jit(solution)/shard_map/ppermute | solution.py:22
  105.8 3.6 %collective-permute-done.33.refs_6_ = f32[16,2304]{1,0:T(8,128)S(1)} collective-permute-done((f32[16,2304]{1,0:T(8,128)S(1)}, f32[16,2304]{1,0:T(8,128)S(1)}, u32[]{:S(2)}, u32[]{:S(2)}) %collective-permute-start.33) | collective-permute-done | bytes 147488 | tf_op jit(solution)/shard_map/ppermute | solution.py:22
  112.7 3.1 %collective-permute-done.35.refs_7_ = f32[16,2304]{1,0:T(8,128)S(1)} collective-permute-done((f32[16,2304]{1,0:T(8,128)S(1)}, f32[16,2304]{1,0:T(8,128)S(1)}, u32[]{:S(2)}, u32[]{:S(2)}) %collective-permute-start.35) | collective-permute-done | bytes 147488 | tf_op jit(solution)/shard_map/ppermute | solution.py:22
  117.9 2.7 %collective-permute-start.37 = (f32[16,1152]{1,0:T(8,128)S(1)}, f32[16,1152]{1,0:T(8,128)S(1)}, u32[]{:S(2)}, u32[]{:S(2)}) collective-permute-start(f32[16,1152]{1,0:T(8,128)S(1)} %slice.45), channel_id=1, source_target_pairs={{0,56},{8,0},{16,8},{24,16},{32,24},{40,32},{48,40},{56,48},{1,57}... | collective-permute-start | bytes 221192 | tf_op jit(solution)/shard_map/ppermute | solution.py:22
  120.6 2.3 %collective-permute-done.36.refs_8_ = f32[16,1152]{1,0:T(8,128)S(1)} collective-permute-done((f32[16,1152]{1,0:T(8,128)S(1)}, f32[16,1152]{1,0:T(8,128)S(1)}, u32[]{:S(2)}, u32[]{:S(2)}) %collective-permute-start.36) | collective-permute-done | bytes 73760 | tf_op jit(solution)/shard_map/ppermute | solution.py:22
  123.0 8.7 %shard_map.80 = (f32[64,128]{1,0:T(8,128)}, f32[64,128]{1,0:T(8,128)}, f32[64,128]{1,0:T(8,128)S(1)}, f32[64,2176]{1,0:T(8,128)S(1)}, f32[64,2176]{1,0:T(8,128)S...) custom-call(f32[64,2048]{1,0:T(8,128)S(1)} %get-tuple-element.70.refs_0_, ...), custom_call_target="tpu_custom_call" | custom-call | tf_op jit(solution)/shard_map/pallas_call | solution.py:57
  131.7 2.2 %collective-permute-start.38 = (f32[64,2176]{1,0:T(8,128)S(1)}, f32[64,2176]{1,0:T(8,128)S(1)}, u32[]{:S(2)}, u32[]{:S(2)}) collective-permute-start(f32[64,2176]{1,0:T(8,128)S(1)} %get-tuple-element.110), channel_id=1, source_target_pairs={{0,192},{64,0},{128,64},{192,128},{1,193},{65,1},{129,65},{193,129... | collective-permute-start | bytes 1671176 | tf_op jit(solution)/shard_map/ppermute | solution.py:22
  138.7 2.1 %collective-permute-done.42 = f32[64,128]{1,0:T(8,128)S(1)} collective-permute-done((f32[64,128]{1,0:T(8,128)S(1)}, f32[64,128]{1,0:T(8,128)S(1)}, u32[]{:S(2)}, u32[]{:S(2)}) %collective-permute-start.42) | collective-permute-done | bytes 32800 | tf_op jit(solution)/shard_map/ppermute | solution.py:104
  140.7 3.5 %collective-permute-start.43 = (f32[64,128]{1,0:T(8,128)S(1)}, f32[64,128]{1,0:T(8,128)S(1)}, u32[]{:S(2)}, u32[]{:S(2)}) collective-permute-start(f32[64,128]{1,0:T(8,128)S(1)} %add.79), channel_id=1, source_target_pairs={{0,4},{2,6},{4,0},{6,2},{1,5},{3,7},{5,1},{7,3},{8,12},{10,14},{12... | collective-permute-start | bytes 98312 | tf_op jit(solution)/shard_map/ppermute | solution.py:22
  146.8 2.7 %collective-permute-done.38.refs_1_ = f32[64,2176]{1,0:T(8,128)S(1)} collective-permute-done((f32[64,2176]{1,0:T(8,128)S(1)}, f32[64,2176]{1,0:T(8,128)S(1)}, u32[]{:S(2)}, u32[]{:S(2)}) %collective-permute-start.38) | collective-permute-done | bytes 557088 | tf_op jit(solution)/shard_map/ppermute | solution.py:22
  149.5 3.7 %collective-permute-done.40.refs_3_ = f32[64,2176]{1,0:T(8,128)S(1)} collective-permute-done((f32[64,2176]{1,0:T(8,128)S(1)}, f32[64,2176]{1,0:T(8,128)S(1)}, u32[]{:S(2)}, u32[]{:S(2)}) %collective-permute-start.40) | collective-permute-done | bytes 557088 | tf_op jit(solution)/shard_map/ppermute | solution.py:22
  (90 shorter events, 49.8 us)
Async XLA Ops:
  1.7 6.8 %collective-permute-start = (f32[8,1536]{1,0:T(8,128)S(1)}, f32[8,1536]{1,0:T(8,128)S(1)}, u32[]{:S(2)}, u32[]{:S(2)}) collective-permute-start(f32[8,1536]{1,0:T(8,128)S(1)} %get-tuple-element.62), channel_id=1, source_target_pairs={{0,192},{64,0},{128,64},{192,128},{1,193},{65,1},{129,65},{193,129... | collective-permute-start | bytes 147464 | tf_op jit(solution)/shard_map/ppermute | solution.py:22
  4.5 5.6 %collective-permute-start.1 = (f32[8,1536]{1,0:T(8,128)S(1)}, f32[8,1536]{1,0:T(8,128)S(1)}, u32[]{:S(2)}, u32[]{:S(2)}) collective-permute-start(f32[8,1536]{1,0:T(8,128)S(1)} %get-tuple-element.63), channel_id=1, source_target_pairs={{0,128},{64,192},{128,0},{192,64},{1,129},{65,193},{129,1},{193,65... | collective-permute-start | bytes 147464 | tf_op jit(solution)/shard_map/ppermute | solution.py:22
  10.7 34.4 %collective-permute-start.3 = (f32[64,2048]{1,0:T(8,128)}, f32[64,2048]{1,0:T(8,128)S(1)}, u32[]{:S(2)}, u32[]{:S(2)}) collective-permute-start(f32[64,2048]{1,0:T(8,128)} %get-tuple-element.71), channel_id=1, source_target_pairs={{0,192},{64,0},{128,64},{192,128},{1,193},{65,1},{129,65},{193,129... | collective-permute-start | bytes 1572872 | tf_op jit(solution)/shard_map/ppermute | solution.py:22
  11.4 33.8 %collective-permute-start.4 = (f32[64,2048]{1,0:T(8,128)}, f32[64,2048]{1,0:T(8,128)S(1)}, u32[]{:S(2)}, u32[]{:S(2)}) collective-permute-start(f32[64,2048]{1,0:T(8,128)} %get-tuple-element.72), channel_id=1, source_target_pairs={{0,128},{64,192},{128,0},{192,64},{1,129},{65,193},{129,1},{193,65... | collective-permute-start | bytes 1572872 | tf_op jit(solution)/shard_map/ppermute | solution.py:22
  12.5 32.6 %collective-permute-start.5 = (f32[64,2048]{1,0:T(8,128)}, f32[64,2048]{1,0:T(8,128)S(1)}, u32[]{:S(2)}, u32[]{:S(2)}) collective-permute-start(f32[64,2048]{1,0:T(8,128)} %get-tuple-element.73), channel_id=1, source_target_pairs={{0,64},{64,128},{128,192},{192,0},{1,65},{65,129},{129,193},{193,1... | collective-permute-start | bytes 1572872 | tf_op jit(solution)/shard_map/ppermute | solution.py:22
  13.7 8.4 %collective-permute-start.7 = (f32[16,2048]{1,0:T(8,128)S(1)}, f32[16,2048]{1,0:T(8,128)S(1)}, u32[]{:S(2)}, u32[]{:S(2)}) collective-permute-start(f32[16,2048]{1,0:T(8,128)S(1)} %get-tuple-element.74.refs_0_), channel_id=1, source_target_pairs={{0,56},{8,0},{16,8},{24,16},{32,24},{40,32},{48,40},{56,48},{1,57}... | collective-permute-start | bytes 393224 | tf_op jit(solution)/shard_map/ppermute | solution.py:22
  19.6 6.2 %collective-permute-start.6 = (f32[16,2048]{1,0:T(8,128)S(1)}, f32[16,2048]{1,0:T(8,128)S(1)}, u32[]{:S(2)}, u32[]{:S(2)}) collective-permute-start(f32[16,2048]{1,0:T(8,128)S(1)} %get-tuple-element.74.refs_0_), channel_id=1, source_target_pairs={{0,8},{8,16},{16,24},{24,32},{32,40},{40,48},{48,56},{56,0},{1,9},... | collective-permute-start | bytes 393224 | tf_op jit(solution)/shard_map/ppermute | solution.py:22
  25.8 5.6 %collective-permute-start.9 = (f32[16,2048]{1,0:T(8,128)S(1)}, f32[16,2048]{1,0:T(8,128)S(1)}, u32[]{:S(2)}, u32[]{:S(2)}) collective-permute-start(f32[16,2048]{1,0:T(8,128)S(1)} %collective-permute-done.7.refs_1_), channel_id=1, source_target_pairs={{0,56},{8,0},{16,8},{24,16},{32,24},{40,32},{48,40},{56,48},{1,57}... | collective-permute-start | bytes 393224 | tf_op jit(solution)/shard_map/ppermute | solution.py:22
  25.8 6.8 %collective-permute-start.8 = (f32[16,2048]{1,0:T(8,128)S(1)}, f32[16,2048]{1,0:T(8,128)S(1)}, u32[]{:S(2)}, u32[]{:S(2)}) collective-permute-start(f32[16,2048]{1,0:T(8,128)S(1)} %collective-permute-done.6.refs_8_), channel_id=1, source_target_pairs={{0,8},{8,16},{16,24},{24,32},{32,40},{40,48},{48,56},{56,0},{1,9},... | collective-permute-start | bytes 393224 | tf_op jit(solution)/shard_map/ppermute | solution.py:22
  32.6 5.7 %collective-permute-start.11 = (f32[16,2048]{1,0:T(8,128)S(1)}, f32[16,2048]{1,0:T(8,128)S(1)}, u32[]{:S(2)}, u32[]{:S(2)}) collective-permute-start(f32[16,2048]{1,0:T(8,128)S(1)} %collective-permute-done.9.refs_2_), channel_id=1, source_target_pairs={{0,56},{8,0},{16,8},{24,16},{32,24},{40,32},{48,40},{56,48},{1,57}... | collective-permute-start | bytes 393224 | tf_op jit(solution)/shard_map/ppermute | solution.py:22
  33.1 6.4 %collective-permute-start.10 = (f32[16,2048]{1,0:T(8,128)S(1)}, f32[16,2048]{1,0:T(8,128)S(1)}, u32[]{:S(2)}, u32[]{:S(2)}) collective-permute-start(f32[16,2048]{1,0:T(8,128)S(1)} %collective-permute-done.8.refs_7_), channel_id=1, source_target_pairs={{0,8},{8,16},{16,24},{24,32},{32,40},{40,48},{48,56},{56,0},{1,9},... | collective-permute-start | bytes 393224 | tf_op jit(solution)/shard_map/ppermute | solution.py:22
  39.5 5.6 %collective-permute-start.12 = (f32[16,1024]{1,0:T(8,128)S(1)}, f32[16,1024]{1,0:T(8,128)S(1)}, u32[]{:S(2)}, u32[]{:S(2)}) collective-permute-start(f32[16,1024]{1,0:T(8,128)S(1)} %slice.36), channel_id=1, source_target_pairs={{0,8},{8,16},{16,24},{24,32},{32,40},{40,48},{48,56},{56,0},{1,9},... | collective-permute-start | bytes 196616 | tf_op jit(solution)/shard_map/ppermute | solution.py:22
  49.4 6.1 %collective-permute-start.16 = (f32[4,1,32,128]{3,2,1,0:T(8,128)S(1)}, f32[4,1,32,128]{3,2,1,0:T(8,128)S(1)}, u32[]{:S(2)}, u32[]{:S(2)}) collective-permute-start(f32[4,1,32,128]{3,2,1,0:T(8,128)S(1)} %dynamic-slice_add_fusion), channel_id=1, source_target_pairs={{0,64},{64,128},{128,192},{192,0},{1,65},{65,129},{129,193},{193,1... | collective-permute-start | bytes 196616 | tf_op jit(solution)/shard_map/ppermute | solution.py:22
  49.9 6.3 %collective-permute-start.15 = (f32[4,1,32,128]{3,2,1,0:T(8,128)S(1)}, f32[4,1,32,128]{3,2,1,0:T(8,128)S(1)}, u32[]{:S(2)}, u32[]{:S(2)}) collective-permute-start(f32[4,1,32,128]{3,2,1,0:T(8,128)S(1)} %dynamic-slice_add_fusion), channel_id=1, source_target_pairs={{0,128},{64,192},{128,0},{192,64},{1,129},{65,193},{129,1},{193,65... | collective-permute-start | bytes 196616 | tf_op jit(solution)/shard_map/ppermute | solution.py:22
  56.2 5.6 %collective-permute-start.20 = (f32[4,1,32,128]{3,2,1,0:T(8,128)S(1)}, f32[4,1,32,128]{3,2,1,0:T(8,128)S(1)}, u32[]{:S(2)}, u32[]{:S(2)}) collective-permute-start(f32[4,1,32,128]{3,2,1,0:T(8,128)S(1)} %fusion.8), channel_id=1, source_target_pairs={{0,6},{2,0},{4,2},{6,4},{1,7},{3,1},{5,3},{7,5},{8,14},{10,8},{12,... | collective-permute-start | bytes 196616 | tf_op jit(solution)/shard_map/ppermute | solution.py:22
  58.3 5.8 %collective-permute-start.18 = (f32[4,1,32,128]{3,2,1,0:T(8,128)S(1)}, f32[4,1,32,128]{3,2,1,0:T(8,128)S(1)}, u32[]{:S(2)}, u32[]{:S(2)}) collective-permute-start(f32[4,1,32,128]{3,2,1,0:T(8,128)S(1)} %fusion.8), channel_id=1, source_target_pairs={{0,4},{2,6},{4,0},{6,2},{1,5},{3,7},{5,1},{7,3},{8,12},{10,14},{12... | collective-permute-start | bytes 196616 | tf_op jit(solution)/shard_map/ppermute | solution.py:22
  66.7 5.9 %collective-permute-start.22 = (f32[16,1152]{1,0:T(8,128)S(1)}, f32[16,1152]{1,0:T(8,128)S(1)}, u32[]{:S(2)}, u32[]{:S(2)}) collective-permute-start(f32[16,1152]{1,0:T(8,128)S(1)} %get-tuple-element.83), channel_id=1, source_target_pairs={{0,8},{8,16},{16,24},{24,32},{32,40},{40,48},{48,56},{56,0},{1,9},... | collective-permute-start | bytes 221192 | tf_op jit(solution)/shard_map/ppermute | solution.py:22
  72.6 6.6 %collective-permute-start.24 = (f32[16,2304]{1,0:T(8,128)S(1)}, f32[16,2304]{1,0:T(8,128)S(1)}, u32[]{:S(2)}, u32[]{:S(2)}) collective-permute-start(f32[16,2304]{1,0:T(8,128)S(1)} %get-tuple-element.89), channel_id=1, source_target_pairs={{0,8},{8,16},{16,24},{24,32},{32,40},{40,48},{48,56},{56,0},{1,9},... | collective-permute-start | bytes 442376 | tf_op jit(solution)/shard_map/ppermute | solution.py:22
  72.7 6.5 %collective-permute-start.25 = (f32[16,2304]{1,0:T(8,128)S(1)}, f32[16,2304]{1,0:T(8,128)S(1)}, u32[]{:S(2)}, u32[]{:S(2)}) collective-permute-start(f32[16,2304]{1,0:T(8,128)S(1)} %get-tuple-element.90), channel_id=1, source_target_pairs={{0,56},{8,0},{16,8},{24,16},{32,24},{40,32},{48,40},{56,48},{1,57}... | collective-permute-start | bytes 442376 | tf_op jit(solution)/shard_map/ppermute | solution.py:22
  79.3 5.8 %collective-permute-start.27 = (f32[16,2304]{1,0:T(8,128)S(1)}, f32[16,2304]{1,0:T(8,128)S(1)}, u32[]{:S(2)}, u32[]{:S(2)}) collective-permute-start(f32[16,2304]{1,0:T(8,128)S(1)} %add.73), channel_id=1, source_target_pairs={{0,56},{8,0},{16,8},{24,16},{32,24},{40,32},{48,40},{56,48},{1,57}... | collective-permute-start | bytes 442376 | tf_op jit(solution)/shard_map/ppermute | solution.py:22
  82.4 6.4 %collective-permute-start.26 = (f32[16,2304]{1,0:T(8,128)S(1)}, f32[16,2304]{1,0:T(8,128)S(1)}, u32[]{:S(2)}, u32[]{:S(2)}) collective-permute-start(f32[16,2304]{1,0:T(8,128)S(1)} %add.72), channel_id=1, source_target_pairs={{0,8},{8,16},{16,24},{24,32},{32,40},{40,48},{48,56},{56,0},{1,9},... | collective-permute-start | bytes 442376 | tf_op jit(solution)/shard_map/ppermute | solution.py:22
  89.0 6.6 %collective-permute-start.28 = (f32[16,2304]{1,0:T(8,128)S(1)}, f32[16,2304]{1,0:T(8,128)S(1)}, u32[]{:S(2)}, u32[]{:S(2)}) collective-permute-start(f32[16,2304]{1,0:T(8,128)S(1)} %add.74), channel_id=1, source_target_pairs={{0,8},{8,16},{16,24},{24,32},{32,40},{40,48},{48,56},{56,0},{1,9},... | collective-permute-start | bytes 442376 | tf_op jit(solution)/shard_map/ppermute | solution.py:22
  95.6 6.9 %collective-permute-start.31 = (f32[16,2304]{1,0:T(8,128)S(1)}, f32[16,2304]{1,0:T(8,128)S(1)}, u32[]{:S(2)}, u32[]{:S(2)}) collective-permute-start(f32[16,2304]{1,0:T(8,128)S(1)} %add_add_fusion.refs_4_), channel_id=1, source_target_pairs={{0,56},{8,0},{16,8},{24,16},{32,24},{40,32},{48,40},{56,48},{1,57}... | collective-permute-start | bytes 442376 | tf_op jit(solution)/shard_map/ppermute | solution.py:22
  96.0 7.8 %collective-permute-start.30 = (f32[16,2304]{1,0:T(8,128)S(1)}, f32[16,2304]{1,0:T(8,128)S(1)}, u32[]{:S(2)}, u32[]{:S(2)}) collective-permute-start(f32[16,2304]{1,0:T(8,128)S(1)} %add_add_fusion.refs_4_), channel_id=1, source_target_pairs={{0,8},{8,16},{16,24},{24,32},{32,40},{40,48},{48,56},{56,0},{1,9},... | collective-permute-start | bytes 442376 | tf_op jit(solution)/shard_map/ppermute | solution.py:22
  103.8 5.7 %collective-permute-start.33 = (f32[16,2304]{1,0:T(8,128)S(1)}, f32[16,2304]{1,0:T(8,128)S(1)}, u32[]{:S(2)}, u32[]{:S(2)}) collective-permute-start(f32[16,2304]{1,0:T(8,128)S(1)} %collective-permute-done.31.refs_5_), channel_id=1, source_target_pairs={{0,56},{8,0},{16,8},{24,16},{32,24},{40,32},{48,40},{56,48},{1,57}... | collective-permute-start | bytes 442376 | tf_op jit(solution)/shard_map/ppermute | solution.py:22
  103.8 6.9 %collective-permute-start.32 = (f32[16,2304]{1,0:T(8,128)S(1)}, f32[16,2304]{1,0:T(8,128)S(1)}, u32[]{:S(2)}, u32[]{:S(2)}) collective-permute-start(f32[16,2304]{1,0:T(8,128)S(1)} %collective-permute-done.30.refs_12_), channel_id=1, source_target_pairs={{0,8},{8,16},{16,24},{24,32},{32,40},{40,48},{48,56},{56,0},{1,9},... | collective-permute-start | bytes 442376 | tf_op jit(solution)/shard_map/ppermute | solution.py:22
  111.0 6.4 %collective-permute-start.34 = (f32[16,2304]{1,0:T(8,128)S(1)}, f32[16,2304]{1,0:T(8,128)S(1)}, u32[]{:S(2)}, u32[]{:S(2)}) collective-permute-start(f32[16,2304]{1,0:T(8,128)S(1)} %collective-permute-done.32.refs_11_), channel_id=1, source_target_pairs={{0,8},{8,16},{16,24},{24,32},{32,40},{40,48},{48,56},{56,0},{1,9},... | collective-permute-start | bytes 442376 | tf_op jit(solution)/shard_map/ppermute | solution.py:22
  117.3 5.6 %collective-permute-start.36 = (f32[16,1152]{1,0:T(8,128)S(1)}, f32[16,1152]{1,0:T(8,128)S(1)}, u32[]{:S(2)}, u32[]{:S(2)}) collective-permute-start(f32[16,1152]{1,0:T(8,128)S(1)} %slice.44), channel_id=1, source_target_pairs={{0,8},{8,16},{16,24},{24,32},{32,40},{40,48},{48,56},{56,0},{1,9},... | collective-permute-start | bytes 221192 | tf_op jit(solution)/shard_map/ppermute | solution.py:22
  131.7 17.8 %collective-permute-start.38 = (f32[64,2176]{1,0:T(8,128)S(1)}, f32[64,2176]{1,0:T(8,128)S(1)}, u32[]{:S(2)}, u32[]{:S(2)}) collective-permute-start(f32[64,2176]{1,0:T(8,128)S(1)} %get-tuple-element.110), channel_id=1, source_target_pairs={{0,192},{64,0},{128,64},{192,128},{1,193},{65,1},{129,65},{193,129... | collective-permute-start | bytes 1671176 | tf_op jit(solution)/shard_map/ppermute | solution.py:22
  133.8 15.6 %collective-permute-start.39 = (f32[64,2176]{1,0:T(8,128)S(1)}, f32[64,2176]{1,0:T(8,128)S(1)}, u32[]{:S(2)}, u32[]{:S(2)}) collective-permute-start(f32[64,2176]{1,0:T(8,128)S(1)} %get-tuple-element.111), channel_id=1, source_target_pairs={{0,128},{64,192},{128,0},{192,64},{1,129},{65,193},{129,1},{193,65... | collective-permute-start | bytes 1671176 | tf_op jit(solution)/shard_map/ppermute | solution.py:22
  134.3 18.9 %collective-permute-start.40 = (f32[64,2176]{1,0:T(8,128)S(1)}, f32[64,2176]{1,0:T(8,128)S(1)}, u32[]{:S(2)}, u32[]{:S(2)}) collective-permute-start(f32[64,2176]{1,0:T(8,128)S(1)} %get-tuple-element.112), channel_id=1, source_target_pairs={{0,64},{64,128},{128,192},{192,0},{1,65},{65,129},{129,193},{193,1... | collective-permute-start | bytes 1671176 | tf_op jit(solution)/shard_map/ppermute | solution.py:22
  140.7 5.4 %collective-permute-start.43 = (f32[64,128]{1,0:T(8,128)S(1)}, f32[64,128]{1,0:T(8,128)S(1)}, u32[]{:S(2)}, u32[]{:S(2)}) collective-permute-start(f32[64,128]{1,0:T(8,128)S(1)} %add.79), channel_id=1, source_target_pairs={{0,4},{2,6},{4,0},{6,2},{1,5},{3,7},{5,1},{7,3},{8,12},{10,14},{12... | collective-permute-start | bytes 98312 | tf_op jit(solution)/shard_map/ppermute | solution.py:22
  (13 other events, 106.4 us)

commit v2 on v1

--- a/solution.py
+++ b/solution.py
@@ -9,7 +9,6 @@
 from jax.sharding import Mesh
 from jax.sharding import PartitionSpec as P
 
-HIGH = lax.Precision.HIGH
 HIGHEST = lax.Precision.HIGHEST
 XS, ZS, YS, CS = 4, 8, 4, 2
 SIZES = {"x": XS, "z": ZS, "y": YS, "c": CS}
@@ -66,14 +65,13 @@
 
 def ring_gather(own):
     out = [own] + [None] * (ZS - 1)
-    half = own.shape[1] // 2
     up = down = own
     for s in range(1, ZS // 2):
         up = moved(up, "z", 1)
         down = moved(down, "z", -1)
         up, down = lax.optimization_barrier((up, down))
         out[-s % ZS], out[s] = up, down
-    out[ZS // 2 :] = [moved(up[:, :half], "z", 1), moved(down[:, half:], "z", -1)] + out[ZS // 2 + 1 :]
+    out[ZS // 2] = moved(up, "z", 1)
     return out
 
 
@@ -85,23 +83,37 @@
     down_out[:, half:] = after_ref[:, half:] + down_ref[...]
 
 
-def ring_scatter(parts):
+def paired(v, axis, bit):
+    return lax.ppermute(v, axis, [(i, i ^ bit) for i in range(SIZES[axis])])
+
+
+def across(v):
+    return lax.ppermute(v, "z", [(i, (i - 1 if i % 2 == 0 else i + 1) % ZS) for i in range(ZS)])
+
+
+def ring_scatter(parts, gram):
     far = ZS // 2
     first, second = parts[far], parts[far + 1]
     parts = parts[: far + 1] + parts[far + 2 :]
-    up, down = lax.optimization_barrier((moved(first, "z", 1), moved(second, "z", -1)))
+    up, down = moved(first, "z", 1), moved(second, "z", -1)
+    up, down, got = lax.optimization_barrier((up, down, paired(gram, "z", 1)))
+    sums = [gram + got]
     ends = [up, down, parts[far - 1], parts[far + 1]]
     up, down = call(merged_kernel, [parts[0].shape] * 2, ends, 4)
     for s in range(far - 2, -1, -1):
-        up, down = lax.optimization_barrier((moved(up, "z", 1), moved(down, "z", -1)))
+        got = across(sums[-1]) if len(sums) % 2 else paired(sums[-1], "z", 1)
+        up, down = moved(up, "z", 1), moved(down, "z", -1)
         if s:
+            up, down, got = lax.optimization_barrier((up, down, got))
             up, down = up + parts[s], down + parts[-s % ZS]
-    return parts[0] + (up + down)
+        sums.append(got)
+    own, one, other, opposite = sums
+    return parts[0] + (up + down), (own + opposite) + (one + other)
 
 
 def summed_col(v):
     v = v + moved(v, "c", 1)
-    v = v + lax.ppermute(v, "y", [(i, i ^ 1) for i in range(YS)])
+    v = v + paired(v, "y", 1)
     return v + moved(v, "y", 2)
 
 
@@ -113,17 +125,23 @@
     return (home == to).astype(jnp.float32)
 
 
-def stacked_kernel(*refs):
-    *ins, out = refs
-    deep, far = ins[0].shape[0], ZS // 2
-    half, wide = ins[far].shape[1], ins[0].shape[1]
+def projected_kernel(*refs):
+    k_refs, ins, (out, b_ref) = refs[:XS], refs[XS:-2], refs[-2:]
+    deep, wide = ins[0].shape
     for j in range(ZS):
-        rows = pl.ds(j * deep, deep)
-        if j == far:
-            out[rows, :half] = ins[far][...]
-            out[rows, half:wide] = ins[far + 1][...]
-        else:
-            out[rows, :wide] = ins[j + (j > far)][...]
+        b_ref[pl.ds(j * deep, deep), :] = ins[j][...]
+    out[...] = jnp.zeros(out.shape, jnp.float32)
+    step = 512
+
+    def tile(t, _):
+        at = pl.ds(pl.multiple_of(t * step, step), step)
+        top, rest = halves(jnp.concatenate([k[:, at] for k in k_refs], 0))
+        b_top, b_rest = halves(b_ref[:, at])
+        dims = ((1,), (1,))
+        out[...] += dot(top, b_top, dims, None) + (dot(top, b_rest, dims, None) + dot(rest, b_top, dims, None))
+        return 0
+
+    lax.fori_loop(0, wide // step, tile, 0)
 
 
 def pack_kernel(b_hbm, r_hbm, *refs):
@@ -205,25 +223,13 @@
 
 
 def parts_kernel(own, proj_ref, r_ref, *refs):
-    k_refs, proj_out, part_refs = refs[:XS], refs[XS], refs[XS + 1 :]
+    k_refs, (proj_out, gram_out), part_refs = refs[:XS], refs[XS : XS + 2], refs[XS + 2 :]
     comp = proj_ref.shape[1]
     group, far = own * XS, ZS // 2
     rows, wide = k_refs[0].shape
     half = part_refs[far].shape[1]
     x, z = lax.axis_index("x"), lax.axis_index("z")
 
-    def put(at, value):
-        end = at + value.shape[1]
-        for j in range(ZS):
-            v = value[j * group : (j + 1) * group]
-            if j != far:
-                part_refs[j + (j > far)][:, at:end] = v
-            else:
-                if at < half:
-                    part_refs[far][:, at : min(end, half)] = v[:, : min(end, half) - at]
-                if end > half:
-                    part_refs[far + 1][:, max(at, half) - half : end - half] = v[:, max(at, half) - at :]
-
     proj = proj_ref[...]
     proj_abs = dot(proj, places(comp, own, z), ((1,), (0,)))
     proj_out[...] = proj_abs
@@ -235,31 +241,42 @@
         return [v[j * rows : (j + 1) * rows] for j in range(XS)]
 
     right = jnp.concatenate([by_x(split(proj_abs)), r_ref[...]], 1)
-    put(wide, dot(by_x(split(proj)), right, ((0,), (0,))))
+    sums = dot(by_x(split(proj)), right, ((0,), (0,)))
+    for j in range(ZS):
+        tail = sums[j * group : (j + 1) * group, comp:]
+        if j == far:
+            part_refs[far + 1][:, wide - half :] = tail
+        else:
+            part_refs[j + (j > far)][:, wide:] = tail
+    gram_out[...] = dot(places(comp, own, z), sums[:, :comp], ((0,), (0,)))
     top, rest = halves(proj)
     step = 512
-    for at in range(0, wide, step):
-        k_top, k_rest = halves(jnp.concatenate([k[:, at : at + step] for k in k_refs], 0))
-        dims = ((0,), (0,))
-        put(at, dot(top, k_top, dims, None) + (dot(top, k_rest, dims, None) + dot(rest, k_top, dims, None)))
-
-
-def inverse_factor(w_ref, v_ref, comp):
+
+    def tiles(t, _):
+        near = pl.ds(pl.multiple_of(t * step, step), step)
+        for side in range(2):
+            at = pl.ds(pl.multiple_of(side * half + t * step, step), step)
+            k_top, k_rest = halves(jnp.concatenate([k[:, at] for k in k_refs], 0))
+            dims = ((0,), (0,))
+            value = dot(top, k_top, dims, None) + (dot(top, k_rest, dims, None) + dot(rest, k_top, dims, None))
+            for j in range(ZS):
+                v = value[j * group : (j + 1) * group]
+                if j == far:
+                    part_refs[far + side][:, near] = v
+                else:
+                    part_refs[j + (j > far)][:, at] = v
+        return 0
+
+    lax.fori_loop(0, half // step, tiles, 0)
+
+
+def inverse_factor(w_ref, v_ref, comp, first, last):
     row = lax.broadcasted_iota(jnp.int32, (PANEL, comp), 0)
-    whole = lax.broadcasted_iota(jnp.int32, (comp, comp), 0)
-    v_ref[...] = jnp.where(whole == lax.broadcasted_iota(jnp.int32, (comp, comp), 1), 1.0, 0.0)
-
-    def panel(p, last):
-        last_w, last_v = last
+
+    def panel(p, _):
         rows = pl.ds(pl.multiple_of(p * PANEL, PANEL), PANEL)
-        shift = (comp - p * PANEL) % comp
-        both = jnp.concatenate([last_w, last_v], 1)
-        near = dot(pltpu.roll(last_w, shift, 1)[:, :PANEL], both, ((0,), (0,)))
-        w, v = w_ref[rows, :] - near[:, :comp], v_ref[rows, :] - near[:, comp:]
-        change = dot(last_w, both, ((0,), (0,)))
-        w_ref[...] = w_ref[...] - change[:, :comp]
-        v_ref[...] = v_ref[...] - jnp.where(whole >= (p + 1) * PANEL, change[:, comp:], 0.0)
-        turned = pltpu.roll(w, shift, 1)
+        w, v = w_ref[rows, :], v_ref[rows, :]
+        turned = pltpu.roll(w, (comp - p * PANEL) % comp, 1)
         cols = [jnp.broadcast_to(turned[:, i : i + 1], (PANEL, comp)) for i in range(PANEL)]
         for i in range(PANEL):
             scale = lax.rsqrt(jnp.broadcast_to(cols[i][i : i + 1, :], (PANEL, comp)))
@@ -272,46 +289,53 @@
             w, v = step(w), step(v)
             cols = [step(c) if k > i else c for k, c in enumerate(cols)]
         v_ref[rows, :] = v
-        return w, v
-
-    zero = jnp.zeros((PANEL, comp), jnp.float32)
-    lax.fori_loop(0, comp // PANEL, panel, (zero, zero))
+        below = lax.broadcasted_iota(jnp.int32, (comp, comp), 0) >= (p + 1) * PANEL
+        change = dot(w, jnp.concatenate([w, v], 1), ((0,), (0,)))
+        w_ref[...] = w_ref[...] - change[:, :comp]
+        v_ref[...] = v_ref[...] - jnp.where(below, change[:, comp:], 0.0)
+        return 0
+
+    lax.fori_loop(first, last, panel, 0)
+
+
+def upper_kernel(row_count, gram_ref, w_ref, v_ref):
+    comp = gram_ref.shape[0]
+    w_ref[...] = gram_ref[...] * (1.0 / row_count)
+    at = [lax.broadcasted_iota(jnp.int32, (comp, comp), d) for d in (0, 1)]
+    v_ref[...] = jnp.where(at[0] == at[1], 1.0, 0.0)
+    inverse_factor(w_ref, v_ref, comp, 0, comp // PANEL // 2)
+
+
+def lower_kernel(w_in, v_in, v_ref, w_ref):
+    comp = w_in.shape[0]
+    w_ref[...], v_ref[...] = w_in[...], v_in[...]
+    inverse_factor(w_ref, v_ref, comp, comp // PANEL // 2, comp // PANEL)
 
 
 def finish_kernel(own, row_count, *refs):
-    k_refs, g_refs = refs[:XS], refs[XS : XS + ZS + 1]
-    proj_ref, resp_ref = refs[XS + ZS + 1 : XS + ZS + 3]
-    scores_ref, weights_ref, next_ref, *d_refs = refs[XS + ZS + 3 : -4]
-    w_ref, v_ref, small_ref, raw_ref = refs[-4:]
+    k_refs, g_refs = refs[:XS], refs[XS : XS + ZS]
+    proj_ref, resp_ref, inv_ref = refs[XS + ZS : XS + ZS + 3]
+    scores_ref, weights_ref, next_ref, *d_refs = refs[XS + ZS + 3 : -2]
+    small_ref, raw_ref = refs[-2:]
     comp = proj_ref.shape[1]
     group = own * XS
     rows, wide = k_refs[0].shape
     resp = resp_ref.shape[1]
     root_rows = math.sqrt(row_count)
     x, z = lax.axis_index("x"), lax.axis_index("z")
-    far = ZS // 2
-    half = (g_refs[far].shape[1])
     for j in range(ZS):
         at = pl.ds(j * group, group)
-        if j == far:
-            raw_ref[at, :half] = g_refs[far][...]
-            raw_ref[at, half:] = g_refs[far + 1][:, : wide - half]
-            small_ref[at, :] = g_refs[far + 1][:, wide - half :]
-        else:
-            ref = g_refs[j if j < far else j + 1]
-            raw_ref[at, :] = ref[:, :wide]
-            small_ref[at, :] = ref[:, wide:]
+        raw_ref[at, :] = g_refs[j][:, :wide]
+        small_ref[at, :] = g_refs[j][:, wide:]
 
     place = places(comp, own, z)
     small = dot(place, small_ref[...], ((0,), (0,)))
-    w_ref[...] = small[:, :comp] * (1.0 / row_count)
-    inverse_factor(w_ref, v_ref, comp)
-    inv = v_ref[...]
+    inv = inv_ref[...]
     inv_place = dot(inv, place, ((1,), (1,)))
     scores_all = dot(proj_ref[...], inv, ((1,), (1,)))
     scores_ref[...] = scores_all[:rows]
     back = dot(scores_all, inv_place, ((1,), (0,))) * (1.0 / row_count)
-    weights = dot(small[:, comp : comp + resp], inv, ((0,), (1,))) * (1.0 / root_rows)
+    weights = dot(small[:, :resp], inv, ((0,), (1,))) * (1.0 / root_rows)
     weights_ref[...] = weights
     next_ref[...] = dot(resp_ref[...], weights, ((1,), (0,)))
 
@@ -393,10 +417,15 @@
     first, *k_blocks = lax.optimization_barrier((first, *k_blocks))
     k_blocks = exchanged(k_blocks)
     b_parts = ring_gather(first)
-    (b_all,) = call(stacked_kernel, [(comp, wide)], b_parts, 8)
-    k_all = jnp.concatenate(k_blocks, 0)
-
-    proj = dot(k_all, b_all, ((1,), (1,)), HIGH).reshape(XS, CS, rows // CS, comp)
+    (proj,) = call(
+        projected_kernel,
+        [(XS * rows, comp)],
+        [*k_blocks, *b_parts],
+        16,
+        scratch=[pltpu.VMEM((comp, wide), jnp.float32)],
+    )
+
+    proj = proj.reshape(XS, CS, rows // CS, comp)
     mine = lax.dynamic_slice_in_dim(proj, c, 1, 1)
     other = lax.dynamic_slice_in_dim(proj, 1 - c, 1, 1)
     proj = mine + moved(other, "c", 1)
@@ -408,21 +437,26 @@
     proj = jnp.concatenate([jnp.where(c == 0, proj, other), jnp.where(c == 0, other, proj)], 1)
     proj = proj.reshape(XS * rows, comp)
 
-    full = wide + 2 * comp
+    full = wide + comp
+    half = full // 256 * 128
     shapes = [(group, full)] * (ZS + 1)
-    shapes[ZS // 2 : ZS // 2 + 2] = [(group, full // 2)] * 2
-    proj_abs, *parts = call(
-        functools.partial(parts_kernel, own), [(XS * rows, comp)] + shapes, [proj, r_all, *k_blocks], 24
-    )
-    total = ring_gather(ring_scatter(parts))
+    shapes[ZS // 2 : ZS // 2 + 2] = [(group, half), (group, full - half)]
+    proj_abs, gram, *parts = call(
+        functools.partial(parts_kernel, own), [(XS * rows, comp), (comp, comp)] + shapes, [proj, r_all, *k_blocks], 24
+    )
+    mine, gram = ring_scatter(parts, gram)
+    square = (comp, comp)
+    state = call(functools.partial(upper_kernel, row_count), [square] * 2, [gram], 4)
+    (inv,) = call(lower_kernel, [square], state, 4, scratch=[pltpu.VMEM(square, jnp.float32)])
+    total = ring_gather(mine)
     scores, weights, nxt, *d_blocks = call(
         functools.partial(finish_kernel, own, row_count),
         [(rows, comp), (resp, comp), (rows, comp)] + [(rows, wide + comp)] * XS,
-        [*k_blocks, *total, proj_abs, responses],
+        [*k_blocks, *total, proj_abs, responses, inv],
         24,
         None,
         None,
-        [pltpu.VMEM(s, jnp.float32) for s in ((comp, comp), (comp, comp), (comp, full - wide), (comp, wide))],
+        [pltpu.VMEM((comp, full - wide), jnp.float32), pltpu.VMEM((comp, wide), jnp.float32)],
     )
     d_blocks = exchanged(d_blocks)
     basis_next = summed_col(nxt) / math.sqrt(resp_count)

time: 157 us -> 151 us (0.962)
  starting transfers between devices: 63 us -> 57.1 us
  Pallas kernels: 15.3 us -> 17.6 us
    ppermute x43 -> x41, waiting for transfers between devices: 72 us -> 61.5 us  [moved(): return lax.ppermute(a, axis, [(i, (i + step) % n) for i in range(n)])]
    ppermute x1 -> x5, waiting for transfers between devices: 2.07 us -> 11.4 us  [the longest x3 6.31 us: paired(): return lax.ppermute(v, axis, [(i, i ^ bit) for i in range(SIZES[axis])])]
    ppermute x43 -> x41, starting transfers between devices: 61.1 us -> 52.5 us  [moved(): return lax.ppermute(a, axis, [(i, (i + step) % n) for i in range(n)])]
    ppermute x1 -> x5, starting transfers between devices: 1.85 us -> 4.59 us  [the longest x2 2.62 us: across(): lax.ppermute(v, 'z', [(i, (i - 1 if i % 2 == 0 else i + 1) % ZS) for i in...]
    pallas_call x8 -> x10, Pallas kernels: 15.3 us -> 17.6 us  [call(): pl.pallas_call(body, out_shape=[jax.ShapeDtypeStruct(s, jnp.float32) for...]
  transfers between devices with their start and end apart: 44 -> 46, of which waited for: 33 -> 31; matrix products, arithmetic and copies ran while one was open for 0% -> 0% of each run, Pallas kernels for 1% -> 5%
where the time goes in v2:
time: 151 us; the launch traced here: 150 us
  waiting for transfers between devices  72.9 us (48%)
  starting transfers between devices  57.1 us (38%)
  Pallas kernels  17.6 us (12%)
    ppermute x41, waiting for transfers between devices, moved(): return lax.ppermute(a, axis, [(i, (i + step) % n) for i in range(n)])  61.5 us
    ppermute x41, starting transfers between devices, moved(): return lax.ppermute(a, axis, [(i, (i + step) % n) for i in range(n)])  52.5 us
    pallas_call x10, Pallas kernels, call(): pl.pallas_call(body, out_shape=[jax.ShapeDtypeStruct(s, jnp.float32) for...  17.6 us
    ppermute x3, waiting for transfers between devices, paired(): return lax.ppermute(v, axis, [(i, i ^ bit) for i in range(SIZES[axis])])  6.31 us
    ppermute x2, waiting for transfers between devices, across(): lax.ppermute(v, 'z', [(i, (i - 1 if i % 2 == 0 else i + 1) % ZS) for i in...  5.09 us
  transfers between devices with their start and end apart: 46, of which 31 were waited for; matrix products, arithmetic and copies ran while one was open for 0% of the time, Pallas kernels for 5%

profile of v2, /device:TPU:8, one launch (start us, length us, event | category | flops | bytes accessed | tf_op | source)
XLA Modules:
  0.0 149.5 jit_solution(18316517899585313129)
XLA Ops:
  1.7 2.8 %collective-permute-start = (f32[8,1536]{1,0:T(8,128)S(1)}, f32[8,1536]{1,0:T(8,128)S(1)}, u32[]{:S(2)}, u32[]{:S(2)}) collective-permute-start(f32[8,1536]{1,0:T(8,128)S(1)} %get-tuple-element.66), channel_id=1, source_target_pairs={{0,192},{64,0},{128,64},{192,128},{1,193},{65,1},{129,65},{193,129... | collective-permute-start | bytes 147464 | tf_op jit(solution)/shard_map/ppermute | solution.py:21
  6.2 2.2 %shard_map.76 = (f32[64,2048]{1,0:T(8,128)S(1)}, f32[64,2048]{1,0:T(8,128)}, f32[64,2048]{1,0:T(8,128)}, f32[64,2048]{1,0:T(8,128)}) custom-call(f32[64,8192]{1,0:T(8,128)} %k_ref.1), custom_call_target="tpu_custom_call" | custom-call | tf_op jit(solution)/shard_map/pallas_call | solution.py:56
  10.7 5.9 %collective-permute-start.7 = (f32[16,2048]{1,0:T(8,128)S(1)}, f32[16,2048]{1,0:T(8,128)S(1)}, u32[]{:S(2)}, u32[]{:S(2)}) collective-permute-start(f32[16,2048]{1,0:T(8,128)S(1)} %get-tuple-element.78.refs_4_), channel_id=1, source_target_pairs={{0,56},{8,0},{16,8},{24,16},{32,24},{40,32},{48,40},{56,48},{1,57}... | collective-permute-start | bytes 393224 | tf_op jit(solution)/shard_map/ppermute | solution.py:21
  19.6 3.3 %collective-permute-done.6.refs_11_ = f32[16,2048]{1,0:T(8,128)S(1)} collective-permute-done((f32[16,2048]{1,0:T(8,128)S(1)}, f32[16,2048]{1,0:T(8,128)S(1)}, u32[]{:S(2)}, u32[]{:S(2)}) %collective-permute-start.6) | collective-permute-done | bytes 131104 | tf_op jit(solution)/shard_map/ppermute | solution.py:21
  22.9 2.0 %collective-permute-start.8 = (f32[16,2048]{1,0:T(8,128)S(1)}, f32[16,2048]{1,0:T(8,128)S(1)}, u32[]{:S(2)}, u32[]{:S(2)}) collective-permute-start(f32[16,2048]{1,0:T(8,128)S(1)} %collective-permute-done.6.refs_11_), channel_id=1, source_target_pairs={{0,8},{8,16},{16,24},{24,32},{32,40},{40,48},{48,56},{56,0},{1,9},... | collective-permute-start | bytes 393224 | tf_op jit(solution)/shard_map/ppermute | solution.py:21
  24.9 3.0 %collective-permute-done.9.refs_6_ = f32[16,2048]{1,0:T(8,128)S(1)} collective-permute-done((f32[16,2048]{1,0:T(8,128)S(1)}, f32[16,2048]{1,0:T(8,128)S(1)}, u32[]{:S(2)}, u32[]{:S(2)}) %collective-permute-start.9) | collective-permute-done | bytes 131104 | tf_op jit(solution)/shard_map/ppermute | solution.py:21
  31.1 2.9 %collective-permute-done.11.refs_7_ = f32[16,2048]{1,0:T(8,128)S(1)} collective-permute-done((f32[16,2048]{1,0:T(8,128)S(1)}, f32[16,2048]{1,0:T(8,128)S(1)}, u32[]{:S(2)}, u32[]{:S(2)}) %collective-permute-start.11) | collective-permute-done | bytes 131104 | tf_op jit(solution)/shard_map/ppermute | solution.py:21
  34.1 2.8 %collective-permute-done.10.refs_9_ = f32[16,2048]{1,0:T(8,128)S(1)} collective-permute-done((f32[16,2048]{1,0:T(8,128)S(1)}, f32[16,2048]{1,0:T(8,128)S(1)}, u32[]{:S(2)}, u32[]{:S(2)}) %collective-permute-start.10) | collective-permute-done | bytes 131104 | tf_op jit(solution)/shard_map/ppermute | solution.py:21
  36.9 6.2 %collective-permute-done.12.refs_8_ = f32[16,2048]{1,0:T(8,128)S(1)} collective-permute-done((f32[16,2048]{1,0:T(8,128)S(1)}, f32[16,2048]{1,0:T(8,128)S(1)}, u32[]{:S(2)}, u32[]{:S(2)}) %collective-permute-start.12) | collective-permute-done | bytes 131104 | tf_op jit(solution)/shard_map/ppermute | solution.py:21
  48.2 3.3 %collective-permute-start.14 = (f32[4,1,32,128]{3,2,1,0:T(8,128)S(1)}, f32[4,1,32,128]{3,2,1,0:T(8,128)S(1)}, u32[]{:S(2)}, u32[]{:S(2)}) collective-permute-start(f32[4,1,32,128]{3,2,1,0:T(8,128)S(1)} %dynamic-slice_add_fusion), channel_id=1, source_target_pairs={{0,128},{64,192},{128,0},{192,64},{1,129},{65,193},{129,1},{193,65... | collective-permute-start | bytes 196616 | tf_op jit(solution)/shard_map/ppermute | solution.py:21
  52.6 2.2 %collective-permute-done.14 = f32[4,1,32,128]{3,2,1,0:T(8,128)S(1)} collective-permute-done((f32[4,1,32,128]{3,2,1,0:T(8,128)S(1)}, f32[4,1,32,128]{3,2,1,0:T(8,128)S(1)}, u32[]{:S(2)}, u32[]{:S(2)}) %collective-permute-start.14) | collective-permute-done | bytes 65568 | tf_op jit(solution)/shard_map/ppermute | solution.py:21
  56.9 3.5 %collective-permute-start.17 = (f32[4,1,32,128]{3,2,1,0:T(8,128)S(1)}, f32[4,1,32,128]{3,2,1,0:T(8,128)S(1)}, u32[]{:S(2)}, u32[]{:S(2)}) collective-permute-start(f32[4,1,32,128]{3,2,1,0:T(8,128)S(1)} %fusion), channel_id=1, source_target_pairs={{0,4},{2,6},{4,0},{6,2},{1,5},{3,7},{5,1},{7,3},{8,12},{10,14},{12... | collective-permute-start | bytes 196616 | tf_op jit(solution)/shard_map/ppermute | solution.py:21
  60.7 2.0 %collective-permute-done.17 = f32[4,1,32,128]{3,2,1,0:T(8,128)S(1)} collective-permute-done((f32[4,1,32,128]{3,2,1,0:T(8,128)S(1)}, f32[4,1,32,128]{3,2,1,0:T(8,128)S(1)}, u32[]{:S(2)}, u32[]{:S(2)}) %collective-permute-start.17) | collective-permute-done | bytes 65568 | tf_op jit(solution)/shard_map/ppermute | solution.py:21
  68.0 4.6 %collective-permute-done.21.up_ref = f32[16,1024]{1,0:T(8,128)S(1)} collective-permute-done((f32[16,1024]{1,0:T(8,128)S(1)}, f32[16,1024]{1,0:T(8,128)S(1)}, u32[]{:S(2)}, u32[]{:S(2)}) %collective-permute-start.21) | collective-permute-done | bytes 65568 | tf_op jit(solution)/shard_map/ppermute | solution.py:21
  73.4 2.6 %collective-permute-start.25 = (f32[16,2176]{1,0:T(8,128)S(1)}, f32[16,2176]{1,0:T(8,128)S(1)}, u32[]{:S(2)}, u32[]{:S(2)}) collective-permute-start(f32[16,2176]{1,0:T(8,128)S(1)} %get-tuple-element.95), channel_id=1, source_target_pairs={{0,56},{8,0},{16,8},{24,16},{32,24},{40,32},{48,40},{56,48},{1,57}... | collective-permute-start | bytes 417800 | tf_op jit(solution)/shard_map/ppermute | solution.py:21
  76.9 4.7 %collective-permute-done.26 = f32[128,128]{1,0:T(8,128)S(1)} collective-permute-done((f32[128,128]{1,0:T(8,128)S(1)}, f32[128,128]{1,0:T(8,128)S(1)}, u32[]{:S(2)}, u32[]{:S(2)}) %collective-permute-start.26) | collective-permute-done | bytes 65568 | tf_op jit(solution)/shard_map/ppermute | solution.py:91
  83.9 4.2 %collective-permute-done.29 = f32[128,128]{1,0:T(8,128)S(1)} collective-permute-done((f32[128,128]{1,0:T(8,128)S(1)}, f32[128,128]{1,0:T(8,128)S(1)}, u32[]{:S(2)}, u32[]{:S(2)}) %collective-permute-start.29) | collective-permute-done | bytes 65568 | tf_op jit(solution)/shard_map/ppermute | solution.py:87
  89.4 2.0 %collective-permute-start.31 = (f32[16,2176]{1,0:T(8,128)S(1)}, f32[16,2176]{1,0:T(8,128)S(1)}, u32[]{:S(2)}, u32[]{:S(2)}) collective-permute-start(f32[16,2176]{1,0:T(8,128)S(1)} %add.88), channel_id=1, source_target_pairs={{0,56},{8,0},{16,8},{24,16},{32,24},{40,32},{48,40},{56,48},{1,57}... | collective-permute-start | bytes 417800 | tf_op jit(solution)/shard_map/ppermute | solution.py:21
  91.6 3.4 %collective-permute-done.31 = f32[16,2176]{1,0:T(8,128)S(1)} collective-permute-done((f32[16,2176]{1,0:T(8,128)S(1)}, f32[16,2176]{1,0:T(8,128)S(1)}, u32[]{:S(2)}, u32[]{:S(2)}) %collective-permute-start.31) | collective-permute-done | bytes 139296 | tf_op jit(solution)/shard_map/ppermute | solution.py:21
  95.0 3.5 %collective-permute-done.30 = f32[16,2176]{1,0:T(8,128)S(1)} collective-permute-done((f32[16,2176]{1,0:T(8,128)S(1)}, f32[16,2176]{1,0:T(8,128)S(1)}, u32[]{:S(2)}, u32[]{:S(2)}) %collective-permute-start.30) | collective-permute-done | bytes 139296 | tf_op jit(solution)/shard_map/ppermute | solution.py:21
  100.9 3.0 %collective-permute-done.33.refs_5_ = f32[16,2176]{1,0:T(8,128)S(1)} collective-permute-done((f32[16,2176]{1,0:T(8,128)S(1)}, f32[16,2176]{1,0:T(8,128)S(1)}, u32[]{:S(2)}, u32[]{:S(2)}) %collective-permute-start.33) | collective-permute-done | bytes 139296 | tf_op jit(solution)/shard_map/ppermute | solution.py:21
  105.3 2.0 %collective-permute-start.34 = (f32[16,2176]{1,0:T(8,128)S(1)}, f32[16,2176]{1,0:T(8,128)S(1)}, u32[]{:S(2)}, u32[]{:S(2)}) collective-permute-start(f32[16,2176]{1,0:T(8,128)S(1)} %collective-permute-done.32.refs_11_), channel_id=1, source_target_pairs={{0,8},{8,16},{16,24},{24,32},{32,40},{40,48},{48,56},{56,0},{1,9},... | collective-permute-start | bytes 417800 | tf_op jit(solution)/shard_map/ppermute | solution.py:21
  107.3 3.0 %collective-permute-done.35.refs_6_ = f32[16,2176]{1,0:T(8,128)S(1)} collective-permute-done((f32[16,2176]{1,0:T(8,128)S(1)}, f32[16,2176]{1,0:T(8,128)S(1)}, u32[]{:S(2)}, u32[]{:S(2)}) %collective-permute-start.35) | collective-permute-done | bytes 139296 | tf_op jit(solution)/shard_map/ppermute | solution.py:21
  119.1 2.8 %shard_map.80 = (f32[128,128]{1,0:T(8,128)S(1)}, f32[128,128]{1,0:T(8,128)S(1)}) custom-call(f32[128,128]{1,0:T(8,128)S(1)} %add_add_fusion.1.gram_ref), custom_call_target="tpu_custom_call" | custom-call | tf_op jit(solution)/shard_map/pallas_call | solution.py:56
  121.9 2.8 %shard_map.81.refs_14_ = f32[128,128]{1,0:T(8,128)S(1)} custom-call(f32[128,128]{1,0:T(8,128)S(1)} %get-tuple-element.114.w_in, f32[128,128]{1,0:T(8,128)S(1)} %get-tuple-element.115.v_in), custom_call_target="tpu_custom_call" | custom-call | tf_op jit(solution)/shard_map/pallas_call | solution.py:56
  124.6 3.3 %shard_map.82 = (f32[64,128]{1,0:T(8,128)}, f32[64,128]{1,0:T(8,128)}, f32[64,128]{1,0:T(8,128)S(1)}, f32[64,2176]{1,0:T(8,128)S(1)}, f32[64,2176]{1,0:T(8,128)S...) custom-call(f32[64,2048]{1,0:T(8,128)S(1)} %get-tuple-element.74.refs_0_, ...), custom_call_target="tpu_custom_call" | custom-call | tf_op jit(solution)/shard_map/pallas_call | solution.py:56
  133.1 1.8 %collective-permute-start.44 = (f32[64,128]{1,0:T(8,128)S(1)}, f32[64,128]{1,0:T(8,128)S(1)}, u32[]{:S(2)}, u32[]{:S(2)}) collective-permute-start(f32[64,128]{1,0:T(8,128)S(1)} %add.94), channel_id=1, source_target_pairs={{0,2},{2,0},{4,6},{6,4},{1,3},{3,1},{5,7},{7,5},{8,10},{10,8},{12,... | collective-permute-start | bytes 98312 | tf_op jit(solution)/shard_map/ppermute | solution.py:87
  134.9 2.1 %collective-permute-done.44 = f32[64,128]{1,0:T(8,128)S(1)} collective-permute-done((f32[64,128]{1,0:T(8,128)S(1)}, f32[64,128]{1,0:T(8,128)S(1)}, u32[]{:S(2)}, u32[]{:S(2)}) %collective-permute-start.44) | collective-permute-done | bytes 32800 | tf_op jit(solution)/shard_map/ppermute | solution.py:87
  137.0 3.5 %collective-permute-start.45 = (f32[64,128]{1,0:T(8,128)S(1)}, f32[64,128]{1,0:T(8,128)S(1)}, u32[]{:S(2)}, u32[]{:S(2)}) collective-permute-start(f32[64,128]{1,0:T(8,128)S(1)} %add.95), channel_id=1, source_target_pairs={{0,4},{2,6},{4,0},{6,2},{1,5},{3,7},{5,1},{7,3},{8,12},{10,14},{12... | collective-permute-start | bytes 98312 | tf_op jit(solution)/shard_map/ppermute | solution.py:21
  140.5 1.9 %collective-permute-done.45 = f32[64,128]{1,0:T(8,128)S(1)} collective-permute-done((f32[64,128]{1,0:T(8,128)S(1)}, f32[64,128]{1,0:T(8,128)S(1)}, u32[]{:S(2)}, u32[]{:S(2)}) %collective-permute-start.45) | collective-permute-done | bytes 32800 | tf_op jit(solution)/shard_map/ppermute | solution.py:21
  143.0 4.3 %collective-permute-done.42.refs_3_ = f32[64,2176]{1,0:T(8,128)S(1)} collective-permute-done((f32[64,2176]{1,0:T(8,128)S(1)}, f32[64,2176]{1,0:T(8,128)S(1)}, u32[]{:S(2)}, u32[]{:S(2)}) %collective-permute-start.42) | collective-permute-done | bytes 557088 | tf_op jit(solution)/shard_map/ppermute | solution.py:21
  147.3 2.0 %shard_map.83 = (f32[64,8192]{1,0:T(8,128)}, f32[4,8192]{1,0:T(4,128)}) custom-call(f32[64,2176]{1,0:T(8,128)S(1)} %get-tuple-element.117.refs_0_, f32[64,2176]{1,0:T(8,128)S(1)} %collective-permute-done.40.refs_1_, f32[64,2176]{1,0:T(8,128)S(1)} %collective-permute-done.41.refs_2_, f32[64,2176]{1,0:T(8,128)S(1)} %collective-permute-done.42.refs_3_), custom_call_target="tpu_custom_call" | custom-call | tf_op jit(solution)/shard_map/pallas_call | solution.py:56
  (93 shorter events, 48.7 us)
Async XLA Ops:
  1.7 6.8 %collective-permute-start = (f32[8,1536]{1,0:T(8,128)S(1)}, f32[8,1536]{1,0:T(8,128)S(1)}, u32[]{:S(2)}, u32[]{:S(2)}) collective-permute-start(f32[8,1536]{1,0:T(8,128)S(1)} %get-tuple-element.66), channel_id=1, source_target_pairs={{0,192},{64,0},{128,64},{192,128},{1,193},{65,1},{129,65},{193,129... | collective-permute-start | bytes 147464 | tf_op jit(solution)/shard_map/ppermute | solution.py:21
  4.5 5.6 %collective-permute-start.1 = (f32[8,1536]{1,0:T(8,128)S(1)}, f32[8,1536]{1,0:T(8,128)S(1)}, u32[]{:S(2)}, u32[]{:S(2)}) collective-permute-start(f32[8,1536]{1,0:T(8,128)S(1)} %get-tuple-element.67), channel_id=1, source_target_pairs={{0,128},{64,192},{128,0},{192,64},{1,129},{65,193},{129,1},{193,65... | collective-permute-start | bytes 147464 | tf_op jit(solution)/shard_map/ppermute | solution.py:21
  10.7 8.9 %collective-permute-start.7 = (f32[16,2048]{1,0:T(8,128)S(1)}, f32[16,2048]{1,0:T(8,128)S(1)}, u32[]{:S(2)}, u32[]{:S(2)}) collective-permute-start(f32[16,2048]{1,0:T(8,128)S(1)} %get-tuple-element.78.refs_4_), channel_id=1, source_target_pairs={{0,56},{8,0},{16,8},{24,16},{32,24},{40,32},{48,40},{56,48},{1,57}... | collective-permute-start | bytes 393224 | tf_op jit(solution)/shard_map/ppermute | solution.py:21
  16.7 6.2 %collective-permute-start.6 = (f32[16,2048]{1,0:T(8,128)S(1)}, f32[16,2048]{1,0:T(8,128)S(1)}, u32[]{:S(2)}, u32[]{:S(2)}) collective-permute-start(f32[16,2048]{1,0:T(8,128)S(1)} %get-tuple-element.78.refs_4_), channel_id=1, source_target_pairs={{0,8},{8,16},{16,24},{24,32},{32,40},{40,48},{48,56},{56,0},{1,9},... | collective-permute-start | bytes 393224 | tf_op jit(solution)/shard_map/ppermute | solution.py:21
  16.7 26.4 %collective-permute-start.3 = (f32[64,2048]{1,0:T(8,128)}, f32[64,2048]{1,0:T(8,128)S(1)}, u32[]{:S(2)}, u32[]{:S(2)}) collective-permute-start(f32[64,2048]{1,0:T(8,128)} %get-tuple-element.75), channel_id=1, source_target_pairs={{0,192},{64,0},{128,64},{192,128},{1,193},{65,1},{129,65},{193,129... | collective-permute-start | bytes 1572872 | tf_op jit(solution)/shard_map/ppermute | solution.py:21
  17.2 25.9 %collective-permute-start.4 = (f32[64,2048]{1,0:T(8,128)}, f32[64,2048]{1,0:T(8,128)S(1)}, u32[]{:S(2)}, u32[]{:S(2)}) collective-permute-start(f32[64,2048]{1,0:T(8,128)} %get-tuple-element.76), channel_id=1, source_target_pairs={{0,128},{64,192},{128,0},{192,64},{1,129},{65,193},{129,1},{193,65... | collective-permute-start | bytes 1572872 | tf_op jit(solution)/shard_map/ppermute | solution.py:21
  18.4 24.7 %collective-permute-start.5 = (f32[64,2048]{1,0:T(8,128)}, f32[64,2048]{1,0:T(8,128)S(1)}, u32[]{:S(2)}, u32[]{:S(2)}) collective-permute-start(f32[64,2048]{1,0:T(8,128)} %get-tuple-element.77), channel_id=1, source_target_pairs={{0,64},{64,128},{128,192},{192,0},{1,65},{65,129},{129,193},{193,1... | collective-permute-start | bytes 1572872 | tf_op jit(solution)/shard_map/ppermute | solution.py:21
  22.9 6.2 %collective-permute-start.8 = (f32[16,2048]{1,0:T(8,128)S(1)}, f32[16,2048]{1,0:T(8,128)S(1)}, u32[]{:S(2)}, u32[]{:S(2)}) collective-permute-start(f32[16,2048]{1,0:T(8,128)S(1)} %collective-permute-done.6.refs_11_), channel_id=1, source_target_pairs={{0,8},{8,16},{16,24},{24,32},{32,40},{40,48},{48,56},{56,0},{1,9},... | collective-permute-start | bytes 393224 | tf_op jit(solution)/shard_map/ppermute | solution.py:21
  29.5 7.5 %collective-permute-start.10 = (f32[16,2048]{1,0:T(8,128)S(1)}, f32[16,2048]{1,0:T(8,128)S(1)}, u32[]{:S(2)}, u32[]{:S(2)}) collective-permute-start(f32[16,2048]{1,0:T(8,128)S(1)} %collective-permute-done.8.refs_10_), channel_id=1, source_target_pairs={{0,8},{8,16},{16,24},{24,32},{32,40},{40,48},{48,56},{56,0},{1,9},... | collective-permute-start | bytes 393224 | tf_op jit(solution)/shard_map/ppermute | solution.py:21
  36.9 6.2 %collective-permute-start.12 = (f32[16,2048]{1,0:T(8,128)S(1)}, f32[16,2048]{1,0:T(8,128)S(1)}, u32[]{:S(2)}, u32[]{:S(2)}) collective-permute-start(f32[16,2048]{1,0:T(8,128)S(1)} %collective-permute-done.10.refs_9_), channel_id=1, source_target_pairs={{0,8},{8,16},{16,24},{24,32},{32,40},{40,48},{48,56},{56,0},{1,9},... | collective-permute-start | bytes 393224 | tf_op jit(solution)/shard_map/ppermute | solution.py:21
  46.1 5.4 %collective-permute-start.16 = (f32[4,1,32,128]{3,2,1,0:T(8,128)S(1)}, f32[4,1,32,128]{3,2,1,0:T(8,128)S(1)}, u32[]{:S(2)}, u32[]{:S(2)}) collective-permute-start(f32[4,1,32,128]{3,2,1,0:T(8,128)S(1)} %dynamic-slice_add_fusion), channel_id=1, source_target_pairs={{0,192},{64,0},{128,64},{192,128},{1,193},{65,1},{129,65},{193,129... | collective-permute-start | bytes 196616 | tf_op jit(solution)/shard_map/ppermute | solution.py:21
  47.1 5.5 %collective-permute-start.15 = (f32[4,1,32,128]{3,2,1,0:T(8,128)S(1)}, f32[4,1,32,128]{3,2,1,0:T(8,128)S(1)}, u32[]{:S(2)}, u32[]{:S(2)}) collective-permute-start(f32[4,1,32,128]{3,2,1,0:T(8,128)S(1)} %dynamic-slice_add_fusion), channel_id=1, source_target_pairs={{0,64},{64,128},{128,192},{192,0},{1,65},{65,129},{129,193},{193,1... | collective-permute-start | bytes 196616 | tf_op jit(solution)/shard_map/ppermute | solution.py:21
  48.2 6.6 %collective-permute-start.14 = (f32[4,1,32,128]{3,2,1,0:T(8,128)S(1)}, f32[4,1,32,128]{3,2,1,0:T(8,128)S(1)}, u32[]{:S(2)}, u32[]{:S(2)}) collective-permute-start(f32[4,1,32,128]{3,2,1,0:T(8,128)S(1)} %dynamic-slice_add_fusion), channel_id=1, source_target_pairs={{0,128},{64,192},{128,0},{192,64},{1,129},{65,193},{129,1},{193,65... | collective-permute-start | bytes 196616 | tf_op jit(solution)/shard_map/ppermute | solution.py:21
  54.8 5.6 %collective-permute-start.19 = (f32[4,1,32,128]{3,2,1,0:T(8,128)S(1)}, f32[4,1,32,128]{3,2,1,0:T(8,128)S(1)}, u32[]{:S(2)}, u32[]{:S(2)}) collective-permute-start(f32[4,1,32,128]{3,2,1,0:T(8,128)S(1)} %fusion), channel_id=1, source_target_pairs={{0,6},{2,0},{4,2},{6,4},{1,7},{3,1},{5,3},{7,5},{8,14},{10,8},{12,... | collective-permute-start | bytes 196616 | tf_op jit(solution)/shard_map/ppermute | solution.py:21
  56.9 5.8 %collective-permute-start.17 = (f32[4,1,32,128]{3,2,1,0:T(8,128)S(1)}, f32[4,1,32,128]{3,2,1,0:T(8,128)S(1)}, u32[]{:S(2)}, u32[]{:S(2)}) collective-permute-start(f32[4,1,32,128]{3,2,1,0:T(8,128)S(1)} %fusion), channel_id=1, source_target_pairs={{0,4},{2,6},{4,0},{6,2},{1,5},{3,7},{5,1},{7,3},{8,12},{10,14},{12... | collective-permute-start | bytes 196616 | tf_op jit(solution)/shard_map/ppermute | solution.py:21
  65.9 6.8 %collective-permute-start.22 = (f32[16,1152]{1,0:T(8,128)S(1)}, f32[16,1152]{1,0:T(8,128)S(1)}, u32[]{:S(2)}, u32[]{:S(2)}) collective-permute-start(f32[16,1152]{1,0:T(8,128)S(1)} %get-tuple-element.88), channel_id=1, source_target_pairs={{0,56},{8,0},{16,8},{24,16},{32,24},{40,32},{48,40},{56,48},{1,57}... | collective-permute-start | bytes 221192 | tf_op jit(solution)/shard_map/ppermute | solution.py:21
  67.2 5.5 %collective-permute-start.21 = (f32[16,1024]{1,0:T(8,128)S(1)}, f32[16,1024]{1,0:T(8,128)S(1)}, u32[]{:S(2)}, u32[]{:S(2)}) collective-permute-start(f32[16,1024]{1,0:T(8,128)S(1)} %get-tuple-element.87), channel_id=1, source_target_pairs={{0,8},{8,16},{16,24},{24,32},{32,40},{40,48},{48,56},{56,0},{1,9},... | collective-permute-start | bytes 196616 | tf_op jit(solution)/shard_map/ppermute | solution.py:21
  72.7 8.9 %collective-permute-start.24 = (f32[16,2176]{1,0:T(8,128)S(1)}, f32[16,2176]{1,0:T(8,128)S(1)}, u32[]{:S(2)}, u32[]{:S(2)}) collective-permute-start(f32[16,2176]{1,0:T(8,128)S(1)} %get-tuple-element.94), channel_id=1, source_target_pairs={{0,8},{8,16},{16,24},{24,32},{32,40},{40,48},{48,56},{56,0},{1,9},... | collective-permute-start | bytes 417800 | tf_op jit(solution)/shard_map/ppermute | solution.py:21
  73.4 8.2 %collective-permute-start.25 = (f32[16,2176]{1,0:T(8,128)S(1)}, f32[16,2176]{1,0:T(8,128)S(1)}, u32[]{:S(2)}, u32[]{:S(2)}) collective-permute-start(f32[16,2176]{1,0:T(8,128)S(1)} %get-tuple-element.95), channel_id=1, source_target_pairs={{0,56},{8,0},{16,8},{24,16},{32,24},{40,32},{48,40},{56,48},{1,57}... | collective-permute-start | bytes 417800 | tf_op jit(solution)/shard_map/ppermute | solution.py:21
  76.0 5.6 %collective-permute-start.26 = (f32[128,128]{1,0:T(8,128)S(1)}, f32[128,128]{1,0:T(8,128)S(1)}, u32[]{:S(2)}, u32[]{:S(2)}) collective-permute-start(f32[128,128]{1,0:T(8,128)S(1)} %add.84), channel_id=1, source_target_pairs={{0,56},{8,16},{16,8},{24,32},{32,24},{40,48},{48,40},{56,0},{1,57}... | collective-permute-start | bytes 196616 | tf_op jit(solution)/shard_map/ppermute | solution.py:91
  81.6 6.5 %collective-permute-start.28 = (f32[16,2176]{1,0:T(8,128)S(1)}, f32[16,2176]{1,0:T(8,128)S(1)}, u32[]{:S(2)}, u32[]{:S(2)}) collective-permute-start(f32[16,2176]{1,0:T(8,128)S(1)} %add.86), channel_id=1, source_target_pairs={{0,56},{8,0},{16,8},{24,16},{32,24},{40,32},{48,40},{56,48},{1,57}... | collective-permute-start | bytes 417800 | tf_op jit(solution)/shard_map/ppermute | solution.py:21
  83.1 6.3 %collective-permute-start.27 = (f32[16,2176]{1,0:T(8,128)S(1)}, f32[16,2176]{1,0:T(8,128)S(1)}, u32[]{:S(2)}, u32[]{:S(2)}) collective-permute-start(f32[16,2176]{1,0:T(8,128)S(1)} %add.85), channel_id=1, source_target_pairs={{0,8},{8,16},{16,24},{24,32},{32,40},{40,48},{48,56},{56,0},{1,9},... | collective-permute-start | bytes 417800 | tf_op jit(solution)/shard_map/ppermute | solution.py:21
  89.4 5.6 %collective-permute-start.31 = (f32[16,2176]{1,0:T(8,128)S(1)}, f32[16,2176]{1,0:T(8,128)S(1)}, u32[]{:S(2)}, u32[]{:S(2)}) collective-permute-start(f32[16,2176]{1,0:T(8,128)S(1)} %add.88), channel_id=1, source_target_pairs={{0,56},{8,0},{16,8},{24,16},{32,24},{40,32},{48,40},{56,48},{1,57}... | collective-permute-start | bytes 417800 | tf_op jit(solution)/shard_map/ppermute | solution.py:21
  91.5 7.0 %collective-permute-start.30 = (f32[16,2176]{1,0:T(8,128)S(1)}, f32[16,2176]{1,0:T(8,128)S(1)}, u32[]{:S(2)}, u32[]{:S(2)}) collective-permute-start(f32[16,2176]{1,0:T(8,128)S(1)} %add.87), channel_id=1, source_target_pairs={{0,8},{8,16},{16,24},{24,32},{32,40},{40,48},{48,56},{56,0},{1,9},... | collective-permute-start | bytes 417800 | tf_op jit(solution)/shard_map/ppermute | solution.py:21
  99.0 6.3 %collective-permute-start.32 = (f32[16,2176]{1,0:T(8,128)S(1)}, f32[16,2176]{1,0:T(8,128)S(1)}, u32[]{:S(2)}, u32[]{:S(2)}) collective-permute-start(f32[16,2176]{1,0:T(8,128)S(1)} %add_add_fusion.refs_4_), channel_id=1, source_target_pairs={{0,8},{8,16},{16,24},{24,32},{32,40},{40,48},{48,56},{56,0},{1,9},... | collective-permute-start | bytes 417800 | tf_op jit(solution)/shard_map/ppermute | solution.py:21
  105.3 6.3 %collective-permute-start.34 = (f32[16,2176]{1,0:T(8,128)S(1)}, f32[16,2176]{1,0:T(8,128)S(1)}, u32[]{:S(2)}, u32[]{:S(2)}) collective-permute-start(f32[16,2176]{1,0:T(8,128)S(1)} %collective-permute-done.32.refs_11_), channel_id=1, source_target_pairs={{0,8},{8,16},{16,24},{24,32},{32,40},{40,48},{48,56},{56,0},{1,9},... | collective-permute-start | bytes 417800 | tf_op jit(solution)/shard_map/ppermute | solution.py:21
  112.1 6.3 %collective-permute-start.36 = (f32[16,2176]{1,0:T(8,128)S(1)}, f32[16,2176]{1,0:T(8,128)S(1)}, u32[]{:S(2)}, u32[]{:S(2)}) collective-permute-start(f32[16,2176]{1,0:T(8,128)S(1)} %collective-permute-done.34.refs_10_), channel_id=1, source_target_pairs={{0,8},{8,16},{16,24},{24,32},{32,40},{40,48},{48,56},{56,0},{1,9},... | collective-permute-start | bytes 417800 | tf_op jit(solution)/shard_map/ppermute | solution.py:21
  113.6 5.5 %collective-permute-start.39 = (f32[128,128]{1,0:T(8,128)S(1)}, f32[128,128]{1,0:T(8,128)S(1)}, u32[]{:S(2)}, u32[]{:S(2)}) collective-permute-start(f32[128,128]{1,0:T(8,128)S(1)} %collective-permute-done.29), channel_id=1, source_target_pairs={{0,56},{8,16},{16,8},{24,32},{32,24},{40,48},{48,40},{56,0},{1,57}... | collective-permute-start | bytes 196616 | tf_op jit(solution)/shard_map/ppermute | solution.py:91
  118.3 6.3 %collective-permute-start.38 = (f32[16,2176]{1,0:T(8,128)S(1)}, f32[16,2176]{1,0:T(8,128)S(1)}, u32[]{:S(2)}, u32[]{:S(2)}) collective-permute-start(f32[16,2176]{1,0:T(8,128)S(1)} %collective-permute-done.36.refs_9_), channel_id=1, source_target_pairs={{0,8},{8,16},{16,24},{24,32},{32,40},{40,48},{48,56},{56,0},{1,9},... | collective-permute-start | bytes 417800 | tf_op jit(solution)/shard_map/ppermute | solution.py:21
  128.0 15.0 %collective-permute-start.40 = (f32[64,2176]{1,0:T(8,128)S(1)}, f32[64,2176]{1,0:T(8,128)S(1)}, u32[]{:S(2)}, u32[]{:S(2)}) collective-permute-start(f32[64,2176]{1,0:T(8,128)S(1)} %get-tuple-element.118), channel_id=1, source_target_pairs={{0,192},{64,0},{128,64},{192,128},{1,193},{65,1},{129,65},{193,129... | collective-permute-start | bytes 1671176 | tf_op jit(solution)/shard_map/ppermute | solution.py:21
  129.8 13.2 %collective-permute-start.41 = (f32[64,2176]{1,0:T(8,128)S(1)}, f32[64,2176]{1,0:T(8,128)S(1)}, u32[]{:S(2)}, u32[]{:S(2)}) collective-permute-start(f32[64,2176]{1,0:T(8,128)S(1)} %get-tuple-element.119), channel_id=1, source_target_pairs={{0,128},{64,192},{128,0},{192,64},{1,129},{65,193},{129,1},{193,65... | collective-permute-start | bytes 1671176 | tf_op jit(solution)/shard_map/ppermute | solution.py:21
  130.4 16.9 %collective-permute-start.42 = (f32[64,2176]{1,0:T(8,128)S(1)}, f32[64,2176]{1,0:T(8,128)S(1)}, u32[]{:S(2)}, u32[]{:S(2)}) collective-permute-start(f32[64,2176]{1,0:T(8,128)S(1)} %get-tuple-element.120), channel_id=1, source_target_pairs={{0,64},{64,128},{128,192},{192,0},{1,65},{65,129},{129,193},{193,1... | collective-permute-start | bytes 1671176 | tf_op jit(solution)/shard_map/ppermute | solution.py:21
  (15 other events, 117.1 us)

commit v3 on v2

--- a/solution.py
+++ b/solution.py
@@ -306,23 +306,38 @@
     inverse_factor(w_ref, v_ref, comp, 0, comp // PANEL // 2)
 
 
-def lower_kernel(w_in, v_in, v_ref, w_ref):
+def lower_kernel(own, rows, row_count, w_in, v_in, proj_ref, v_ref, scores_ref, left_ref, w_ref):
     comp = w_in.shape[0]
+    x, z = lax.axis_index("x"), lax.axis_index("z")
     w_ref[...], v_ref[...] = w_in[...], v_in[...]
     inverse_factor(w_ref, v_ref, comp, comp // PANEL // 2, comp // PANEL)
+    inv = v_ref[...]
+    inv_place = dot(inv, places(comp, own, z), ((1,), (1,)))
+    scores_all = dot(proj_ref[...], inv, ((1,), (1,)))
+    scores_ref[...] = scores_all[:rows]
+    back = dot(scores_all, inv_place, ((1,), (0,))) * (1.0 / row_count)
+    at = lax.broadcasted_iota(jnp.int32, (XS * SUB, comp), 0)
+    to = lax.broadcasted_iota(jnp.int32, (XS * SUB, comp), 1)
+    wanted = (((x + at // SUB) % XS) * ZS + z) * own + at % own
+    pick = jnp.where(wanted == to, 1.0, 0.0)
+    picks = dot(pick, inv_place, ((1,), (0,))) * (1.0 / math.sqrt(row_count))
+    for j in range(XS):
+        base = j * (rows + SUB)
+        left_ref[base : base + rows, :] = back[j * rows : (j + 1) * rows]
+        left_ref[base + rows : base + rows + SUB, :] = picks[j * SUB : (j + 1) * SUB]
 
 
 def finish_kernel(own, row_count, *refs):
     k_refs, g_refs = refs[:XS], refs[XS : XS + ZS]
-    proj_ref, resp_ref, inv_ref = refs[XS + ZS : XS + ZS + 3]
-    scores_ref, weights_ref, next_ref, *d_refs = refs[XS + ZS + 3 : -2]
+    resp_ref, inv_ref, left_ref = refs[XS + ZS : XS + ZS + 3]
+    weights_ref, next_ref, *d_refs = refs[XS + ZS + 3 : -2]
     small_ref, raw_ref = refs[-2:]
-    comp = proj_ref.shape[1]
+    comp = inv_ref.shape[1]
     group = own * XS
     rows, wide = k_refs[0].shape
     resp = resp_ref.shape[1]
     root_rows = math.sqrt(row_count)
-    x, z = lax.axis_index("x"), lax.axis_index("z")
+    z = lax.axis_index("z")
     for j in range(ZS):
         at = pl.ds(j * group, group)
         raw_ref[at, :] = g_refs[j][:, :wide]
@@ -331,24 +346,11 @@
     place = places(comp, own, z)
     small = dot(place, small_ref[...], ((0,), (0,)))
     inv = inv_ref[...]
-    inv_place = dot(inv, place, ((1,), (1,)))
-    scores_all = dot(proj_ref[...], inv, ((1,), (1,)))
-    scores_ref[...] = scores_all[:rows]
-    back = dot(scores_all, inv_place, ((1,), (0,))) * (1.0 / row_count)
     weights = dot(small[:, :resp], inv, ((0,), (1,))) * (1.0 / root_rows)
     weights_ref[...] = weights
     next_ref[...] = dot(resp_ref[...], weights, ((1,), (0,)))
 
-    at = lax.broadcasted_iota(jnp.int32, (XS * SUB, comp), 0)
-    to = lax.broadcasted_iota(jnp.int32, (XS * SUB, comp), 1)
-    wanted = (((x + at // SUB) % XS) * ZS + z) * own + at % own
-    pick = jnp.where(wanted == to, 1.0, 0.0)
-    picks = dot(pick, inv_place, ((1,), (0,))) * (1.0 / root_rows)
-    left = []
-    for j in range(XS):
-        left += [back[j * rows : (j + 1) * rows], picks[j * SUB : (j + 1) * SUB]]
-    left = jnp.concatenate(left, 0)
-    left_top, left_rest = halves(left)
+    left_top, left_rest = halves(left_ref[...])
     step = 512
     upper = lax.broadcasted_iota(jnp.int32, (SUB, 128), 0) < own
 
@@ -442,17 +444,26 @@
     shapes = [(group, full)] * (ZS + 1)
     shapes[ZS // 2 : ZS // 2 + 2] = [(group, half), (group, full - half)]
     proj_abs, gram, *parts = call(
-        functools.partial(parts_kernel, own), [(XS * rows, comp), (comp, comp)] + shapes, [proj, r_all, *k_blocks], 24
+        functools.partial(parts_kernel, own),
+        [(XS * rows, comp), (comp, comp)] + shapes,
+        [proj, r_all, *k_blocks],
+        24,
     )
     mine, gram = ring_scatter(parts, gram)
     square = (comp, comp)
     state = call(functools.partial(upper_kernel, row_count), [square] * 2, [gram], 4)
-    (inv,) = call(lower_kernel, [square], state, 4, scratch=[pltpu.VMEM(square, jnp.float32)])
+    inv, scores, left = call(
+        functools.partial(lower_kernel, own, rows, row_count),
+        [square, (rows, comp), (XS * (rows + SUB), comp)],
+        [*state, proj_abs],
+        8,
+        scratch=[pltpu.VMEM(square, jnp.float32)],
+    )
     total = ring_gather(mine)
-    scores, weights, nxt, *d_blocks = call(
+    weights, nxt, *d_blocks = call(
         functools.partial(finish_kernel, own, row_count),
-        [(rows, comp), (resp, comp), (rows, comp)] + [(rows, wide + comp)] * XS,
-        [*k_blocks, *total, proj_abs, responses, inv],
+        [(resp, comp), (rows, comp)] + [(rows, wide + comp)] * XS,
+        [*k_blocks, *total, responses, inv, left],
         24,
         None,
         None,
@@ -460,7 +471,9 @@
     )
     d_blocks = exchanged(d_blocks)
     basis_next = summed_col(nxt) / math.sqrt(resp_count)
-    deflated, loadings = call(joined_kernel, [(rows, cols), (own, cols)], d_blocks, 8, None, [hbm, vmem], dma)
+    deflated, loadings = call(
+        joined_kernel, [(rows, cols), (own, cols)], d_blocks, 8, None, [hbm, vmem], dma
+    )
     return (scores, loadings, weights, deflated, basis_next)
 
 

time: 151 us -> 152 us (level)
  transfers between devices with their start and end apart: 46 -> 46, of which waited for: 31 -> 32; matrix products, arithmetic and copies ran while one was open for 0% -> 0% of each run, Pallas kernels for 5% -> 6%
where the time goes in v3:
time: 152 us; the launch traced here: 150 us
  waiting for transfers between devices  72.9 us (48%)
  starting transfers between devices  57.1 us (38%)
  Pallas kernels  18.3 us (12%)
    ppermute x41, waiting for transfers between devices, moved(): return lax.ppermute(a, axis, [(i, (i + step) % n) for i in range(n)])  61.5 us
    ppermute x41, starting transfers between devices, moved(): return lax.ppermute(a, axis, [(i, (i + step) % n) for i in range(n)])  52.5 us
    pallas_call x10, Pallas kernels, call(): pl.pallas_call(body, out_shape=[jax.ShapeDtypeStruct(s, jnp.float32) for...  18.3 us
    ppermute x3, waiting for transfers between devices, paired(): return lax.ppermute(v, axis, [(i, i ^ bit) for i in range(SIZES[axis])])  6.31 us
    ppermute x2, waiting for transfers between devices, across(): lax.ppermute(v, 'z', [(i, (i - 1 if i % 2 == 0 else i + 1) % ZS) for i in...  5.09 us
  transfers between devices with their start and end apart: 46, of which 32 were waited for; matrix products, arithmetic and copies ran while one was open for 0% of the time, Pallas kernels for 6%

profile of v3, /device:TPU:8, one launch (start us, length us, event | category | flops | bytes accessed | tf_op | source)
XLA Modules:
  0.0 150.2 jit_solution(16209707383078420679)
XLA Ops:
  1.7 2.8 %collective-permute-start = (f32[8,1536]{1,0:T(8,128)S(1)}, f32[8,1536]{1,0:T(8,128)S(1)}, u32[]{:S(2)}, u32[]{:S(2)}) collective-permute-start(f32[8,1536]{1,0:T(8,128)S(1)} %get-tuple-element.68), channel_id=1, source_target_pairs={{0,192},{64,0},{128,64},{192,128},{1,193},{65,1},{129,65},{193,129... | collective-permute-start | bytes 147464 | tf_op jit(solution)/shard_map/ppermute | solution.py:21
  6.2 2.2 %shard_map.76 = (f32[64,2048]{1,0:T(8,128)S(1)}, f32[64,2048]{1,0:T(8,128)}, f32[64,2048]{1,0:T(8,128)}, f32[64,2048]{1,0:T(8,128)}) custom-call(f32[64,8192]{1,0:T(8,128)} %k_ref.1), custom_call_target="tpu_custom_call" | custom-call | tf_op jit(solution)/shard_map/pallas_call | solution.py:56
  10.7 5.9 %collective-permute-start.7 = (f32[16,2048]{1,0:T(8,128)S(1)}, f32[16,2048]{1,0:T(8,128)S(1)}, u32[]{:S(2)}, u32[]{:S(2)}) collective-permute-start(f32[16,2048]{1,0:T(8,128)S(1)} %get-tuple-element.80.refs_4_), channel_id=1, source_target_pairs={{0,56},{8,0},{16,8},{24,16},{32,24},{40,32},{48,40},{56,48},{1,57}... | collective-permute-start | bytes 393224 | tf_op jit(solution)/shard_map/ppermute | solution.py:21
  19.6 3.3 %collective-permute-done.6.refs_11_ = f32[16,2048]{1,0:T(8,128)S(1)} collective-permute-done((f32[16,2048]{1,0:T(8,128)S(1)}, f32[16,2048]{1,0:T(8,128)S(1)}, u32[]{:S(2)}, u32[]{:S(2)}) %collective-permute-start.6) | collective-permute-done | bytes 131104 | tf_op jit(solution)/shard_map/ppermute | solution.py:21
  22.9 2.0 %collective-permute-start.8 = (f32[16,2048]{1,0:T(8,128)S(1)}, f32[16,2048]{1,0:T(8,128)S(1)}, u32[]{:S(2)}, u32[]{:S(2)}) collective-permute-start(f32[16,2048]{1,0:T(8,128)S(1)} %collective-permute-done.6.refs_11_), channel_id=1, source_target_pairs={{0,8},{8,16},{16,24},{24,32},{32,40},{40,48},{48,56},{56,0},{1,9},... | collective-permute-start | bytes 393224 | tf_op jit(solution)/shard_map/ppermute | solution.py:21
  24.9 3.0 %collective-permute-done.9.refs_6_ = f32[16,2048]{1,0:T(8,128)S(1)} collective-permute-done((f32[16,2048]{1,0:T(8,128)S(1)}, f32[16,2048]{1,0:T(8,128)S(1)}, u32[]{:S(2)}, u32[]{:S(2)}) %collective-permute-start.9) | collective-permute-done | bytes 131104 | tf_op jit(solution)/shard_map/ppermute | solution.py:21
  31.1 2.9 %collective-permute-done.11.refs_7_ = f32[16,2048]{1,0:T(8,128)S(1)} collective-permute-done((f32[16,2048]{1,0:T(8,128)S(1)}, f32[16,2048]{1,0:T(8,128)S(1)}, u32[]{:S(2)}, u32[]{:S(2)}) %collective-permute-start.11) | collective-permute-done | bytes 131104 | tf_op jit(solution)/shard_map/ppermute | solution.py:21
  34.1 2.8 %collective-permute-done.10.refs_9_ = f32[16,2048]{1,0:T(8,128)S(1)} collective-permute-done((f32[16,2048]{1,0:T(8,128)S(1)}, f32[16,2048]{1,0:T(8,128)S(1)}, u32[]{:S(2)}, u32[]{:S(2)}) %collective-permute-start.10) | collective-permute-done | bytes 131104 | tf_op jit(solution)/shard_map/ppermute | solution.py:21
  36.9 6.2 %collective-permute-done.12.refs_8_ = f32[16,2048]{1,0:T(8,128)S(1)} collective-permute-done((f32[16,2048]{1,0:T(8,128)S(1)}, f32[16,2048]{1,0:T(8,128)S(1)}, u32[]{:S(2)}, u32[]{:S(2)}) %collective-permute-start.12) | collective-permute-done | bytes 131104 | tf_op jit(solution)/shard_map/ppermute | solution.py:21
  48.2 3.3 %collective-permute-start.14 = (f32[4,1,32,128]{3,2,1,0:T(8,128)S(1)}, f32[4,1,32,128]{3,2,1,0:T(8,128)S(1)}, u32[]{:S(2)}, u32[]{:S(2)}) collective-permute-start(f32[4,1,32,128]{3,2,1,0:T(8,128)S(1)} %dynamic-slice_add_fusion), channel_id=1, source_target_pairs={{0,128},{64,192},{128,0},{192,64},{1,129},{65,193},{129,1},{193,65... | collective-permute-start | bytes 196616 | tf_op jit(solution)/shard_map/ppermute | solution.py:21
  52.6 2.2 %collective-permute-done.14 = f32[4,1,32,128]{3,2,1,0:T(8,128)S(1)} collective-permute-done((f32[4,1,32,128]{3,2,1,0:T(8,128)S(1)}, f32[4,1,32,128]{3,2,1,0:T(8,128)S(1)}, u32[]{:S(2)}, u32[]{:S(2)}) %collective-permute-start.14) | collective-permute-done | bytes 65568 | tf_op jit(solution)/shard_map/ppermute | solution.py:21
  56.9 3.5 %collective-permute-start.17 = (f32[4,1,32,128]{3,2,1,0:T(8,128)S(1)}, f32[4,1,32,128]{3,2,1,0:T(8,128)S(1)}, u32[]{:S(2)}, u32[]{:S(2)}) collective-permute-start(f32[4,1,32,128]{3,2,1,0:T(8,128)S(1)} %fusion), channel_id=1, source_target_pairs={{0,4},{2,6},{4,0},{6,2},{1,5},{3,7},{5,1},{7,3},{8,12},{10,14},{12... | collective-permute-start | bytes 196616 | tf_op jit(solution)/shard_map/ppermute | solution.py:21
  60.7 2.0 %collective-permute-done.17 = f32[4,1,32,128]{3,2,1,0:T(8,128)S(1)} collective-permute-done((f32[4,1,32,128]{3,2,1,0:T(8,128)S(1)}, f32[4,1,32,128]{3,2,1,0:T(8,128)S(1)}, u32[]{:S(2)}, u32[]{:S(2)}) %collective-permute-start.17) | collective-permute-done | bytes 65568 | tf_op jit(solution)/shard_map/ppermute | solution.py:21
  68.0 4.6 %collective-permute-done.21.up_ref = f32[16,1024]{1,0:T(8,128)S(1)} collective-permute-done((f32[16,1024]{1,0:T(8,128)S(1)}, f32[16,1024]{1,0:T(8,128)S(1)}, u32[]{:S(2)}, u32[]{:S(2)}) %collective-permute-start.21) | collective-permute-done | bytes 65568 | tf_op jit(solution)/shard_map/ppermute | solution.py:21
  73.4 2.6 %collective-permute-start.25 = (f32[16,2176]{1,0:T(8,128)S(1)}, f32[16,2176]{1,0:T(8,128)S(1)}, u32[]{:S(2)}, u32[]{:S(2)}) collective-permute-start(f32[16,2176]{1,0:T(8,128)S(1)} %get-tuple-element.97), channel_id=1, source_target_pairs={{0,56},{8,0},{16,8},{24,16},{32,24},{40,32},{48,40},{56,48},{1,57}... | collective-permute-start | bytes 417800 | tf_op jit(solution)/shard_map/ppermute | solution.py:21
  76.9 4.7 %collective-permute-done.26 = f32[128,128]{1,0:T(8,128)S(1)} collective-permute-done((f32[128,128]{1,0:T(8,128)S(1)}, f32[128,128]{1,0:T(8,128)S(1)}, u32[]{:S(2)}, u32[]{:S(2)}) %collective-permute-start.26) | collective-permute-done | bytes 65568 | tf_op jit(solution)/shard_map/ppermute | solution.py:91
  83.9 4.2 %collective-permute-done.29 = f32[128,128]{1,0:T(8,128)S(1)} collective-permute-done((f32[128,128]{1,0:T(8,128)S(1)}, f32[128,128]{1,0:T(8,128)S(1)}, u32[]{:S(2)}, u32[]{:S(2)}) %collective-permute-start.29) | collective-permute-done | bytes 65568 | tf_op jit(solution)/shard_map/ppermute | solution.py:87
  89.4 2.0 %collective-permute-start.32 = (f32[16,2176]{1,0:T(8,128)S(1)}, f32[16,2176]{1,0:T(8,128)S(1)}, u32[]{:S(2)}, u32[]{:S(2)}) collective-permute-start(f32[16,2176]{1,0:T(8,128)S(1)} %add.91), channel_id=1, source_target_pairs={{0,56},{8,0},{16,8},{24,16},{32,24},{40,32},{48,40},{56,48},{1,57}... | collective-permute-start | bytes 417800 | tf_op jit(solution)/shard_map/ppermute | solution.py:21
  91.6 3.4 %collective-permute-done.32 = f32[16,2176]{1,0:T(8,128)S(1)} collective-permute-done((f32[16,2176]{1,0:T(8,128)S(1)}, f32[16,2176]{1,0:T(8,128)S(1)}, u32[]{:S(2)}, u32[]{:S(2)}) %collective-permute-start.32) | collective-permute-done | bytes 139296 | tf_op jit(solution)/shard_map/ppermute | solution.py:21
  95.0 3.5 %collective-permute-done.31 = f32[16,2176]{1,0:T(8,128)S(1)} collective-permute-done((f32[16,2176]{1,0:T(8,128)S(1)}, f32[16,2176]{1,0:T(8,128)S(1)}, u32[]{:S(2)}, u32[]{:S(2)}) %collective-permute-start.31) | collective-permute-done | bytes 139296 | tf_op jit(solution)/shard_map/ppermute | solution.py:21
  100.8 3.0 %collective-permute-done.34.refs_5_ = f32[16,2176]{1,0:T(8,128)S(1)} collective-permute-done((f32[16,2176]{1,0:T(8,128)S(1)}, f32[16,2176]{1,0:T(8,128)S(1)}, u32[]{:S(2)}, u32[]{:S(2)}) %collective-permute-start.34) | collective-permute-done | bytes 139296 | tf_op jit(solution)/shard_map/ppermute | solution.py:21
  105.3 2.0 %collective-permute-start.35 = (f32[16,2176]{1,0:T(8,128)S(1)}, f32[16,2176]{1,0:T(8,128)S(1)}, u32[]{:S(2)}, u32[]{:S(2)}) collective-permute-start(f32[16,2176]{1,0:T(8,128)S(1)} %collective-permute-done.33.refs_11_), channel_id=1, source_target_pairs={{0,8},{8,16},{16,24},{24,32},{32,40},{40,48},{48,56},{56,0},{1,9},... | collective-permute-start | bytes 417800 | tf_op jit(solution)/shard_map/ppermute | solution.py:21
  107.3 3.0 %collective-permute-done.36.refs_6_ = f32[16,2176]{1,0:T(8,128)S(1)} collective-permute-done((f32[16,2176]{1,0:T(8,128)S(1)}, f32[16,2176]{1,0:T(8,128)S(1)}, u32[]{:S(2)}, u32[]{:S(2)}) %collective-permute-start.36) | collective-permute-done | bytes 139296 | tf_op jit(solution)/shard_map/ppermute | solution.py:21
  119.1 2.8 %shard_map.80 = (f32[128,128]{1,0:T(8,128)S(1)}, f32[128,128]{1,0:T(8,128)S(1)}) custom-call(f32[128,128]{1,0:T(8,128)S(1)} %add_add_fusion.1.gram_ref), custom_call_target="tpu_custom_call" | custom-call | tf_op jit(solution)/shard_map/pallas_call | solution.py:56
  121.9 3.8 %shard_map.81 = (f32[128,128]{1,0:T(8,128)S(1)}, f32[64,128]{1,0:T(8,128)}, f32[288,128]{1,0:T(8,128)S(1)}) custom-call(f32[128,128]{1,0:T(8,128)S(1)} %get-tuple-element.104.w_in, f32[128,128]{1,0:T(8,128)S(1)} %get-tuple-element.105.v_in, f32[256,128]{1,0:T(8,128)S(1)} %get-tuple-element.106.proj_ref), custom_call_target="tpu_custom_call" | custom-call | tf_op jit(solution)/shard_map/pallas_call | solution.py:56
  125.7 3.0 %shard_map.82 = (f32[64,128]{1,0:T(8,128)}, f32[64,128]{1,0:T(8,128)S(1)}, f32[64,2176]{1,0:T(8,128)S(1)}, f32[64,2176]{1,0:T(8,128)S(1)}, f32[64,2176]{1,0:T(8,128)S(1)}, /*index=5*/f32[64,2176]{1,0:T(8,128)S(1)}) custom-call(f32[64,2048]{1,0:T(8,128)S(1)} %get-tuple-element.76.refs_0_, f32[64,2048]{1,0:T(8,128)S(1)} %collective-permute-done.3.refs_1_, ...), custom_call_target="tpu_custom_call" | custom-call | tf_op jit(solution)/shard_map/pallas_call | solution.py:56
  133.7 1.8 %collective-permute-start.44 = (f32[64,128]{1,0:T(8,128)S(1)}, f32[64,128]{1,0:T(8,128)S(1)}, u32[]{:S(2)}, u32[]{:S(2)}) collective-permute-start(f32[64,128]{1,0:T(8,128)S(1)} %add.94), channel_id=1, source_target_pairs={{0,2},{2,0},{4,6},{6,4},{1,3},{3,1},{5,7},{7,5},{8,10},{10,8},{12,... | collective-permute-start | bytes 98312 | tf_op jit(solution)/shard_map/ppermute | solution.py:87
  135.6 2.1 %collective-permute-done.44 = f32[64,128]{1,0:T(8,128)S(1)} collective-permute-done((f32[64,128]{1,0:T(8,128)S(1)}, f32[64,128]{1,0:T(8,128)S(1)}, u32[]{:S(2)}, u32[]{:S(2)}) %collective-permute-start.44) | collective-permute-done | bytes 32800 | tf_op jit(solution)/shard_map/ppermute | solution.py:87
  137.6 3.5 %collective-permute-start.45 = (f32[64,128]{1,0:T(8,128)S(1)}, f32[64,128]{1,0:T(8,128)S(1)}, u32[]{:S(2)}, u32[]{:S(2)}) collective-permute-start(f32[64,128]{1,0:T(8,128)S(1)} %add.95), channel_id=1, source_target_pairs={{0,4},{2,6},{4,0},{6,2},{1,5},{3,7},{5,1},{7,3},{8,12},{10,14},{12... | collective-permute-start | bytes 98312 | tf_op jit(solution)/shard_map/ppermute | solution.py:21
  141.1 1.9 %collective-permute-done.45 = f32[64,128]{1,0:T(8,128)S(1)} collective-permute-done((f32[64,128]{1,0:T(8,128)S(1)}, f32[64,128]{1,0:T(8,128)S(1)}, u32[]{:S(2)}, u32[]{:S(2)}) %collective-permute-start.45) | collective-permute-done | bytes 32800 | tf_op jit(solution)/shard_map/ppermute | solution.py:21
  144.3 3.7 %collective-permute-done.42.refs_3_ = f32[64,2176]{1,0:T(8,128)S(1)} collective-permute-done((f32[64,2176]{1,0:T(8,128)S(1)}, f32[64,2176]{1,0:T(8,128)S(1)}, u32[]{:S(2)}, u32[]{:S(2)}) %collective-permute-start.42) | collective-permute-done | bytes 557088 | tf_op jit(solution)/shard_map/ppermute | solution.py:21
  148.0 2.0 %shard_map.83 = (f32[64,8192]{1,0:T(8,128)}, f32[4,8192]{1,0:T(4,128)}) custom-call(f32[64,2176]{1,0:T(8,128)S(1)} %get-tuple-element.121.refs_0_, f32[64,2176]{1,0:T(8,128)S(1)} %collective-permute-done.40.refs_1_, f32[64,2176]{1,0:T(8,128)S(1)} %collective-permute-done.41.refs_2_, f32[64,2176]{1,0:T(8,128)S(1)} %collective-permute-done.42.refs_3_), custom_call_target="tpu_custom_call" | custom-call | tf_op jit(solution)/shard_map/pallas_call | solution.py:56
  (93 shorter events, 49.3 us)
Async XLA Ops:
  1.7 6.8 %collective-permute-start = (f32[8,1536]{1,0:T(8,128)S(1)}, f32[8,1536]{1,0:T(8,128)S(1)}, u32[]{:S(2)}, u32[]{:S(2)}) collective-permute-start(f32[8,1536]{1,0:T(8,128)S(1)} %get-tuple-element.68), channel_id=1, source_target_pairs={{0,192},{64,0},{128,64},{192,128},{1,193},{65,1},{129,65},{193,129... | collective-permute-start | bytes 147464 | tf_op jit(solution)/shard_map/ppermute | solution.py:21
  4.5 5.6 %collective-permute-start.1 = (f32[8,1536]{1,0:T(8,128)S(1)}, f32[8,1536]{1,0:T(8,128)S(1)}, u32[]{:S(2)}, u32[]{:S(2)}) collective-permute-start(f32[8,1536]{1,0:T(8,128)S(1)} %get-tuple-element.69), channel_id=1, source_target_pairs={{0,128},{64,192},{128,0},{192,64},{1,129},{65,193},{129,1},{193,65... | collective-permute-start | bytes 147464 | tf_op jit(solution)/shard_map/ppermute | solution.py:21
  10.7 8.9 %collective-permute-start.7 = (f32[16,2048]{1,0:T(8,128)S(1)}, f32[16,2048]{1,0:T(8,128)S(1)}, u32[]{:S(2)}, u32[]{:S(2)}) collective-permute-start(f32[16,2048]{1,0:T(8,128)S(1)} %get-tuple-element.80.refs_4_), channel_id=1, source_target_pairs={{0,56},{8,0},{16,8},{24,16},{32,24},{40,32},{48,40},{56,48},{1,57}... | collective-permute-start | bytes 393224 | tf_op jit(solution)/shard_map/ppermute | solution.py:21
  16.7 6.2 %collective-permute-start.6 = (f32[16,2048]{1,0:T(8,128)S(1)}, f32[16,2048]{1,0:T(8,128)S(1)}, u32[]{:S(2)}, u32[]{:S(2)}) collective-permute-start(f32[16,2048]{1,0:T(8,128)S(1)} %get-tuple-element.80.refs_4_), channel_id=1, source_target_pairs={{0,8},{8,16},{16,24},{24,32},{32,40},{40,48},{48,56},{56,0},{1,9},... | collective-permute-start | bytes 393224 | tf_op jit(solution)/shard_map/ppermute | solution.py:21
  16.7 26.4 %collective-permute-start.3 = (f32[64,2048]{1,0:T(8,128)}, f32[64,2048]{1,0:T(8,128)S(1)}, u32[]{:S(2)}, u32[]{:S(2)}) collective-permute-start(f32[64,2048]{1,0:T(8,128)} %get-tuple-element.77), channel_id=1, source_target_pairs={{0,192},{64,0},{128,64},{192,128},{1,193},{65,1},{129,65},{193,129... | collective-permute-start | bytes 1572872 | tf_op jit(solution)/shard_map/ppermute | solution.py:21
  17.2 25.9 %collective-permute-start.4 = (f32[64,2048]{1,0:T(8,128)}, f32[64,2048]{1,0:T(8,128)S(1)}, u32[]{:S(2)}, u32[]{:S(2)}) collective-permute-start(f32[64,2048]{1,0:T(8,128)} %get-tuple-element.78), channel_id=1, source_target_pairs={{0,128},{64,192},{128,0},{192,64},{1,129},{65,193},{129,1},{193,65... | collective-permute-start | bytes 1572872 | tf_op jit(solution)/shard_map/ppermute | solution.py:21
  18.4 24.7 %collective-permute-start.5 = (f32[64,2048]{1,0:T(8,128)}, f32[64,2048]{1,0:T(8,128)S(1)}, u32[]{:S(2)}, u32[]{:S(2)}) collective-permute-start(f32[64,2048]{1,0:T(8,128)} %get-tuple-element.79), channel_id=1, source_target_pairs={{0,64},{64,128},{128,192},{192,0},{1,65},{65,129},{129,193},{193,1... | collective-permute-start | bytes 1572872 | tf_op jit(solution)/shard_map/ppermute | solution.py:21
  22.9 6.2 %collective-permute-start.8 = (f32[16,2048]{1,0:T(8,128)S(1)}, f32[16,2048]{1,0:T(8,128)S(1)}, u32[]{:S(2)}, u32[]{:S(2)}) collective-permute-start(f32[16,2048]{1,0:T(8,128)S(1)} %collective-permute-done.6.refs_11_), channel_id=1, source_target_pairs={{0,8},{8,16},{16,24},{24,32},{32,40},{40,48},{48,56},{56,0},{1,9},... | collective-permute-start | bytes 393224 | tf_op jit(solution)/shard_map/ppermute | solution.py:21
  29.5 7.5 %collective-permute-start.10 = (f32[16,2048]{1,0:T(8,128)S(1)}, f32[16,2048]{1,0:T(8,128)S(1)}, u32[]{:S(2)}, u32[]{:S(2)}) collective-permute-start(f32[16,2048]{1,0:T(8,128)S(1)} %collective-permute-done.8.refs_10_), channel_id=1, source_target_pairs={{0,8},{8,16},{16,24},{24,32},{32,40},{40,48},{48,56},{56,0},{1,9},... | collective-permute-start | bytes 393224 | tf_op jit(solution)/shard_map/ppermute | solution.py:21
  36.9 6.2 %collective-permute-start.12 = (f32[16,2048]{1,0:T(8,128)S(1)}, f32[16,2048]{1,0:T(8,128)S(1)}, u32[]{:S(2)}, u32[]{:S(2)}) collective-permute-start(f32[16,2048]{1,0:T(8,128)S(1)} %collective-permute-done.10.refs_9_), channel_id=1, source_target_pairs={{0,8},{8,16},{16,24},{24,32},{32,40},{40,48},{48,56},{56,0},{1,9},... | collective-permute-start | bytes 393224 | tf_op jit(solution)/shard_map/ppermute | solution.py:21
  46.1 5.4 %collective-permute-start.16 = (f32[4,1,32,128]{3,2,1,0:T(8,128)S(1)}, f32[4,1,32,128]{3,2,1,0:T(8,128)S(1)}, u32[]{:S(2)}, u32[]{:S(2)}) collective-permute-start(f32[4,1,32,128]{3,2,1,0:T(8,128)S(1)} %dynamic-slice_add_fusion), channel_id=1, source_target_pairs={{0,192},{64,0},{128,64},{192,128},{1,193},{65,1},{129,65},{193,129... | collective-permute-start | bytes 196616 | tf_op jit(solution)/shard_map/ppermute | solution.py:21
  47.1 5.5 %collective-permute-start.15 = (f32[4,1,32,128]{3,2,1,0:T(8,128)S(1)}, f32[4,1,32,128]{3,2,1,0:T(8,128)S(1)}, u32[]{:S(2)}, u32[]{:S(2)}) collective-permute-start(f32[4,1,32,128]{3,2,1,0:T(8,128)S(1)} %dynamic-slice_add_fusion), channel_id=1, source_target_pairs={{0,64},{64,128},{128,192},{192,0},{1,65},{65,129},{129,193},{193,1... | collective-permute-start | bytes 196616 | tf_op jit(solution)/shard_map/ppermute | solution.py:21
  48.2 6.6 %collective-permute-start.14 = (f32[4,1,32,128]{3,2,1,0:T(8,128)S(1)}, f32[4,1,32,128]{3,2,1,0:T(8,128)S(1)}, u32[]{:S(2)}, u32[]{:S(2)}) collective-permute-start(f32[4,1,32,128]{3,2,1,0:T(8,128)S(1)} %dynamic-slice_add_fusion), channel_id=1, source_target_pairs={{0,128},{64,192},{128,0},{192,64},{1,129},{65,193},{129,1},{193,65... | collective-permute-start | bytes 196616 | tf_op jit(solution)/shard_map/ppermute | solution.py:21
  54.8 5.6 %collective-permute-start.19 = (f32[4,1,32,128]{3,2,1,0:T(8,128)S(1)}, f32[4,1,32,128]{3,2,1,0:T(8,128)S(1)}, u32[]{:S(2)}, u32[]{:S(2)}) collective-permute-start(f32[4,1,32,128]{3,2,1,0:T(8,128)S(1)} %fusion), channel_id=1, source_target_pairs={{0,6},{2,0},{4,2},{6,4},{1,7},{3,1},{5,3},{7,5},{8,14},{10,8},{12,... | collective-permute-start | bytes 196616 | tf_op jit(solution)/shard_map/ppermute | solution.py:21
  56.9 5.8 %collective-permute-start.17 = (f32[4,1,32,128]{3,2,1,0:T(8,128)S(1)}, f32[4,1,32,128]{3,2,1,0:T(8,128)S(1)}, u32[]{:S(2)}, u32[]{:S(2)}) collective-permute-start(f32[4,1,32,128]{3,2,1,0:T(8,128)S(1)} %fusion), channel_id=1, source_target_pairs={{0,4},{2,6},{4,0},{6,2},{1,5},{3,7},{5,1},{7,3},{8,12},{10,14},{12... | collective-permute-start | bytes 196616 | tf_op jit(solution)/shard_map/ppermute | solution.py:21
  65.9 6.8 %collective-permute-start.22 = (f32[16,1152]{1,0:T(8,128)S(1)}, f32[16,1152]{1,0:T(8,128)S(1)}, u32[]{:S(2)}, u32[]{:S(2)}) collective-permute-start(f32[16,1152]{1,0:T(8,128)S(1)} %get-tuple-element.90), channel_id=1, source_target_pairs={{0,56},{8,0},{16,8},{24,16},{32,24},{40,32},{48,40},{56,48},{1,57}... | collective-permute-start | bytes 221192 | tf_op jit(solution)/shard_map/ppermute | solution.py:21
  67.2 5.5 %collective-permute-start.21 = (f32[16,1024]{1,0:T(8,128)S(1)}, f32[16,1024]{1,0:T(8,128)S(1)}, u32[]{:S(2)}, u32[]{:S(2)}) collective-permute-start(f32[16,1024]{1,0:T(8,128)S(1)} %get-tuple-element.89), channel_id=1, source_target_pairs={{0,8},{8,16},{16,24},{24,32},{32,40},{40,48},{48,56},{56,0},{1,9},... | collective-permute-start | bytes 196616 | tf_op jit(solution)/shard_map/ppermute | solution.py:21
  72.7 8.9 %collective-permute-start.24 = (f32[16,2176]{1,0:T(8,128)S(1)}, f32[16,2176]{1,0:T(8,128)S(1)}, u32[]{:S(2)}, u32[]{:S(2)}) collective-permute-start(f32[16,2176]{1,0:T(8,128)S(1)} %get-tuple-element.96), channel_id=1, source_target_pairs={{0,8},{8,16},{16,24},{24,32},{32,40},{40,48},{48,56},{56,0},{1,9},... | collective-permute-start | bytes 417800 | tf_op jit(solution)/shard_map/ppermute | solution.py:21
  73.4 8.2 %collective-permute-start.25 = (f32[16,2176]{1,0:T(8,128)S(1)}, f32[16,2176]{1,0:T(8,128)S(1)}, u32[]{:S(2)}, u32[]{:S(2)}) collective-permute-start(f32[16,2176]{1,0:T(8,128)S(1)} %get-tuple-element.97), channel_id=1, source_target_pairs={{0,56},{8,0},{16,8},{24,16},{32,24},{40,32},{48,40},{56,48},{1,57}... | collective-permute-start | bytes 417800 | tf_op jit(solution)/shard_map/ppermute | solution.py:21
  76.0 5.6 %collective-permute-start.26 = (f32[128,128]{1,0:T(8,128)S(1)}, f32[128,128]{1,0:T(8,128)S(1)}, u32[]{:S(2)}, u32[]{:S(2)}) collective-permute-start(f32[128,128]{1,0:T(8,128)S(1)} %add.84), channel_id=1, source_target_pairs={{0,56},{8,16},{16,8},{24,32},{32,24},{40,48},{48,40},{56,0},{1,57}... | collective-permute-start | bytes 196616 | tf_op jit(solution)/shard_map/ppermute | solution.py:91
  81.6 6.5 %collective-permute-start.28 = (f32[16,2176]{1,0:T(8,128)S(1)}, f32[16,2176]{1,0:T(8,128)S(1)}, u32[]{:S(2)}, u32[]{:S(2)}) collective-permute-start(f32[16,2176]{1,0:T(8,128)S(1)} %add.86), channel_id=1, source_target_pairs={{0,56},{8,0},{16,8},{24,16},{32,24},{40,32},{48,40},{56,48},{1,57}... | collective-permute-start | bytes 417800 | tf_op jit(solution)/shard_map/ppermute | solution.py:21
  83.1 6.3 %collective-permute-start.27 = (f32[16,2176]{1,0:T(8,128)S(1)}, f32[16,2176]{1,0:T(8,128)S(1)}, u32[]{:S(2)}, u32[]{:S(2)}) collective-permute-start(f32[16,2176]{1,0:T(8,128)S(1)} %add.85), channel_id=1, source_target_pairs={{0,8},{8,16},{16,24},{24,32},{32,40},{40,48},{48,56},{56,0},{1,9},... | collective-permute-start | bytes 417800 | tf_op jit(solution)/shard_map/ppermute | solution.py:21
  89.4 5.6 %collective-permute-start.32 = (f32[16,2176]{1,0:T(8,128)S(1)}, f32[16,2176]{1,0:T(8,128)S(1)}, u32[]{:S(2)}, u32[]{:S(2)}) collective-permute-start(f32[16,2176]{1,0:T(8,128)S(1)} %add.91), channel_id=1, source_target_pairs={{0,56},{8,0},{16,8},{24,16},{32,24},{40,32},{48,40},{56,48},{1,57}... | collective-permute-start | bytes 417800 | tf_op jit(solution)/shard_map/ppermute | solution.py:21
  91.5 7.0 %collective-permute-start.31 = (f32[16,2176]{1,0:T(8,128)S(1)}, f32[16,2176]{1,0:T(8,128)S(1)}, u32[]{:S(2)}, u32[]{:S(2)}) collective-permute-start(f32[16,2176]{1,0:T(8,128)S(1)} %add.90), channel_id=1, source_target_pairs={{0,8},{8,16},{16,24},{24,32},{32,40},{40,48},{48,56},{56,0},{1,9},... | collective-permute-start | bytes 417800 | tf_op jit(solution)/shard_map/ppermute | solution.py:21
  99.0 6.3 %collective-permute-start.33 = (f32[16,2176]{1,0:T(8,128)S(1)}, f32[16,2176]{1,0:T(8,128)S(1)}, u32[]{:S(2)}, u32[]{:S(2)}) collective-permute-start(f32[16,2176]{1,0:T(8,128)S(1)} %add_add_fusion.refs_4_), channel_id=1, source_target_pairs={{0,8},{8,16},{16,24},{24,32},{32,40},{40,48},{48,56},{56,0},{1,9},... | collective-permute-start | bytes 417800 | tf_op jit(solution)/shard_map/ppermute | solution.py:21
  105.3 6.3 %collective-permute-start.35 = (f32[16,2176]{1,0:T(8,128)S(1)}, f32[16,2176]{1,0:T(8,128)S(1)}, u32[]{:S(2)}, u32[]{:S(2)}) collective-permute-start(f32[16,2176]{1,0:T(8,128)S(1)} %collective-permute-done.33.refs_11_), channel_id=1, source_target_pairs={{0,8},{8,16},{16,24},{24,32},{32,40},{40,48},{48,56},{56,0},{1,9},... | collective-permute-start | bytes 417800 | tf_op jit(solution)/shard_map/ppermute | solution.py:21
  112.1 6.3 %collective-permute-start.37 = (f32[16,2176]{1,0:T(8,128)S(1)}, f32[16,2176]{1,0:T(8,128)S(1)}, u32[]{:S(2)}, u32[]{:S(2)}) collective-permute-start(f32[16,2176]{1,0:T(8,128)S(1)} %collective-permute-done.35.refs_10_), channel_id=1, source_target_pairs={{0,8},{8,16},{16,24},{24,32},{32,40},{40,48},{48,56},{56,0},{1,9},... | collective-permute-start | bytes 417800 | tf_op jit(solution)/shard_map/ppermute | solution.py:21
  113.6 5.5 %collective-permute-start.30 = (f32[128,128]{1,0:T(8,128)S(1)}, f32[128,128]{1,0:T(8,128)S(1)}, u32[]{:S(2)}, u32[]{:S(2)}) collective-permute-start(f32[128,128]{1,0:T(8,128)S(1)} %collective-permute-done.29), channel_id=1, source_target_pairs={{0,56},{8,16},{16,8},{24,32},{32,24},{40,48},{48,40},{56,0},{1,57}... | collective-permute-start | bytes 196616 | tf_op jit(solution)/shard_map/ppermute | solution.py:91
  118.3 7.3 %collective-permute-start.39 = (f32[16,2176]{1,0:T(8,128)S(1)}, f32[16,2176]{1,0:T(8,128)S(1)}, u32[]{:S(2)}, u32[]{:S(2)}) collective-permute-start(f32[16,2176]{1,0:T(8,128)S(1)} %collective-permute-done.37.refs_9_), channel_id=1, source_target_pairs={{0,8},{8,16},{16,24},{24,32},{32,40},{40,48},{48,56},{56,0},{1,9},... | collective-permute-start | bytes 417800 | tf_op jit(solution)/shard_map/ppermute | solution.py:21
  128.6 15.7 %collective-permute-start.40 = (f32[64,2176]{1,0:T(8,128)S(1)}, f32[64,2176]{1,0:T(8,128)S(1)}, u32[]{:S(2)}, u32[]{:S(2)}) collective-permute-start(f32[64,2176]{1,0:T(8,128)S(1)} %get-tuple-element.122), channel_id=1, source_target_pairs={{0,192},{64,0},{128,64},{192,128},{1,193},{65,1},{129,65},{193,129... | collective-permute-start | bytes 1671176 | tf_op jit(solution)/shard_map/ppermute | solution.py:21
  130.4 13.9 %collective-permute-start.41 = (f32[64,2176]{1,0:T(8,128)S(1)}, f32[64,2176]{1,0:T(8,128)S(1)}, u32[]{:S(2)}, u32[]{:S(2)}) collective-permute-start(f32[64,2176]{1,0:T(8,128)S(1)} %get-tuple-element.123), channel_id=1, source_target_pairs={{0,128},{64,192},{128,0},{192,64},{1,129},{65,193},{129,1},{193,65... | collective-permute-start | bytes 1671176 | tf_op jit(solution)/shard_map/ppermute | solution.py:21
  131.1 16.9 %collective-permute-start.42 = (f32[64,2176]{1,0:T(8,128)S(1)}, f32[64,2176]{1,0:T(8,128)S(1)}, u32[]{:S(2)}, u32[]{:S(2)}) collective-permute-start(f32[64,2176]{1,0:T(8,128)S(1)} %get-tuple-element.124), channel_id=1, source_target_pairs={{0,64},{64,128},{128,192},{192,0},{1,65},{65,129},{129,193},{193,1... | collective-permute-start | bytes 1671176 | tf_op jit(solution)/shard_map/ppermute | solution.py:21
  (15 other events, 118.1 us)
